TPU v7x, 256 devices: a whole 4x4x8 slice. The times are simulated.
256 devices in a mesh: grp: 8 (over z_hi, y), row: 32 (over z_lo, x, core).
Axes of the slice: x: 4, y: 4, z: 8 (z_hi: 2, z_lo: 4; z = z_hi * 4 + z_lo), core: 2. Of those that a mesh axis runs over, the one named last changes fastest.
Arguments:
- points: bfloat16 [524288, 128], P(('grp', 'row')), as said below
- centers: bfloat16 [8192, 128], replicated, as said below
- inner_factor: bfloat16 [8192, 8192], P('row'), as said below
- outer_factor: bfloat16 [8192, 8192], P('row'), as said below
- iterate: float32 [64, 8192], P(None, 'row'), may hold values from -6 to 6
- residual: float32 [64, 8192], P(None, 'row'), as said below
- direction: float32 [64, 8192], P(None, 'row'), as said below
Outputs:
- next_iterate: float32 [64, 8192], P(None, 'row')
- next_residual: float32 [64, 8192], P(None, 'row')
- next_direction: float32 [64, 8192], P(None, 'row')
Inputs may be any that keep to these rules, and one draw needn't show every extreme that they name: `inner_factor`: upper triangular: zero below the diagonal, positive on it. `outer_factor`: upper triangular: zero below the diagonal, positive on it. `residual`: finite real values. `direction`: finite real values. `points`: finite real values. `centers`: finite real values.
All inputs are finite; a program needn't handle non-finite values.
Results may differ from a plain program's by a relative error of at most 0.0056.
Values may be sent and summed in bfloat16 or wider, within the bound.
No kernel may reach another device: no remote copies, remote signals or barrier semaphores. Data moves between devices by JAX's collectives and lax.ppermute only.
A program may use at most 64 MiB of HBM per device.

v0:
```python
import jax
import jax.numpy as jnp
from jax import lax
from jax.sharding import PartitionSpec as P

ridge_weight = 0.5


def kernel_rows(block_points, centers, center_norms):
    point_wide = block_points.astype(jnp.float32)
    point_norms = jnp.sum(point_wide * point_wide, axis=1)
    cross_term = lax.dot_general(
        block_points, centers, (((1,), (1,)), ((), ())), preferred_element_type=jnp.float32
    )
    distance = point_norms[:, None] + center_norms[None, :] - 2.0 * cross_term
    return jnp.exp(distance * (-4.0 / block_points.shape[1])).astype(jnp.bfloat16)


def local(points, centers, inner_factor, outer_factor, iterate, residual, direction):
    contract_last = (((1,), (1,)), ((), ()))
    own_rows = inner_factor.shape[0]
    targets = direction.shape[0]
    direction_half = direction.astype(jnp.bfloat16)
    columns = inner_factor
    inner_term = lax.dot_general(
        lax.all_gather(direction_half, "row", axis=1, tiled=True),
        columns,
        contract_last,
        preferred_element_type=jnp.float32,
    )
    inner_half = inner_term.astype(jnp.bfloat16)
    columns = outer_factor
    outer_rows = lax.dot_general(
        lax.all_gather(inner_half, "row", axis=1, tiled=True),
        columns,
        contract_last,
        preferred_element_type=jnp.float32,
    )
    outer_half = lax.all_gather(outer_rows.astype(jnp.bfloat16), "row", axis=1, tiled=True)
    center_wide = centers.astype(jnp.float32)
    center_norms = jnp.sum(center_wide * center_wide, axis=1)
    local_points = points.shape[0]
    block_rows = min(512, local_points)
    point_blocks = points.reshape(local_points // block_rows, block_rows, points.shape[1])

    def one_block(carried, block_points):
        kernel_block = kernel_rows(block_points, centers, center_norms)
        fitted = lax.dot_general(
            outer_half, kernel_block, contract_last, preferred_element_type=jnp.float32
        ).astype(jnp.bfloat16)
        return (carried + jnp.dot(fitted, kernel_block, preferred_element_type=jnp.float32), None)

    partial_sums, _ = lax.scan(
        one_block, jnp.zeros((targets, centers.shape[0]), jnp.float32), point_blocks
    )
    summed_all = lax.psum(partial_sums, ("grp", "row"))
    own_normal = lax.dynamic_slice_in_dim(summed_all, lax.axis_index("row") * own_rows, own_rows, 1)
    normal_half = own_normal.astype(jnp.bfloat16)
    point_count = local_points * lax.axis_size("grp") * lax.axis_size("row")
    outer_terms = jnp.dot(normal_half, outer_factor, preferred_element_type=jnp.float32)
    shaped = (
        lax.psum_scatter(outer_terms, "row", scatter_dimension=1, tiled=True) / point_count
        + ridge_weight * inner_term
    )
    shaped_half = shaped.astype(jnp.bfloat16)
    inner_terms = jnp.dot(shaped_half, inner_factor, preferred_element_type=jnp.float32)
    operator_image = lax.psum_scatter(inner_terms, "row", scatter_dimension=1, tiled=True)
    old_norm = lax.psum(jnp.sum(residual * residual, axis=1), "row")
    curvature = lax.psum(jnp.sum(direction * operator_image, axis=1), "row")
    step_size = old_norm / curvature
    next_residual = residual - step_size[:, None] * operator_image
    new_norm = lax.psum(jnp.sum(next_residual * next_residual, axis=1), "row")
    next_iterate = iterate + step_size[:, None] * direction
    next_direction = next_residual + (new_norm / old_norm)[:, None] * direction
    return (next_iterate, next_residual, next_direction)


def solution(mesh):
    placed = (
        P(("grp", "row"), None),
        P(),
        P("row", None),
        P("row", None),
        P(None, "row"),
        P(None, "row"),
        P(None, "row"),
    )
    return jax.shard_map(
        local,
        mesh=mesh,
        in_specs=placed,
        out_specs=(P(None, "row"), P(None, "row"), P(None, "row")),
        check_vma=False,
    )
```

profile of v0, /device:TPU:1, one launch (start us, length us, event | category | flops | bytes accessed | tf_op | source)
XLA Modules:
  0.0 819.4 jit_solution(775019206389307324)
XLA Ops:
  7.2 1.5 convert_element_type.29
  8.7 66.0 %all-gather.4.cloned.1.call-done = bf16[64,8192]{1,0:T(8,128)(2,1)} async-done(((bf16[64,256]{1,0:T(8,128)(2,1)}), bf16[64,8192]{1,0:T(8,128)(2,1)}) %all-gather.4.cloned.1.call-update) | async-done | bytes 1048592 | tf_op jit(solution)/shard_map/all_gather | solution.py:26
  74.8 4.5 fusion.10
  79.4 59.4 %all-gather.6.cloned.1.call-done = bf16[64,8192]{1,0:T(8,128)(2,1)} async-done(((bf16[64,256]{1,0:T(8,128)(2,1)}), bf16[64,8192]{1,0:T(8,128)(2,1)}) %all-gather.6.cloned.1.call-update) | async-done | bytes 1048592 | tf_op jit(solution)/shard_map/all_gather | solution.py:34
  138.7 4.5 convolution_convert_fusion.1
  143.5 2.7 multiply_reduce_fusion.1
  146.3 56.4 %all-gather.8.cloned.1.call-done = bf16[64,8192]{1,0:T(8,128)(2,1)} async-done(((bf16[64,256]{1,0:T(8,128)(2,1)}), bf16[64,8192]{1,0:T(8,128)(2,1)}) %all-gather.8.cloned.1.call-update) | async-done | bytes 1048592 | tf_op jit(solution)/shard_map/all_gather | solution.py:39
  202.7 87.9 %while.11 = (s32[]{:T(128)}, f32[64,8192]{1,0:T(8,128)S(1)}, bf16[4,512,128]{2,1,0:T(8,128)(2,1)}, f32[8192]{0:T(1024)S(1)}, bf16[8192,128]{1,0:T(8,128)(2,1)}, ...) while((s32[]{:T(128)}, f32[64,8192]{1,0:T(8,128)S(1)}, bf16[4,512,128]{2,1,0:T(8,128)(2,1)}, ...), condition=%wide.region_5.6_spmd.clone, body=%wide.region_3.0_spmd.clone.sunk | while | flops 2169732608 | bytes 28610700 | solution.py:53
  203.7 9.0 %exponential_convert_fusion.2 = bf16[512,8192]{1,0:T(8,128)(2,1)} fusion(bf16[8192,128]{1,0:T(8,128)(2,1)} %get-tuple-element.134, f32[8192]{0:T(1024)S(1)} %get-tuple-element.133, f32[512]{0:T(512)S(1)} %multiply_reduce_fusion.6, bf16[4,512,128]{2,1,0:T(8,128)(2,1)} %get-tuple-element.132, s32[]{:T(128)S(6)} %copy.12), kind=kOutput, calls=%fused_computation.clone.1 | convolution fusion | flops 1094713344 | bytes 10651652 | tf_op jit(solution)/shard_map/while/body/eval_jaxpr/dot_general | solution.py:12
  212.8 11.9 %convolution_add_fusion.2 = f32[64,8192]{1,0:T(8,128)S(1)} fusion(bf16[512,8192]{1,0:T(8,128)(2,1)} %exponential_convert_fusion.2, f32[64,8192]{1,0:T(8,128)S(1)} %get-tuple-element.123, pred[]{:T(512)S(6)} %compare.3, bf16[64,8192]{1,0:T(8,128)(2,1)S(1)} %copy-done), kind=kOutput, calls=%fused_computation.1.clone.1 | convolution fusion | flops 1074823168 | bytes 13631489 | tf_op jit(solution)/shard_map/while/body/eval_jaxpr/dot_general | solution.py:51
  224.7 1.1 multiply_reduce_fusion.6
  225.7 9.0 %exponential_convert_fusion.2 = bf16[512,8192]{1,0:T(8,128)(2,1)} fusion(bf16[8192,128]{1,0:T(8,128)(2,1)} %get-tuple-element.134, f32[8192]{0:T(1024)S(1)} %get-tuple-element.133, f32[512]{0:T(512)S(1)} %multiply_reduce_fusion.6, bf16[4,512,128]{2,1,0:T(8,128)(2,1)} %get-tuple-element.132, s32[]{:T(128)S(6)} %copy.12), kind=kOutput, calls=%fused_computation.clone.1 | convolution fusion | flops 1094713344 | bytes 10651652 | tf_op jit(solution)/shard_map/while/body/eval_jaxpr/dot_general | solution.py:12
  234.8 11.9 %convolution_add_fusion.2 = f32[64,8192]{1,0:T(8,128)S(1)} fusion(bf16[512,8192]{1,0:T(8,128)(2,1)} %exponential_convert_fusion.2, f32[64,8192]{1,0:T(8,128)S(1)} %get-tuple-element.123, pred[]{:T(512)S(6)} %compare.3, bf16[64,8192]{1,0:T(8,128)(2,1)S(1)} %copy-done), kind=kOutput, calls=%fused_computation.1.clone.1 | convolution fusion | flops 1074823168 | bytes 13631489 | tf_op jit(solution)/shard_map/while/body/eval_jaxpr/dot_general | solution.py:51
  247.7 9.0 %exponential_convert_fusion.2 = bf16[512,8192]{1,0:T(8,128)(2,1)} fusion(bf16[8192,128]{1,0:T(8,128)(2,1)} %get-tuple-element.134, f32[8192]{0:T(1024)S(1)} %get-tuple-element.133, f32[512]{0:T(512)S(1)} %multiply_reduce_fusion.6, bf16[4,512,128]{2,1,0:T(8,128)(2,1)} %get-tuple-element.132, s32[]{:T(128)S(6)} %copy.12), kind=kOutput, calls=%fused_computation.clone.1 | convolution fusion | flops 1094713344 | bytes 10651652 | tf_op jit(solution)/shard_map/while/body/eval_jaxpr/dot_general | solution.py:12
  256.7 11.9 %convolution_add_fusion.2 = f32[64,8192]{1,0:T(8,128)S(1)} fusion(bf16[512,8192]{1,0:T(8,128)(2,1)} %exponential_convert_fusion.2, f32[64,8192]{1,0:T(8,128)S(1)} %get-tuple-element.123, pred[]{:T(512)S(6)} %compare.3, bf16[64,8192]{1,0:T(8,128)(2,1)S(1)} %copy-done), kind=kOutput, calls=%fused_computation.1.clone.1 | convolution fusion | flops 1074823168 | bytes 13631489 | tf_op jit(solution)/shard_map/while/body/eval_jaxpr/dot_general | solution.py:51
  269.7 9.0 %exponential_convert_fusion.2 = bf16[512,8192]{1,0:T(8,128)(2,1)} fusion(bf16[8192,128]{1,0:T(8,128)(2,1)} %get-tuple-element.134, f32[8192]{0:T(1024)S(1)} %get-tuple-element.133, f32[512]{0:T(512)S(1)} %multiply_reduce_fusion.6, bf16[4,512,128]{2,1,0:T(8,128)(2,1)} %get-tuple-element.132, s32[]{:T(128)S(6)} %copy.12), kind=kOutput, calls=%fused_computation.clone.1 | convolution fusion | flops 1094713344 | bytes 10651652 | tf_op jit(solution)/shard_map/while/body/eval_jaxpr/dot_general | solution.py:12
  278.7 11.9 %convolution_add_fusion.2 = f32[64,8192]{1,0:T(8,128)S(1)} fusion(bf16[512,8192]{1,0:T(8,128)(2,1)} %exponential_convert_fusion.2, f32[64,8192]{1,0:T(8,128)S(1)} %get-tuple-element.123, pred[]{:T(512)S(6)} %compare.3, bf16[64,8192]{1,0:T(8,128)(2,1)S(1)} %copy-done), kind=kOutput, calls=%fused_computation.1.clone.1 | convolution fusion | flops 1074823168 | bytes 13631489 | tf_op jit(solution)/shard_map/while/body/eval_jaxpr/dot_general | solution.py:51
  290.6 85.9 %all-reduce.2 = bf16[64,8192]{1,0:T(8,128)(2,1)S(1)} all-reduce(f32[64,8192]{1,0:T(8,128)S(1)} %get-tuple-element.35), channel_id=1, replica_groups=mesh['grp'=8,'row'=32] {'grp','row'}, use_global_device_ids=true, to_apply=%region_6.7 | all-reduce | flops 524288 | bytes 3145728 | tf_op jit(solution)/shard_map/psum | solution.py:56
  376.5 4.4 fusion.3
  380.9 139.3 %reduce-scatter.3.cloned.1.call-done = f32[64,256]{1,0:T(8,128)} async-done(((f32[64,8192]{1,0:T(8,128)}), f32[64,256]{1,0:T(8,128)}) %reduce-scatter.3.cloned.1.call-update) | async-done | bytes 65552 | tf_op jit(solution)/shard_map/reduce_scatter | solution.py:62
  520.3 4.5 fusion.4
  524.9 144.8 %reduce-scatter.5.cloned.1.call-done = f32[64,256]{1,0:T(8,128)} async-done(((f32[64,8192]{1,0:T(8,128)}), f32[64,256]{1,0:T(8,128)}) %reduce-scatter.5.cloned.1.call-update) | async-done | bytes 65552 | tf_op jit(solution)/shard_map/reduce_scatter | solution.py:67
  670.7 72.6 %all-reduce = (f32[64]{0:T(128)S(1)}, f32[64]{0:T(128)S(1)}) all-reduce(f32[64]{0:T(128)S(1)} %multiply_reduce_fusion.4, f32[64]{0:T(128)S(1)} %multiply_reduce_fusion.3), channel_id=1, replica_groups=mesh['grp'=8,'row'=32] {'row'}, use_global_device_ids=true, to_apply=%region_1.2 | all-reduce | flops 128 | bytes 1024 | tf_op jit(solution)/shard_map/psum | solution.py:68
  744.3 67.9 %psum.31 = f32[64]{0:T(128)S(1)} all-reduce(f32[64]{0:T(128)S(1)} %get-tuple-element.71), channel_id=1, replica_groups=mesh['grp'=8,'row'=32] {'row'}, use_global_device_ids=true, to_apply=%region_12.13 | all-reduce | flops 64 | bytes 512 | tf_op jit(solution)/shard_map/psum | solution.py:72
  (36 shorter events, 6.5 us)
Async XLA Ops:
  7.2 67.6 %all-gather.4.cloned.1.call-start = ((), (), s32[]{:S(2)}) async-start(), calls=%async_computation.2 | async-start | bytes 1081344 | tf_op jit(solution)/shard_map/all_gather | solution.py:26
  8.7 130.0 %all-gather.6.cloned.1.call-start = ((), (), s32[]{:S(2)}) async-start(), calls=%async_computation.3 | async-start | bytes 1081344 | tf_op jit(solution)/shard_map/all_gather | solution.py:34
  79.3 123.4 %all-gather.8.cloned.1.call-start = ((), (), s32[]{:S(2)}) async-start(), calls=%async_computation.4 | async-start | bytes 1081344 | tf_op jit(solution)/shard_map/all_gather | solution.py:39
  143.3 377.0 %reduce-scatter.3.cloned.1.call-start = ((), (), s32[]{:S(2)}) async-start(), calls=%async_computation.5 | async-start | bytes 2162688 | tf_op jit(solution)/shard_map/reduce_scatter | solution.py:62
  203.7 9.1 %copy-start = (bf16[64,8192]{1,0:T(8,128)(2,1)S(1)}, bf16[64,8192]{1,0:T(8,128)(2,1)}, u32[]{:S(2)}) copy-start(bf16[64,8192]{1,0:T(8,128)(2,1)} %get-tuple-element.135) | copy-start | bytes 3145732 | tf_op jit(solution)/shard_map/while
  225.7 9.1 %copy-start = (bf16[64,8192]{1,0:T(8,128)(2,1)S(1)}, bf16[64,8192]{1,0:T(8,128)(2,1)}, u32[]{:S(2)}) copy-start(bf16[64,8192]{1,0:T(8,128)(2,1)} %get-tuple-element.135) | copy-start | bytes 3145732 | tf_op jit(solution)/shard_map/while
  247.7 9.1 %copy-start = (bf16[64,8192]{1,0:T(8,128)(2,1)S(1)}, bf16[64,8192]{1,0:T(8,128)(2,1)}, u32[]{:S(2)}) copy-start(bf16[64,8192]{1,0:T(8,128)(2,1)} %get-tuple-element.135) | copy-start | bytes 3145732 | tf_op jit(solution)/shard_map/while
  269.7 9.1 %copy-start = (bf16[64,8192]{1,0:T(8,128)(2,1)S(1)}, bf16[64,8192]{1,0:T(8,128)(2,1)}, u32[]{:S(2)}) copy-start(bf16[64,8192]{1,0:T(8,128)(2,1)} %get-tuple-element.135) | copy-start | bytes 3145732 | tf_op jit(solution)/shard_map/while
  380.9 288.8 %reduce-scatter.5.cloned.1.call-start = ((), (), s32[]{:S(2)}) async-start(), calls=%async_computation.6 | async-start | bytes 2162688 | tf_op jit(solution)/shard_map/reduce_scatter | solution.py:67
  520.3 4.5 copy-start.3
  520.3 149.4 %copy-start.1 = (f32[64,256]{1,0:T(8,128)S(1)}, f32[64,256]{1,0:T(8,128)}, u32[]{:S(2)}) copy-start(f32[64,256]{1,0:T(8,128)} %param.15) | copy-start | bytes 196612
  520.3 291.8 %copy-start.4 = (f32[64,256]{1,0:T(8,128)S(1)}, f32[64,256]{1,0:T(8,128)}, u32[]{:S(2)}) copy-start(f32[64,256]{1,0:T(8,128)} %param.13) | copy-start | bytes 196612
  744.3 68.6 %copy-start.2 = (f32[64,256]{1,0:T(8,128)}, f32[64,256]{1,0:T(8,128)S(1)}, u32[]{:S(2)}) copy-start(f32[64,256]{1,0:T(8,128)S(1)} %get-tuple-element.72) | copy-start | bytes 196612
Sparse Core Ops, SparseCore 0:
  10.3 64.4 all-gather.3
  79.4 59.2 all-gather.5
  143.4 59.2 all-gather.7
  381.0 139.2 reduce-scatter.2
  524.9 144.7 reduce-scatter.4
where the time goes:
time: 820 us; the launch traced here: 819 us
  waiting for transfers between devices  466 us (57%)
  blocking collectives  226 us (28%)
  matrix products  101 us (12%)
  between operations  13.8 us (2%)
  other arithmetic  11.2 us (1%)
    reduce_scatter x1, waiting for transfers between devices, local(): lax.psum_scatter(inner_terms, 'row', scatter_dimension=1, tiled=True)  145 us
    reduce_scatter x1, waiting for transfers between devices, local(): lax.psum_scatter(outer_terms, 'row', scatter_dimension=1, tiled=True)  139 us
    psum x1, blocking collectives, local(): summed_all = lax.psum(partial_sums, ('grp', 'row'))  85.9 us
    psum x1, blocking collectives, local(): old_norm = lax.psum(jnp.sum(residual * residual, axis=1), 'row')  72.6 us
    psum x1, blocking collectives, local(): new_norm = lax.psum(jnp.sum(next_residual * next_residual, axis=1), 'row')  67.9 us
    all_gather x1, waiting for transfers between devices, local(): lax.all_gather(direction_half, 'row', axis=1, tiled=True)  66 us
    all_gather x1, waiting for transfers between devices, local(): lax.all_gather(inner_half, 'row', axis=1, tiled=True)  59.4 us
    all_gather x1, waiting for transfers between devices, local(): lax.all_gather(outer_rows.astype(jnp.bfloat16), 'row', axis=1, tiled=True)  56.4 us
  transfers between devices with their start and end apart: 5, of which 5 were waited for; matrix products, arithmetic and copies ran while one was open for 0% of the time, Pallas kernels for 0%

commit v1 on v0

v1 whole, which is shorter than its diff:
```python
import functools
import jax
import jax.numpy as jnp
from jax import lax
from jax.sharding import Mesh, PartitionSpec as P
from jax.experimental import pallas as pl
from jax.experimental.pallas import tpu as pltpu

ridge_weight = 0.5
bf16, f32 = jnp.bfloat16, jnp.float32
ROW = ("zl", "x", "c")
GRP = ("zh", "y")
CHIPS = ("zh", "y", "zl", "x")
ALL = GRP + ROW
LAST = (((1,), (1,)), ((), ()))
VM = pl.BlockSpec(memory_space=pltpu.VMEM)
SM = pl.BlockSpec(memory_space=pltpu.SMEM)


def call(body, outs, args, specs=None, scratch=(), vmem=None, name=None):
    return pl.pallas_call(
        body,
        out_shape=outs,
        in_specs=specs or [VM] * len(args),
        out_specs=jax.tree.map(lambda _: VM, outs),
        scratch_shapes=scratch,
        compiler_params=pltpu.CompilerParams(vmem_limit_bytes=vmem),
        name=name,
    )(*args)


def sds(shape, dtype):
    return jax.ShapeDtypeStruct(shape, dtype)


def exchange(v, axes):
    return lax.all_to_all(v, axes, 0, 0, tiled=True)


def prep_body(g_ref, d_ref, out_ref):
    d = d_ref[pl.ds(pl.multiple_of(g_ref[0] * 8, 8), 8), :]
    hi = d.astype(bf16)
    lo = (d - hi.astype(f32)).astype(bf16)
    both = jnp.concatenate([hi, lo], axis=0)
    for r in range(out_ref.shape[0]):
        out_ref[r] = both


def rows_dot(x_ref, f_ref):
    acc = None
    for r in range(x_ref.shape[0]):
        part = lax.dot_general(
            x_ref[r], f_ref[:, r * 256 : (r + 1) * 256], LAST, preferred_element_type=f32
        )
        acc = part if acc is None else acc + part
    return acc


def inner_body(x_ref, f_ref, term_ref, full_ref, out_ref):
    acc = rows_dot(x_ref, f_ref)
    term_ref[...] = acc[:8]
    full_ref[...] = acc[:8] + acc[8:]
    half = acc[:8].astype(bf16)
    for r in range(out_ref.shape[0]):
        out_ref[r] = half


def outer_body(x_ref, f_ref, out_ref):
    half = rows_dot(x_ref, f_ref).astype(bf16)
    for r in range(out_ref.shape[0]):
        out_ref[r] = half


def pieces(rows, lane):
    wide = rows.astype(f32)
    norm = jnp.sum(wide * wide, axis=1, keepdims=True) * -0.5
    one = norm.astype(bf16).astype(f32)
    two = (norm - one).astype(bf16).astype(f32)
    three = norm - one - two
    return one, two, three


def with_norms(rows, first):
    lane = lax.broadcasted_iota(jnp.int32, rows.shape, 1)
    one, two, three = pieces(rows, lane)
    a, b = (0, 3) if first else (3, 0)
    extra = jnp.where(
        lane == a, one, jnp.where(lane == a + 1, two, jnp.where(lane == a + 2, three, 0.0))
    )
    extra = jnp.where((lane >= b) & (lane < b + 3), 1.0, extra)
    return jnp.concatenate([rows, extra.astype(bf16)], axis=1)


def kernel_body(c_ref, p_ref, cen_ref, w_ref, own_ref, oth_ref, k_ref, pa_ref, fit_ref):
    points = p_ref.shape[0]
    step = 256
    chunks = k_ref.shape[0]
    fit_ref[...] = jnp.zeros_like(fit_ref)
    for i in range(points // step):
        rows = pl.ds(i * step, step)
        pa_ref[rows, :] = with_norms(p_ref[rows, :], True)

    def first(j, carry):
        ca = with_norms(cen_ref[pl.ds(pl.multiple_of(j * 256, 256), 256), :], False)
        w = w_ref[j % 2, :, j // 2, :, :].reshape(64, 256)
        for i in range(points // step):
            rows = pl.ds(i * step, step)
            d = lax.dot_general(pa_ref[rows, :], ca, LAST, preferred_element_type=f32)
            k = jnp.exp(d * (8.0 / 128.0)).astype(bf16)
            k_ref[j, rows, :] = k
            fit_ref[:, rows] += lax.dot_general(w, k, LAST, preferred_element_type=f32)
        return carry

    lax.fori_loop(0, chunks, first, 0)
    fitted = fit_ref[...].astype(bf16)
    c = c_ref[0]

    def second(z, carry):
        for which, ref in ((0, own_ref), (1, oth_ref)):
            j = z * 2 + (c if which == 0 else 1 - c)
            n = jnp.dot(fitted, k_ref[j], preferred_element_type=f32)
            ref[:, z, :, :] = n.reshape(8, 8, 256).astype(ref.dtype)
        return carry

    lax.fori_loop(0, chunks // 2, second, 0)


def add_body(a_ref, b_ref, out_ref):
    out_ref[...] = (a_ref[...] + b_ref[...].astype(f32)).astype(out_ref.dtype)


def sum_blocks(ref, lanes=None):
    parts = [
        (ref[r] if lanes is None else ref[r, :, lanes[0] : lanes[1]]).astype(f32)
        for r in range(ref.shape[0])
    ]
    while len(parts) > 1:
        parts = [a + b for a, b in zip(parts[::2], parts[1::2])]
    return parts[0]


def back_outer_body(x_ref, f_ref, out_ref):
    half = sum_blocks(x_ref).astype(bf16)
    for r in range(out_ref.shape[0]):
        out_ref[r] = jnp.dot(half, f_ref[:, r * 256 : (r + 1) * 256], preferred_element_type=f32)


def back_inner_body(count, g_ref, x_ref, f_ref, term_ref, full_ref, res_ref, out_ref):
    shaped = sum_blocks(x_ref) / count + ridge_weight * term_ref[...]
    half = shaped.astype(bf16)
    curve = jnp.sum(half.astype(f32) * full_ref[...], axis=1, keepdims=True)
    res = res_ref[pl.ds(pl.multiple_of(g_ref[0] * 8, 8), 8), :]
    old = jnp.sum(res * res, axis=1, keepdims=True)
    lane = lax.broadcasted_iota(jnp.int32, (8, 128), 1)
    extra = jnp.where(lane == 0, curve, old)
    for r in range(out_ref.shape[0]):
        out_ref[r, :, :256] = jnp.dot(
            half, f_ref[:, r * 256 : (r + 1) * 256], preferred_element_type=f32
        )
        out_ref[r, :, 256:] = extra


def step_body(g_ref, x_ref, res_ref, keep_ref, out_ref):
    image = sum_blocks(x_ref, (0, 256))
    extra = sum_blocks(x_ref, (256, 384))
    curve, old = extra[:, 0:1], extra[:, 1:2]
    alpha = old / curve
    res = res_ref[pl.ds(pl.multiple_of(g_ref[0] * 8, 8), 8), :]
    new = res - alpha * image
    keep_ref[:, :256] = new
    lane = lax.broadcasted_iota(jnp.int32, (8, 128), 1)
    keep_ref[:, 256:] = jnp.where(lane == 0, alpha, old)
    part = jnp.broadcast_to(jnp.sum(new * new, axis=1, keepdims=True), (8, 128))
    for r in range(out_ref.shape[0]):
        out_ref[r] = part


def beta_body(x_ref, keep_ref, out_ref):
    total = sum_blocks(x_ref)
    new, extra = keep_ref[:, :256], keep_ref[:, 256:]
    lane = lax.broadcasted_iota(jnp.int32, (8, 128), 1)
    beta = total[:, 0:1] / extra[:, 1:2]
    extra = jnp.where(lane == 0, extra, beta)
    for r in range(out_ref.shape[0]):
        out_ref[r, :, :256] = new
        out_ref[r, :, 256:] = extra


def final_body(x_ref, it_ref, d_ref, ni_ref, nr_ref, nd_ref):
    for g in range(x_ref.shape[0]):
        rows = slice(g * 8, g * 8 + 8)
        new = x_ref[g, :, :256]
        alpha = x_ref[g, :, 256:257]
        beta = x_ref[g, :, 257:258]
        d = d_ref[rows, :]
        ni_ref[rows, :] = it_ref[rows, :] + alpha * d
        nr_ref[rows, :] = new
        nd_ref[rows, :] = new + beta * d


def local(points, centers, inner_factor, outer_factor, iterate, residual, direction):
    g = (lax.axis_index("zh") * 4 + lax.axis_index("y")).reshape(1)
    c = lax.axis_index("c").reshape(1)
    count = float(points.shape[0] * 256)
    x = call(prep_body, sds((32, 16, 256), bf16), (g, direction), [SM, VM], name="prep")
    x = exchange(x, ROW)
    term, full, x = call(
        inner_body,
        (sds((8, 256), f32), sds((8, 256), f32), sds((32, 8, 256), bf16)),
        (x, inner_factor),
        name="inner",
    )
    x = exchange(x, ROW)
    x = call(outer_body, sds((128, 8, 256), bf16), (x, outer_factor), name="outer")
    x = exchange(x, CHIPS)
    w = lax.all_gather(x, "c", axis=0, tiled=False).reshape(2, 8, 16, 8, 256)
    own, other = call(
        kernel_body,
        (sds((8, 16, 8, 256), f32), sds((8, 16, 8, 256), f32)),
        (c, points, centers, w),
        [SM, VM, VM, VM],
        scratch=[
            pltpu.VMEM((32, points.shape[0], 256), bf16),
            pltpu.VMEM((points.shape[0], 256), bf16),
            pltpu.VMEM((64, points.shape[0]), f32),
        ],
        vmem=56 * 1024 * 1024,
        name="kernel",
    )
    other = lax.ppermute(other, "c", [(0, 1), (1, 0)])
    x = call(add_body, sds((8, 16, 8, 256), bf16), (own, other), name="add")
    x = exchange(x.reshape(128, 8, 256), CHIPS)
    x = call(back_outer_body, sds((32, 8, 256), f32), (x, outer_factor), name="back_outer")
    x = exchange(x, ROW)
    x = call(
        functools.partial(back_inner_body, count),
        sds((32, 8, 384), f32),
        (g, x, inner_factor, term, full, residual),
        [SM] + [VM] * 5,
        name="back_inner",
    )
    x = exchange(x, ROW)
    keep, x = call(
        step_body,
        (sds((8, 384), f32), sds((32, 8, 128), f32)),
        (g, x, residual),
        [SM, VM, VM],
        name="step",
    )
    x = exchange(x, ROW)
    x = call(beta_body, sds((8, 8, 384), f32), (x, keep), name="beta")
    x = exchange(x, GRP)
    out = sds((64, 256), f32)
    return call(final_body, (out, out, out), (x, iterate, direction), name="final")


def solution(mesh):
    fine = Mesh(mesh.devices.reshape(2, 4, 4, 4, 2), ("zh", "y", "zl", "x", "c"))
    placed = (
        P(ALL, None),
        P(),
        P(ROW, None),
        P(ROW, None),
        P(None, ROW),
        P(None, ROW),
        P(None, ROW),
    )
    return jax.shard_map(
        local,
        mesh=fine,
        in_specs=placed,
        out_specs=(P(None, ROW),) * 3,
        check_vma=False,
    )
```

time: 820 us -> 256 us (0.31)
  waiting for transfers between devices: 466 us -> 12.6 us
  matrix products: 101 us -> 0 us
  Pallas kernels: 0 us -> 68 us
  blocking collectives: 226 us -> 159 us
  other arithmetic: 11.2 us -> 0 us
    reduce_scatter x2 -> x0, waiting for transfers between devices: 284 us -> none  [the longest x1 145 us: local(): lax.psum_scatter(inner_terms, 'row', scatter_dimension=1, tiled=True)]
    psum x3 -> x0, blocking collectives: 226 us -> none  [the longest x1 85.9 us: local(): summed_all = lax.psum(partial_sums, ('grp', 'row'))]
    all_gather x3 -> x1, waiting for transfers between devices: 182 us -> 9.91 us  [local(): w = lax.all_gather(x, 'c', axis=0, tiled=False).reshape(2, 8, 16, 8, 256)]
    all_to_all x0 -> x8, blocking collectives: none -> 159 us  [exchange(): return lax.all_to_all(v, axes, 0, 0, tiled=True)]
    dot_general x12 -> x0, matrix products: 101 us -> none  [the longest x4 47.4 us: one_block(): jnp.dot(fitted, kernel_block, preferred_element_type=jnp.float32)]
    pallas_call x0 -> x10, Pallas kernels: none -> 68 us  [call(): pl.pallas_call(body, out_shape=outs, in_specs=specs or [VM] * len(args),...]
    reduce_sum x8 -> x0, other arithmetic: 9.03 us -> none  [the longest x4 4.21 us: kernel_rows(): point_norms = jnp.sum(point_wide * point_wide, axis=1)]
  transfers between devices with their start and end apart: 5 -> 2, of which waited for: 5 -> 2; matrix products, arithmetic and copies ran while one was open for 0% -> 0% of each run, Pallas kernels for 0% -> 0%
where the time goes in v1:
time: 256 us; the launch traced here: 255 us
  blocking collectives  159 us (62%)
  Pallas kernels  68 us (27%)
  between operations  14 us (5%)
  waiting for transfers between devices  12.6 us (5%)
    all_to_all x8, blocking collectives, exchange(): return lax.all_to_all(v, axes, 0, 0, tiled=True)  159 us
    pallas_call x10, Pallas kernels, call(): pl.pallas_call(body, out_shape=outs, in_specs=specs or [VM] * len(args),...  68 us
    all_gather x1, waiting for transfers between devices, local(): w = lax.all_gather(x, 'c', axis=0, tiled=False).reshape(2, 8, 16, 8, 256)  9.91 us
  transfers between devices with their start and end apart: 2, of which 2 were waited for; matrix products, arithmetic and copies ran while one was open for 0% of the time, Pallas kernels for 0%

profile of v1, /device:TPU:1, one launch (start us, length us, event | category | flops | bytes accessed | tf_op | source)
XLA Modules:
  0.0 255.4 jit_solution(2589225748613454931)
XLA Ops:
  7.2 0.0 all-gather.3.cloned.1.call-start
  7.2 1.6 prep.1
  8.8 21.2 %all_to_all.40.x_ref = bf16[32,16,256]{2,1,0:T(8,128)(2,1)} all-to-all(bf16[32,16,256]{2,1,0:T(8,128)(2,1)} %prep.1), channel_id=1, replica_groups=mesh['zh'=2,'y'=4,'zl'=4,'x'=4,'c'=2] {'zl','x','c'}, dimensions={0} | all-to-all | bytes 524288 | tf_op jit(solution)/shard_map/all_to_all | solution.py:37
  30.0 4.1 %inner.1 = (f32[8,256]{1,0:T(8,128)}, f32[8,256]{1,0:T(8,128)}, bf16[32,8,256]{2,1,0:T(8,128)(2,1)}) custom-call(bf16[32,16,256]{2,1,0:T(8,128)(2,1)} %all_to_all.40.x_ref, bf16[256,8192]{1,0:T(8,128)(2,1)} %f_ref.7), custom_call_target="tpu_custom_call" | custom-call | tf_op jit(solution)/shard_map/inner/pallas_call | solution.py:21
  34.1 13.0 %all_to_all.41.x_ref = bf16[32,8,256]{2,1,0:T(8,128)(2,1)} all-to-all(bf16[32,8,256]{2,1,0:T(8,128)(2,1)} %get-tuple-element.10), channel_id=1, replica_groups=mesh['zh'=2,'y'=4,'zl'=4,'x'=4,'c'=2] {'zl','x','c'}, dimensions={0} | all-to-all | bytes 262144 | tf_op jit(solution)/shard_map/all_to_all | solution.py:37
  47.2 4.3 %outer.1 = bf16[128,8,256]{2,1,0:T(8,128)(2,1)} custom-call(bf16[32,8,256]{2,1,0:T(8,128)(2,1)} %all_to_all.41.x_ref, bf16[256,8192]{1,0:T(8,128)(2,1)} %f_ref.6), custom_call_target="tpu_custom_call" | custom-call | tf_op jit(solution)/shard_map/outer/pallas_call | solution.py:21
  51.4 30.3 %all_to_all.42 = bf16[128,8,256]{2,1,0:T(8,128)(2,1)} all-to-all(bf16[128,8,256]{2,1,0:T(8,128)(2,1)} %outer.1), channel_id=1, replica_groups=mesh['zh'=2,'y'=4,'zl'=4,'x'=4,'c'=2] {'zh','y','zl','x'}, dimensions={0} | all-to-all | bytes 1048576 | tf_op jit(solution)/shard_map/all_to_all | solution.py:37
  81.7 0.0 all-gather.3.cloned.1.call-update
  81.8 9.9 %all-gather.3.cloned.1.call-done = bf16[256,8,256]{2,1,0:T(8,128)(2,1)} async-done(((bf16[128,8,256]{2,1,0:T(8,128)(2,1)}), bf16[256,8,256]{2,1,0:T(8,128)(2,1)}) %all-gather.3.cloned.1.call-update) | async-done | bytes 1048592 | tf_op jit(solution)/shard_map/all_gather | solution.py:216
  91.7 42.9 %kernel.1 = (f32[8,16,8,256]{3,2,1,0:T(8,128)}, f32[8,16,8,256]{3,2,1,0:T(8,128)}) custom-call(s32[1]{0:T(128)} %bitcast.1.c_ref, bf16[2048,128]{1,0:T(8,128)(2,1)} %p_ref.1, bf16[8192,128]{1,0:T(8,128)(2,1)} %cen_ref.1, bf16[2,8,16,8,256]{4,3,2,1,0:T(8,128)(2,1)} %bitcast.5), custom_call_target="tpu_custom_call" | custom-call | tf_op jit(solution)/shard_map/kernel/pallas_call | solution.py:21
  134.6 0.2 collective-permute-start
  134.8 2.7 %collective-permute-done.b_ref = f32[8,16,8,256]{3,2,1,0:T(8,128)S(1)} collective-permute-done((f32[8,16,8,256]{3,2,1,0:T(8,128)}, f32[8,16,8,256]{3,2,1,0:T(8,128)S(1)}, u32[]{:S(2)}, u32[]{:S(2)}) %collective-permute-start) | collective-permute-done | bytes 1048608 | tf_op jit(solution)/shard_map/ppermute | solution.py:230
  137.5 1.0 copy-done
  138.5 2.4 add.5
  140.9 33.0 %all_to_all.43.x_ref = bf16[128,8,256]{2,1,0:T(8,128)(2,1)} all-to-all(bf16[128,8,256]{2,1,0:T(8,128)(2,1)} %bitcast.4), channel_id=1, replica_groups=mesh['zh'=2,'y'=4,'zl'=4,'x'=4,'c'=2] {'zh','y','zl','x'}, dimensions={0} | all-to-all | bytes 1048576 | tf_op jit(solution)/shard_map/all_to_all | solution.py:37
  173.9 3.8 %back_outer.1 = f32[32,8,256]{2,1,0:T(8,128)} custom-call(bf16[128,8,256]{2,1,0:T(8,128)(2,1)} %all_to_all.43.x_ref, bf16[256,8192]{1,0:T(8,128)(2,1)} %f_ref.6), custom_call_target="tpu_custom_call" | custom-call | tf_op jit(solution)/shard_map/back_outer/pallas_call | solution.py:21
  177.7 17.6 %all_to_all.44.x_ref = f32[32,8,256]{2,1,0:T(8,128)} all-to-all(f32[32,8,256]{2,1,0:T(8,128)} %back_outer.1), channel_id=1, replica_groups=mesh['zh'=2,'y'=4,'zl'=4,'x'=4,'c'=2] {'zl','x','c'}, dimensions={0} | all-to-all | bytes 524288 | tf_op jit(solution)/shard_map/all_to_all | solution.py:37
  195.3 3.6 %back_inner.1 = f32[32,8,384]{2,1,0:T(8,128)} custom-call(s32[1]{0:T(128)} %bitcast.g_ref, f32[32,8,256]{2,1,0:T(8,128)} %all_to_all.44.x_ref, bf16[256,8192]{1,0:T(8,128)(2,1)} %f_ref.7, f32[8,256]{1,0:T(8,128)} %get-tuple-element.13.term_ref, f32[8,256]{1,0:T(8,128)} %get-tuple-element.14.full_ref, f32[64,256]{1,0:T(8,128)} %res_ref.3), custom_call_target="tpu_custom_call" | custom-call | tf_op jit(solution)/shard_map/back_inner/pallas_call | solution.py:21
  199.0 18.3 %all_to_all.45.x_ref = f32[32,8,384]{2,1,0:T(8,128)} all-to-all(f32[32,8,384]{2,1,0:T(8,128)} %back_inner.1), channel_id=1, replica_groups=mesh['zh'=2,'y'=4,'zl'=4,'x'=4,'c'=2] {'zl','x','c'}, dimensions={0} | all-to-all | bytes 786432 | tf_op jit(solution)/shard_map/all_to_all | solution.py:37
  217.3 1.9 step.1
  219.2 12.9 %all_to_all.46.x_ref = f32[32,8,128]{2,1,0:T(8,128)} all-to-all(f32[32,8,128]{2,1,0:T(8,128)} %get-tuple-element.15), channel_id=1, replica_groups=mesh['zh'=2,'y'=4,'zl'=4,'x'=4,'c'=2] {'zl','x','c'}, dimensions={0} | all-to-all | bytes 262144 | tf_op jit(solution)/shard_map/all_to_all | solution.py:37
  232.0 1.7 beta.1
  233.7 13.2 %all_to_all.47.x_ref = f32[8,8,384]{2,1,0:T(8,128)} all-to-all(f32[8,8,384]{2,1,0:T(8,128)} %beta.1), channel_id=1, replica_groups=mesh['zh'=2,'y'=4,'zl'=4,'x'=4,'c'=2] {'zh','y'}, dimensions={0} | all-to-all | bytes 196608 | tf_op jit(solution)/shard_map/all_to_all | solution.py:37
  246.9 1.7 final.1
  (1 shorter events, 0.0 us)
Async XLA Ops:
  7.2 84.5 %all-gather.3.cloned.1.call-start = ((), (), s32[]{:S(2)}) async-start(), calls=%async_computation.8 | async-start | bytes 1572864 | tf_op jit(solution)/shard_map/all_gather | solution.py:216
  134.6 2.9 %collective-permute-start = (f32[8,16,8,256]{3,2,1,0:T(8,128)}, f32[8,16,8,256]{3,2,1,0:T(8,128)S(1)}, u32[]{:S(2)}, u32[]{:S(2)}) collective-permute-start(f32[8,16,8,256]{3,2,1,0:T(8,128)} %get-tuple-element.12), channel_id=1, source_target_pairs={{0,1},{1,0},{2,3},{3,2},{4,5},{5,4},{6,7},{7,6},{8,9},{9,8},{10,11... | collective-permute-start | bytes 3145736 | tf_op jit(solution)/shard_map/ppermute | solution.py:230
  137.5 1.0 copy-start
Sparse Core Ops, SparseCore 0:
  81.9 9.7 all-gather.2

commit v2 on v1

--- a/solution.py
+++ b/solution.py
@@ -12,19 +12,22 @@
 GRP = ("zh", "y")
 CHIPS = ("zh", "y", "zl", "x")
 ALL = GRP + ROW
+SWAP = [(0, 1), (1, 0)]
+LOG2E = 1.4426950408889634
+MIB = 1024 * 1024
 LAST = (((1,), (1,)), ((), ()))
 VM = pl.BlockSpec(memory_space=pltpu.VMEM)
 SM = pl.BlockSpec(memory_space=pltpu.SMEM)
 
 
-def call(body, outs, args, specs=None, scratch=(), vmem=None, name=None):
+def call(body, outs, args, specs=None, scratch=(), vmem=16, name=None):
     return pl.pallas_call(
         body,
         out_shape=outs,
         in_specs=specs or [VM] * len(args),
         out_specs=jax.tree.map(lambda _: VM, outs),
         scratch_shapes=scratch,
-        compiler_params=pltpu.CompilerParams(vmem_limit_bytes=vmem),
+        compiler_params=pltpu.CompilerParams(vmem_limit_bytes=vmem * MIB),
         name=name,
     )(*args)
 
@@ -71,58 +74,97 @@
         out_ref[r] = half
 
 
-def pieces(rows, lane):
+def norm_lanes(rows, first):
     wide = rows.astype(f32)
+    lane = lax.broadcasted_iota(jnp.int32, (1, 128), 1)
     norm = jnp.sum(wide * wide, axis=1, keepdims=True) * -0.5
     one = norm.astype(bf16).astype(f32)
-    two = (norm - one).astype(bf16).astype(f32)
-    three = norm - one - two
-    return one, two, three
-
-
-def with_norms(rows, first):
-    lane = lax.broadcasted_iota(jnp.int32, rows.shape, 1)
-    one, two, three = pieces(rows, lane)
+    rest = norm - one
+    two = rest.astype(bf16).astype(f32)
+    three = rest - two
     a, b = (0, 3) if first else (3, 0)
-    extra = jnp.where(
-        lane == a, one, jnp.where(lane == a + 1, two, jnp.where(lane == a + 2, three, 0.0))
-    )
-    extra = jnp.where((lane >= b) & (lane < b + 3), 1.0, extra)
-    return jnp.concatenate([rows, extra.astype(bf16)], axis=1)
-
-
-def kernel_body(c_ref, p_ref, cen_ref, w_ref, own_ref, oth_ref, k_ref, pa_ref, fit_ref):
-    points = p_ref.shape[0]
+    ones = jnp.where((lane >= b) & (lane < b + 3), 1.0, 0.0)
+    out = jnp.where(lane == a + 2, three, ones)
+    out = jnp.where(lane == a + 1, two, out)
+    return jnp.where(lane == a, one, out).astype(bf16)
+
+
+def kernel_body(
+    c_ref, p_ref, cen_ref, wo_ref, wx_ref, own_ref, oth_ref,
+    k_ref, pa_ref, ca_ref, fit_ref, even_ref, odd_ref,
+):
+    nz = k_ref.shape[0]
     step = 256
-    chunks = k_ref.shape[0]
+    parts = p_ref.shape[0] // step
+    c = c_ref[0]
     fit_ref[...] = jnp.zeros_like(fit_ref)
-    for i in range(points // step):
+    pa_ref[:, :128] = p_ref[...]
+    for i in range(parts):
         rows = pl.ds(i * step, step)
-        pa_ref[rows, :] = with_norms(p_ref[rows, :], True)
-
-    def first(j, carry):
-        ca = with_norms(cen_ref[pl.ds(pl.multiple_of(j * 256, 256), 256), :], False)
-        w = w_ref[j % 2, :, j // 2, :, :].reshape(64, 256)
-        for i in range(points // step):
-            rows = pl.ds(i * step, step)
-            d = lax.dot_general(pa_ref[rows, :], ca, LAST, preferred_element_type=f32)
-            k = jnp.exp(d * (8.0 / 128.0)).astype(bf16)
-            k_ref[j, rows, :] = k
-            fit_ref[:, rows] += lax.dot_general(w, k, LAST, preferred_element_type=f32)
+        pa_ref[rows, 128:] = norm_lanes(p_ref[rows, :], True)
+
+    def load(z, slot):
+        for h in range(2):
+            start = pl.multiple_of((z * 2 + (c if h == 0 else 1 - c)) * 256, 256)
+            block = cen_ref[pl.ds(start, 256), :]
+            ca_ref[slot, h * 256 : h * 256 + 256, :128] = block
+            ca_ref[slot, h * 256 : h * 256 + 256, 128:] = norm_lanes(block, False)
+
+    def fill(z, slot, buf, i):
+        rows = pl.ds(i * step, step)
+        for h in range(2):
+            cols = slice(h * 256, h * 256 + 256)
+            d = lax.dot_general(
+                pa_ref[rows, :], ca_ref[slot, cols, :], LAST, preferred_element_type=f32
+            )
+            k = jnp.exp2(d * (LOG2E * 8.0 / 128.0)).astype(bf16)
+            k_ref[z, rows, cols] = k
+            buf[rows, cols] = k
+
+    def weights(z):
+        own = wo_ref[:, z, :, :].reshape(64, 256)
+        return jnp.concatenate([own, wx_ref[:, z, :, :].reshape(64, 256)], axis=1)
+
+    def fit(w, buf, i):
+        rows = pl.ds(i * step, step)
+        fit_ref[rows, :] += lax.dot_general(buf[rows, :], w, LAST, preferred_element_type=f32)
+
+    load(0, 0)
+    load(1, 1)
+    for i in range(parts):
+        fill(0, 0, even_ref, i)
+
+    def pair(h, carry):
+        z = 2 * h + 1
+        w = weights(z - 1)
+        for i in range(parts):
+            fit(w, even_ref, i)
+            fill(z, 1, odd_ref, i)
+        load(z + 1, 0)
+        w = weights(z)
+        for i in range(parts):
+            fit(w, odd_ref, i)
+            fill(z + 1, 0, even_ref, i)
+        load(z + 2, 1)
         return carry
 
-    lax.fori_loop(0, chunks, first, 0)
-    fitted = fit_ref[...].astype(bf16)
-    c = c_ref[0]
+    lax.fori_loop(0, nz // 2 - 1, pair, 0)
+    w = weights(nz - 2)
+    for i in range(parts):
+        fit(w, even_ref, i)
+        fill(nz - 1, 1, odd_ref, i)
+    w = weights(nz - 1)
+    for i in range(parts):
+        fit(w, odd_ref, i)
+    fitted = fit_ref[...].T.astype(bf16)
 
     def second(z, carry):
-        for which, ref in ((0, own_ref), (1, oth_ref)):
-            j = z * 2 + (c if which == 0 else 1 - c)
-            n = jnp.dot(fitted, k_ref[j], preferred_element_type=f32)
+        for h, ref in ((0, own_ref), (1, oth_ref)):
+            n = jnp.dot(fitted, k_ref[z, :, h * 256 : h * 256 + 256], preferred_element_type=f32)
             ref[:, z, :, :] = n.reshape(8, 8, 256).astype(ref.dtype)
         return carry
 
-    lax.fori_loop(0, chunks // 2, second, 0)
+    lax.fori_loop(0, nz, second, 0, unroll=2)
 
 
 def add_body(a_ref, b_ref, out_ref):
@@ -213,21 +255,24 @@
     x = exchange(x, ROW)
     x = call(outer_body, sds((128, 8, 256), bf16), (x, outer_factor), name="outer")
     x = exchange(x, CHIPS)
-    w = lax.all_gather(x, "c", axis=0, tiled=False).reshape(2, 8, 16, 8, 256)
+    x = x.reshape(8, 16, 8, 256)
     own, other = call(
         kernel_body,
         (sds((8, 16, 8, 256), f32), sds((8, 16, 8, 256), f32)),
-        (c, points, centers, w),
-        [SM, VM, VM, VM],
+        (c, points, centers, x, lax.ppermute(x, "c", SWAP)),
+        [SM] + [VM] * 4,
         scratch=[
-            pltpu.VMEM((32, points.shape[0], 256), bf16),
+            pltpu.VMEM((16, points.shape[0], 512), bf16),
             pltpu.VMEM((points.shape[0], 256), bf16),
-            pltpu.VMEM((64, points.shape[0]), f32),
+            pltpu.VMEM((2, 512, 256), bf16),
+            pltpu.VMEM((points.shape[0], 64), f32),
+            pltpu.VMEM((points.shape[0], 512), bf16),
+            pltpu.VMEM((points.shape[0], 512), bf16),
         ],
-        vmem=56 * 1024 * 1024,
+        vmem=48,
         name="kernel",
     )
-    other = lax.ppermute(other, "c", [(0, 1), (1, 0)])
+    other = lax.ppermute(other, "c", SWAP)
     x = call(add_body, sds((8, 16, 8, 256), bf16), (own, other), name="add")
     x = exchange(x.reshape(128, 8, 256), CHIPS)
     x = call(back_outer_body, sds((32, 8, 256), f32), (x, outer_factor), name="back_outer")

time: 256 us -> 191 us (0.75)
  Pallas kernels: 68 us -> 32.6 us
  between operations: 14 us -> 0.72 us
  blocking collectives: 159 us -> 148 us
  waiting for transfers between devices: 12.6 us -> 3.96 us
    pallas_call x10, Pallas kernels: 68 us -> 32.6 us  [call(): pl.pallas_call(body, out_shape=outs, in_specs=specs or [VM] * len(args),...]
    all_to_all x8, blocking collectives: 159 us -> 148 us  [exchange(): return lax.all_to_all(v, axes, 0, 0, tiled=True)]
    all_gather x1 -> x0, waiting for transfers between devices: 9.91 us -> none  [local(): w = lax.all_gather(x, 'c', axis=0, tiled=False).reshape(2, 8, 16, 8, 256)]
    ppermute x1 -> x2, starting transfers between devices: 0.22 us -> 2.8 us  [the longest x1 2.34 us: local(): lax.ppermute(x, 'c', SWAP)]
where the time goes in v2:
time: 191 us
  blocking collectives  148 us (77%)
  Pallas kernels  32.6 us (17%)
  waiting for transfers between devices  3.96 us (2%)
  local copies, waits for them, and re-layouts  3.21 us (2%)
  starting transfers between devices  2.8 us (1%)
    all_to_all x8, blocking collectives, exchange(): return lax.all_to_all(v, axes, 0, 0, tiled=True)  148 us
    pallas_call x10, Pallas kernels, call(): pl.pallas_call(body, out_shape=outs, in_specs=specs or [VM] * len(args),...  32.6 us
  transfers between devices with their start and end apart: 2, of which 2 were waited for; matrix products, arithmetic and copies ran while one was open for 0% of the time, Pallas kernels for 0%

profile of v2, /device:TPU:1, one launch (start us, length us, event | category | flops | bytes accessed | tf_op | source)
XLA Modules:
  0.0 190.9 jit_solution(965109672566136924)
XLA Ops:
  0.6 0.0 copy-start
  0.7 1.0 copy-done.7
  1.7 21.0 %all_to_all.40.x_ref = bf16[32,16,256]{2,1,0:T(8,128)(2,1)S(1)} all-to-all(bf16[32,16,256]{2,1,0:T(8,128)(2,1)S(1)} %prep.1), channel_id=1, replica_groups=mesh['zh'=2,'y'=4,'zl'=4,'x'=4,'c'=2] {'zl','x','c'}, dimensions={0} | all-to-all | bytes 524288 | tf_op jit(solution)/shard_map/all_to_all | solution.py:40
  22.7 2.2 %copy-done.2 = bf16[256,8192]{1,0:T(8,128)(2,1)S(1)} copy-done((bf16[256,8192]{1,0:T(8,128)(2,1)S(1)}, bf16[256,8192]{1,0:T(8,128)(2,1)}, u32[]{:S(2)}) %copy-start.2) | copy-done | bytes 4194328
  24.9 1.2 inner.1
  26.1 12.3 %all_to_all.41.x_ref = bf16[32,8,256]{2,1,0:T(8,128)(2,1)S(1)} all-to-all(bf16[32,8,256]{2,1,0:T(8,128)(2,1)S(1)} %get-tuple-element.10), channel_id=1, replica_groups=mesh['zh'=2,'y'=4,'zl'=4,'x'=4,'c'=2] {'zl','x','c'}, dimensions={0} | all-to-all | bytes 262144 | tf_op jit(solution)/shard_map/all_to_all | solution.py:40
  38.4 1.2 outer.1
  39.6 30.0 %all_to_all.42 = bf16[128,8,256]{2,1,0:T(8,128)(2,1)S(1)} all-to-all(bf16[128,8,256]{2,1,0:T(8,128)(2,1)S(1)} %outer.1), channel_id=1, replica_groups=mesh['zh'=2,'y'=4,'zl'=4,'x'=4,'c'=2] {'zh','y','zl','x'}, dimensions={0} | all-to-all | bytes 1048576 | tf_op jit(solution)/shard_map/all_to_all | solution.py:40
  69.6 2.3 %collective-permute-start = (bf16[8,16,8,256]{3,2,1,0:T(8,128)(2,1)S(1)}, bf16[8,16,8,256]{3,2,1,0:T(8,128)(2,1)}, u32[]{:S(2)}, u32[]{:S(2)}) collective-permute-start(bf16[8,16,8,256]{3,2,1,0:T(8,128)(2,1)S(1)} %bitcast.5), channel_id=1, source_target_pairs={{0,1},{1,0},{2,3},{3,2},{4,5},{5,4},{6,7},{7,6},{8,9},{9,8},{10,11... | collective-permute-start | bytes 1572872 | tf_op jit(solution)/shard_map/ppermute | solution.py:262
  72.0 1.7 collective-permute-done.wx_ref
  73.6 27.6 %kernel.1 = (f32[8,16,8,256]{3,2,1,0:T(8,128)S(1)}, f32[8,16,8,256]{3,2,1,0:T(8,128)S(1)}) custom-call(s32[1]{0:T(128)} %bitcast.1.c_ref, bf16[2048,128]{1,0:T(8,128)(2,1)S(1)} %copy-done.5, bf16[8192,128]{1,0:T(8,128)(2,1)S(1)} %copy-done.4, bf16[8,16,8,256]{3,2,1,0:T(8,128)(2,1)S(1)} %bitcast.6, bf16[8,16,8,256]{3,2,1,0:T(8,128)(2,1)} %collective-permute-done.wx_ref), custom_call_target="tpu_custom_call" | custom-call | tf_op jit(solution)/shard_map/kernel/pallas_call | solution.py:24
  101.2 0.5 collective-permute-start.1
  101.7 2.3 %collective-permute-done.1.b_ref = f32[8,16,8,256]{3,2,1,0:T(8,128)S(1)} collective-permute-done((f32[8,16,8,256]{3,2,1,0:T(8,128)S(1)}, f32[8,16,8,256]{3,2,1,0:T(8,128)S(1)}, u32[]{:S(2)}, u32[]{:S(2)}) %collective-permute-start.1) | collective-permute-done | bytes 1048608 | tf_op jit(solution)/shard_map/ppermute | solution.py:275
  104.0 0.1 add.5
  104.1 25.2 %all_to_all.43.x_ref = bf16[128,8,256]{2,1,0:T(8,128)(2,1)S(1)} all-to-all(bf16[128,8,256]{2,1,0:T(8,128)(2,1)S(1)} %bitcast.4), channel_id=1, replica_groups=mesh['zh'=2,'y'=4,'zl'=4,'x'=4,'c'=2] {'zh','y','zl','x'}, dimensions={0} | all-to-all | bytes 1048576 | tf_op jit(solution)/shard_map/all_to_all | solution.py:40
  129.3 0.7 back_outer.1
  130.0 16.4 %all_to_all.44.x_ref = f32[32,8,256]{2,1,0:T(8,128)S(1)} all-to-all(f32[32,8,256]{2,1,0:T(8,128)S(1)} %back_outer.1), channel_id=1, replica_groups=mesh['zh'=2,'y'=4,'zl'=4,'x'=4,'c'=2] {'zl','x','c'}, dimensions={0} | all-to-all | bytes 524288 | tf_op jit(solution)/shard_map/all_to_all | solution.py:40
  146.5 0.7 back_inner.1
  147.1 17.4 %all_to_all.45.x_ref = f32[32,8,384]{2,1,0:T(8,128)S(1)} all-to-all(f32[32,8,384]{2,1,0:T(8,128)S(1)} %back_inner.1), channel_id=1, replica_groups=mesh['zh'=2,'y'=4,'zl'=4,'x'=4,'c'=2] {'zl','x','c'}, dimensions={0} | all-to-all | bytes 786432 | tf_op jit(solution)/shard_map/all_to_all | solution.py:40
  164.5 0.2 step.1
  164.8 12.3 %all_to_all.46.x_ref = f32[32,8,128]{2,1,0:T(8,128)S(1)} all-to-all(f32[32,8,128]{2,1,0:T(8,128)S(1)} %get-tuple-element.15), channel_id=1, replica_groups=mesh['zh'=2,'y'=4,'zl'=4,'x'=4,'c'=2] {'zl','x','c'}, dimensions={0} | all-to-all | bytes 262144 | tf_op jit(solution)/shard_map/all_to_all | solution.py:40
  177.0 0.1 beta.1
  177.2 12.9 %all_to_all.47.x_ref = f32[8,8,384]{2,1,0:T(8,128)S(1)} all-to-all(f32[8,8,384]{2,1,0:T(8,128)S(1)} %beta.1), channel_id=1, replica_groups=mesh['zh'=2,'y'=4,'zl'=4,'x'=4,'c'=2] {'zh','y'}, dimensions={0} | all-to-all | bytes 196608 | tf_op jit(solution)/shard_map/all_to_all | solution.py:40
  190.1 0.7 final.1
  (18 shorter events, 0.1 us)
Async XLA Ops:
  0.6 37.7 %copy-start = (bf16[256,8192]{1,0:T(8,128)(2,1)S(1)}, bf16[256,8192]{1,0:T(8,128)(2,1)}, u32[]{:S(2)}) copy-start(bf16[256,8192]{1,0:T(8,128)(2,1)} %f_ref.6) | copy-start | bytes 12582916
  0.6 1.0 copy-start.7
  22.7 2.2 %copy-start.2 = (bf16[256,8192]{1,0:T(8,128)(2,1)S(1)}, bf16[256,8192]{1,0:T(8,128)(2,1)}, u32[]{:S(2)}) copy-start(bf16[256,8192]{1,0:T(8,128)(2,1)} %f_ref.7) | copy-start | bytes 12582916
  26.1 47.5 %copy-start.4 = (bf16[8192,128]{1,0:T(8,128)(2,1)S(1)}, bf16[8192,128]{1,0:T(8,128)(2,1)}, u32[]{:S(2)}) copy-start(bf16[8192,128]{1,0:T(8,128)(2,1)} %cen_ref.1) | copy-start | bytes 6291460
  26.1 47.5 %copy-start.5 = (bf16[2048,128]{1,0:T(8,128)(2,1)S(1)}, bf16[2048,128]{1,0:T(8,128)(2,1)}, u32[]{:S(2)}) copy-start(bf16[2048,128]{1,0:T(8,128)(2,1)} %p_ref.1) | copy-start | bytes 1572868
  69.6 4.0 %collective-permute-start = (bf16[8,16,8,256]{3,2,1,0:T(8,128)(2,1)S(1)}, bf16[8,16,8,256]{3,2,1,0:T(8,128)(2,1)}, u32[]{:S(2)}, u32[]{:S(2)}) collective-permute-start(bf16[8,16,8,256]{3,2,1,0:T(8,128)(2,1)S(1)} %bitcast.5), channel_id=1, source_target_pairs={{0,1},{1,0},{2,3},{3,2},{4,5},{5,4},{6,7},{7,6},{8,9},{9,8},{10,11... | collective-permute-start | bytes 1572872 | tf_op jit(solution)/shard_map/ppermute | solution.py:262
  72.0 57.3 %copy-start.1 = (bf16[256,8192]{1,0:T(8,128)(2,1)S(1)}, bf16[256,8192]{1,0:T(8,128)(2,1)}, u32[]{:S(2)}) copy-start(bf16[256,8192]{1,0:T(8,128)(2,1)} %f_ref.6) | copy-start | bytes 12582916
  101.2 2.7 %collective-permute-start.1 = (f32[8,16,8,256]{3,2,1,0:T(8,128)S(1)}, f32[8,16,8,256]{3,2,1,0:T(8,128)S(1)}, u32[]{:S(2)}, u32[]{:S(2)}) collective-permute-start(f32[8,16,8,256]{3,2,1,0:T(8,128)S(1)} %get-tuple-element.12), channel_id=1, source_target_pairs={{0,1},{1,0},{2,3},{3,2},{4,5},{5,4},{6,7},{7,6},{8,9},{9,8},{10,11... | collective-permute-start | bytes 3145736 | tf_op jit(solution)/shard_map/ppermute | solution.py:275
  104.0 42.5 %copy-start.3 = (bf16[256,8192]{1,0:T(8,128)(2,1)S(1)}, bf16[256,8192]{1,0:T(8,128)(2,1)}, u32[]{:S(2)}) copy-start(bf16[256,8192]{1,0:T(8,128)(2,1)} %f_ref.7) | copy-start | bytes 12582916
  104.0 42.5 %copy-start.6 = (f32[64,256]{1,0:T(8,128)S(1)}, f32[64,256]{1,0:T(8,128)}, u32[]{:S(2)}) copy-start(f32[64,256]{1,0:T(8,128)} %res_ref.3) | copy-start | bytes 196612
  130.0 60.1 %copy-start.8 = (f32[64,256]{1,0:T(8,128)S(1)}, f32[64,256]{1,0:T(8,128)}, u32[]{:S(2)}) copy-start(f32[64,256]{1,0:T(8,128)} %d_ref.3) | copy-start | bytes 196612
  130.0 60.1 %copy-start.9 = (f32[64,256]{1,0:T(8,128)S(1)}, f32[64,256]{1,0:T(8,128)}, u32[]{:S(2)}) copy-start(f32[64,256]{1,0:T(8,128)} %it_ref.1) | copy-start | bytes 196612

commit v3 on v2

v3 whole, which is shorter than its diff:
```python
import functools
import jax
import jax.numpy as jnp
from jax import lax
from jax.sharding import Mesh, PartitionSpec as P
from jax.experimental import pallas as pl
from jax.experimental.pallas import tpu as pltpu

ridge_weight = 0.5
bf16, f32 = jnp.bfloat16, jnp.float32
ROW = ("zl", "x", "c")
LINE = ("zl", "x")
CHIPS = ("y", "zl", "x")
ALL = ("zh", "y") + ROW
SWAP = [(0, 1), (1, 0)]
LOG2E = 1.4426950408889634
MIB = 1024 * 1024
LAST = (((1,), (1,)), ((), ()))
VM = pl.BlockSpec(memory_space=pltpu.VMEM)
SM = pl.BlockSpec(memory_space=pltpu.SMEM)


def call(body, outs, args, specs=None, scratch=(), vmem=16, name=None):
    return pl.pallas_call(
        body,
        out_shape=outs,
        in_specs=specs or [VM] * len(args),
        out_specs=jax.tree.map(lambda _: VM, outs),
        scratch_shapes=scratch,
        compiler_params=pltpu.CompilerParams(vmem_limit_bytes=vmem * MIB),
        name=name,
    )(*args)


def sds(shape, dtype):
    return jax.ShapeDtypeStruct(shape, dtype)


def exchange(v, axes):
    return lax.all_to_all(v, axes, 0, 0, tiled=True)


def own_rows(at_ref, ref):
    return ref[pl.ds(pl.multiple_of(at_ref[0] * 16, 16), 16), :]


def columns(at_ref, z, which):
    c = at_ref[1]
    return pl.ds(pl.multiple_of((2 * z + (c if which == 0 else 1 - c)) * 256, 256), 256)


def spread(value, ref):
    for r in range(ref.shape[0]):
        ref[r] = value


def fold(value):
    return jnp.concatenate([value[:8], value[8:]], axis=1)


def unfold(value):
    return jnp.concatenate([value[:, :256], value[:, 256:512]], axis=0)


def prep_body(at_ref, d_ref, out_ref):
    d = own_rows(at_ref, d_ref)
    hi = d.astype(bf16)
    lo = (d - hi.astype(f32)).astype(bf16)
    spread(jnp.concatenate([hi, lo], axis=0), out_ref)


def rows_dot(at_ref, x_ref, y_ref, f_ref):
    acc = None
    for which, ref in ((0, x_ref), (1, y_ref)):
        for z in range(ref.shape[0]):
            part = lax.dot_general(
                ref[z], f_ref[:, columns(at_ref, z, which)], LAST, preferred_element_type=f32
            )
            acc = part if acc is None else acc + part
    return acc


def inner_body(at_ref, x_ref, y_ref, f_ref, term_ref, full_ref, out_ref):
    acc = rows_dot(at_ref, x_ref, y_ref, f_ref)
    term_ref[...] = acc[:16]
    full_ref[...] = acc[:16] + acc[16:]
    spread(acc[:16].astype(bf16), out_ref)


def outer_body(at_ref, x_ref, y_ref, f_ref, out_ref):
    spread(rows_dot(at_ref, x_ref, y_ref, f_ref).astype(bf16), out_ref)


def norm_lanes(rows, first):
    wide = rows.astype(f32)
    lane = lax.broadcasted_iota(jnp.int32, (1, 128), 1)
    norm = jnp.sum(wide * wide, axis=1, keepdims=True) * -0.5
    one = norm.astype(bf16).astype(f32)
    rest = norm - one
    two = rest.astype(bf16).astype(f32)
    three = rest - two
    a, b = (0, 3) if first else (3, 0)
    ones = jnp.where((lane >= b) & (lane < b + 3), 1.0, 0.0)
    out = jnp.where(lane == a + 2, three, ones)
    out = jnp.where(lane == a + 1, two, out)
    return jnp.where(lane == a, one, out).astype(bf16)


def kernel_body(
    at_ref, p_ref, cen_ref, wo_ref, wx_ref, own_ref, oth_ref,
    k_ref, pa_ref, ca_ref, fit_ref, even_ref, odd_ref,
):
    nz = k_ref.shape[0]
    step = 256
    parts = p_ref.shape[0] // step
    c = at_ref[1]
    fit_ref[...] = jnp.zeros_like(fit_ref)
    pa_ref[:, :128] = p_ref[...]
    for i in range(parts):
        rows = pl.ds(i * step, step)
        pa_ref[rows, 128:] = norm_lanes(p_ref[rows, :], True)

    def load(z, slot):
        for h in range(2):
            start = pl.multiple_of((z * 2 + (c if h == 0 else 1 - c)) * 256, 256)
            block = cen_ref[pl.ds(start, 256), :]
            ca_ref[slot, h * 256 : h * 256 + 256, :128] = block
            ca_ref[slot, h * 256 : h * 256 + 256, 128:] = norm_lanes(block, False)

    def fill(z, slot, buf, i):
        rows = pl.ds(i * step, step)
        for h in range(2):
            cols = slice(h * 256, h * 256 + 256)
            d = lax.dot_general(
                pa_ref[rows, :], ca_ref[slot, cols, :], LAST, preferred_element_type=f32
            )
            k = jnp.exp2(d * (LOG2E * 8.0 / 128.0)).astype(bf16)
            k_ref[z, rows, cols] = k
            buf[rows, cols] = k

    def weights(z):
        own = wo_ref[:, z, :, :].reshape(64, 256)
        return jnp.concatenate([own, wx_ref[:, z, :, :].reshape(64, 256)], axis=1)

    def fit(w, buf, i):
        rows = pl.ds(i * step, step)
        fit_ref[rows, :] += lax.dot_general(buf[rows, :], w, LAST, preferred_element_type=f32)

    load(0, 0)
    load(1, 1)
    for i in range(parts):
        fill(0, 0, even_ref, i)

    def pair(h, carry):
        z = 2 * h + 1
        w = weights(z - 1)
        for i in range(parts):
            fit(w, even_ref, i)
            fill(z, 1, odd_ref, i)
        load(z + 1, 0)
        w = weights(z)
        for i in range(parts):
            fit(w, odd_ref, i)
            fill(z + 1, 0, even_ref, i)
        load(z + 2, 1)
        return carry

    lax.fori_loop(0, nz // 2 - 1, pair, 0)
    w = weights(nz - 2)
    for i in range(parts):
        fit(w, even_ref, i)
        fill(nz - 1, 1, odd_ref, i)
    w = weights(nz - 1)
    for i in range(parts):
        fit(w, odd_ref, i)
    fitted = fit_ref[...].T.astype(bf16)

    def second(z, carry):
        for h, ref in ((0, own_ref), (1, oth_ref)):
            n = jnp.dot(fitted, k_ref[z, :, h * 256 : h * 256 + 256], preferred_element_type=f32)
            ref[:, z, :, :] = n.reshape(4, 16, 256).astype(ref.dtype)
        return carry

    lax.fori_loop(0, nz, second, 0, unroll=2)


def add_body(a_ref, b_ref, out_ref):
    out_ref[...] = (a_ref[...] + b_ref[...].astype(f32)).astype(out_ref.dtype)


def sum_blocks(ref):
    parts = [ref[r].astype(f32) for r in range(ref.shape[0])]
    while len(parts) > 1:
        parts = [a + b for a, b in zip(parts[::2], parts[1::2])]
    return parts[0]


def total_body(x_ref, out_ref):
    out_ref[...] = sum_blocks(x_ref)


def back_outer_body(at_ref, x_ref, y_ref, f_ref, own_ref, oth_ref):
    half = (x_ref[...] + y_ref[...]).astype(bf16)
    for which, ref in ((0, own_ref), (1, oth_ref)):
        for z in range(ref.shape[0]):
            ref[z] = jnp.dot(half, f_ref[:, columns(at_ref, z, which)], preferred_element_type=f32)


def back_inner_body(count, at_ref, x_ref, f_ref, term_ref, full_ref, res_ref, own_ref, oth_ref):
    shaped = sum_blocks(x_ref) / count + ridge_weight * term_ref[...]
    half = shaped.astype(bf16)
    curve = jnp.sum(half.astype(f32) * full_ref[...], axis=1, keepdims=True)
    res = own_rows(at_ref, res_ref)
    old = jnp.sum(res * res, axis=1, keepdims=True)
    extra = lanes4(curve, old)
    for which, ref in ((0, own_ref), (1, oth_ref)):
        for z in range(ref.shape[0]):
            ref[z, :, :512] = fold(
                jnp.dot(half, f_ref[:, columns(at_ref, z, which)], preferred_element_type=f32)
            )
            ref[z, :, 512:] = extra


def lanes4(a, b):
    lane = lax.broadcasted_iota(jnp.int32, (1, 128), 1)
    out = jnp.where(lane == 2, b[:8], b[8:])
    out = jnp.where(lane == 1, a[8:], out)
    return jnp.where(lane == 0, a[:8], out)


def pair(tile, at):
    return jnp.concatenate([tile[:, at : at + 1], tile[:, at + 1 : at + 2]], axis=0)


def step_body(at_ref, x_ref, res_ref, keep_ref, out_ref):
    block = sum_blocks(x_ref)
    image, extra = unfold(block), block[:, 512:]
    curve, old = pair(extra, 0), pair(extra, 2)
    alpha = old / curve
    new = own_rows(at_ref, res_ref) - alpha * image
    keep_ref[:, :512] = fold(new)
    keep_ref[:, 512:] = lanes4(alpha, old)
    part = jnp.sum(new * new, axis=1, keepdims=True)
    spread(lanes4(part, part), out_ref)


def beta_body(x_ref, keep_ref, out_ref):
    total = pair(sum_blocks(x_ref), 0)
    extra = keep_ref[:, 512:]
    alpha, old = pair(extra, 0), pair(extra, 2)
    extra = lanes4(alpha, total / old)
    for r in range(out_ref.shape[0]):
        out_ref[r, :, :512] = keep_ref[:, :512]
        out_ref[r, :, 512:] = extra


def final_body(x_ref, it_ref, d_ref, ni_ref, nr_ref, nd_ref):
    for g in range(x_ref.shape[0]):
        rows = slice(g * 16, g * 16 + 16)
        block = x_ref[g]
        new, extra = unfold(block), block[:, 512:]
        d = d_ref[rows, :]
        ni_ref[rows, :] = it_ref[rows, :] + pair(extra, 0) * d
        nr_ref[rows, :] = new
        nd_ref[rows, :] = new + pair(extra, 2) * d


def local(points, centers, inner_factor, outer_factor, iterate, residual, direction):
    at = jnp.stack([lax.axis_index("y"), lax.axis_index("c")])
    count = float(points.shape[0] * 256)

    def swap(v):
        return lax.ppermute(v, "c", SWAP)

    x = call(prep_body, sds((16, 32, 256), bf16), (at, direction), [SM, VM], name="prep")
    x = exchange(x, LINE)
    term, full, x = call(
        inner_body,
        (sds((16, 256), f32), sds((16, 256), f32), sds((16, 16, 256), bf16)),
        (at, x, swap(x), inner_factor),
        [SM] + [VM] * 3,
        name="inner",
    )
    x = exchange(x, LINE)
    x = call(
        outer_body,
        sds((64, 16, 256), bf16),
        (at, x, swap(x), outer_factor),
        [SM] + [VM] * 3,
        name="outer",
    )
    x = exchange(x, CHIPS).reshape(4, 16, 16, 256)
    own, other = call(
        kernel_body,
        (sds((4, 16, 16, 256), f32), sds((4, 16, 16, 256), f32)),
        (at, points, centers, x, swap(x)),
        [SM] + [VM] * 4,
        scratch=[
            pltpu.VMEM((16, points.shape[0], 512), bf16),
            pltpu.VMEM((points.shape[0], 256), bf16),
            pltpu.VMEM((2, 512, 256), bf16),
            pltpu.VMEM((points.shape[0], 64), f32),
            pltpu.VMEM((points.shape[0], 512), bf16),
            pltpu.VMEM((points.shape[0], 512), bf16),
        ],
        vmem=48,
        name="kernel",
    )
    x = call(add_body, sds((4, 16, 16, 256), bf16), (own, swap(other)), name="add")
    x = exchange(x.reshape(64, 16, 256), CHIPS)
    x = call(total_body, sds((16, 256), f32), (x,), name="total")
    own, other = call(
        back_outer_body,
        (sds((16, 16, 256), f32), sds((16, 16, 256), f32)),
        (at, x, lax.ppermute(x, "zh", SWAP), outer_factor),
        [SM] + [VM] * 3,
        name="back_outer",
    )
    x = call(add_body, sds((16, 16, 256), f32), (own, swap(other)), name="add")
    x = exchange(x, LINE)
    own, other = call(
        functools.partial(back_inner_body, count),
        (sds((16, 8, 640), f32), sds((16, 8, 640), f32)),
        (at, x, inner_factor, term, full, residual),
        [SM] + [VM] * 5,
        name="back_inner",
    )
    x = call(add_body, sds((16, 8, 640), f32), (own, swap(other)), name="add")
    x = exchange(x, LINE)
    keep, x = call(
        step_body,
        (sds((8, 640), f32), sds((32, 8, 128), f32)),
        (at, x, residual),
        [SM, VM, VM],
        name="step",
    )
    x = exchange(x, ROW)
    x = call(beta_body, sds((4, 8, 640), f32), (x, keep), name="beta")
    x = exchange(x, ("y",))
    out = sds((64, 256), f32)
    return call(final_body, (out, out, out), (x, iterate, direction), name="final")


def solution(mesh):
    fine = Mesh(mesh.devices.reshape(2, 4, 4, 4, 2), ("zh", "y", "zl", "x", "c"))
    placed = (
        P(ALL, None),
        P(),
        P(ROW, None),
        P(ROW, None),
        P(None, ROW),
        P(None, ROW),
        P(None, ROW),
    )
    return jax.shard_map(
        local,
        mesh=fine,
        in_specs=placed,
        out_specs=(P(None, ROW),) * 3,
        check_vma=False,
    )
```

time: 191 us -> 190 us (level)
  blocking collectives: 148 us -> 123 us
  starting transfers between devices: 2.8 us -> 15.4 us
  waiting for transfers between devices: 3.96 us -> 10.7 us
  Pallas kernels: 32.6 us -> 35.8 us
    all_to_all x8, blocking collectives: 148 us -> 123 us  [exchange(): return lax.all_to_all(v, axes, 0, 0, tiled=True)]
    ppermute x2 -> x7, starting transfers between devices: 2.8 us -> 15.4 us  [the longest x6 11.1 us: swap(): return lax.ppermute(v, 'c', SWAP)]
    ppermute x2 -> x7, waiting for transfers between devices: 3.96 us -> 10.7 us  [the longest x6 8.39 us: swap(): return lax.ppermute(v, 'c', SWAP)]
    pallas_call x10 -> x13, Pallas kernels: 32.6 us -> 35.8 us  [call(): pl.pallas_call(body, out_shape=outs, in_specs=specs or [VM] * len(args),...]
  transfers between devices with their start and end apart: 2 -> 7, of which waited for: 2 -> 7; matrix products, arithmetic and copies ran while one was open for 0% -> 0% of each run, Pallas kernels for 0% -> 0%
where the time goes in v3:
time: 190 us; the launch traced here: 189 us
  blocking collectives  123 us (65%)
  Pallas kernels  35.8 us (19%)
  starting transfers between devices  15.4 us (8%)
  waiting for transfers between devices  10.7 us (6%)
  local copies, waits for them, and re-layouts  3.21 us (2%)
    all_to_all x8, blocking collectives, exchange(): return lax.all_to_all(v, axes, 0, 0, tiled=True)  123 us
    pallas_call x13, Pallas kernels, call(): pl.pallas_call(body, out_shape=outs, in_specs=specs or [VM] * len(args),...  35.8 us
    ppermute x6, starting transfers between devices, swap(): return lax.ppermute(v, 'c', SWAP)  11.1 us
    ppermute x6, waiting for transfers between devices, swap(): return lax.ppermute(v, 'c', SWAP)  8.39 us
    ppermute x1, starting transfers between devices, local(): lax.ppermute(x, 'zh', SWAP)  4.31 us
  transfers between devices with their start and end apart: 7, of which 7 were waited for; matrix products, arithmetic and copies ran while one was open for 0% of the time, Pallas kernels for 0%

profile of v3, /device:TPU:1, one launch (start us, length us, event | category | flops | bytes accessed | tf_op | source)
XLA Modules:
  0.0 189.1 jit_solution(11061530323312588642)
XLA Ops:
  2.3 18.4 %all_to_all.40.x_ref = bf16[16,32,256]{2,1,0:T(8,128)(2,1)S(1)} all-to-all(bf16[16,32,256]{2,1,0:T(8,128)(2,1)S(1)} %prep.1), channel_id=1, replica_groups=mesh['zh'=2,'y'=4,'zl'=4,'x'=4,'c'=2] {'zl','x'}, dimensions={0} | all-to-all | bytes 524288 | tf_op jit(solution)/shard_map/all_to_all | solution.py:40
  20.7 2.1 %collective-permute-start = (bf16[16,32,256]{2,1,0:T(8,128)(2,1)S(1)}, bf16[16,32,256]{2,1,0:T(8,128)(2,1)S(1)}, u32[]{:S(2)}, u32[]{:S(2)}) collective-permute-start(bf16[16,32,256]{2,1,0:T(8,128)(2,1)S(1)} %all_to_all.40.x_ref), channel_id=1, source_target_pairs={{0,1},{1,0},{2,3},{3,2},{4,5},{5,4},{6,7},{7,6},{8,9},{9,8},{10,11... | collective-permute-start | bytes 786440 | tf_op jit(solution)/shard_map/ppermute | solution.py:273
  23.9 2.2 %copy-done.1 = bf16[256,8192]{1,0:T(8,128)(2,1)S(1)} copy-done((bf16[256,8192]{1,0:T(8,128)(2,1)S(1)}, bf16[256,8192]{1,0:T(8,128)(2,1)}, u32[]{:S(2)}) %copy-start.1) | copy-done | bytes 4194328
  26.1 1.9 inner.1
  28.0 11.2 %all_to_all.41.x_ref = bf16[16,16,256]{2,1,0:T(8,128)(2,1)S(1)} all-to-all(bf16[16,16,256]{2,1,0:T(8,128)(2,1)S(1)} %get-tuple-element.14), channel_id=1, replica_groups=mesh['zh'=2,'y'=4,'zl'=4,'x'=4,'c'=2] {'zl','x'}, dimensions={0} | all-to-all | bytes 262144 | tf_op jit(solution)/shard_map/all_to_all | solution.py:40
  39.2 1.8 collective-permute-start.1
  42.0 1.8 outer.1
  43.8 23.5 %all_to_all.42 = bf16[64,16,256]{2,1,0:T(8,128)(2,1)S(1)} all-to-all(bf16[64,16,256]{2,1,0:T(8,128)(2,1)S(1)} %outer.1), channel_id=1, replica_groups=mesh['zh'=2,'y'=4,'zl'=4,'x'=4,'c'=2] {'y','zl','x'}, dimensions={0} | all-to-all | bytes 1048576 | tf_op jit(solution)/shard_map/all_to_all | solution.py:40
  67.3 1.9 %collective-permute-start.2 = (bf16[4,16,16,256]{3,2,1,0:T(8,128)(2,1)S(1)}, bf16[4,16,16,256]{3,2,1,0:T(8,128)(2,1)S(1)}, u32[]{:S(2)}, u32[]{:S(2)}) collective-permute-start(bf16[4,16,16,256]{3,2,1,0:T(8,128)(2,1)S(1)} %bitcast.5), channel_id=1, source_target_pairs={{0,1},{1,0},{2,3},{3,2},{4,5},{5,4},{6,7},{7,6},{8,9},{9,8},{10,11... | collective-permute-start | bytes 1572872 | tf_op jit(solution)/shard_map/ppermute | solution.py:273
  69.2 1.5 collective-permute-done.2.wx_ref
  70.7 27.1 %kernel.1 = (f32[4,16,16,256]{3,2,1,0:T(8,128)S(1)}, f32[4,16,16,256]{3,2,1,0:T(8,128)S(1)}) custom-call(s32[2]{0:T(128)S(1)} %pad_add_fusion.at_ref, bf16[2048,128]{1,0:T(8,128)(2,1)S(1)} %copy-done.4, bf16[8192,128]{1,0:T(8,128)(2,1)S(1)} %copy-done.3, bf16[4,16,16,256]{3,2,1,0:T(8,128)(2,1)S(1)} %bitcast.6, ...), custom_call_target="tpu_custom_call" | custom-call | tf_op jit(solution)/shard_map/kernel/pallas_call | solution.py:24
  98.3 2.3 %collective-permute-done.3.b_ref = f32[4,16,16,256]{3,2,1,0:T(8,128)S(1)} collective-permute-done((f32[4,16,16,256]{3,2,1,0:T(8,128)S(1)}, f32[4,16,16,256]{3,2,1,0:T(8,128)S(1)}, u32[]{:S(2)}, u32[]{:S(2)}) %collective-permute-start.3) | collective-permute-done | bytes 1048608 | tf_op jit(solution)/shard_map/ppermute | solution.py:273
  100.7 22.0 %all_to_all.43.x_ref = bf16[64,16,256]{2,1,0:T(8,128)(2,1)S(1)} all-to-all(bf16[64,16,256]{2,1,0:T(8,128)(2,1)S(1)} %bitcast.4), channel_id=1, replica_groups=mesh['zh'=2,'y'=4,'zl'=4,'x'=4,'c'=2] {'y','zl','x'}, dimensions={0} | all-to-all | bytes 1048576 | tf_op jit(solution)/shard_map/all_to_all | solution.py:40
  122.8 4.3 %collective-permute-start.4 = (f32[16,256]{1,0:T(8,128)S(1)}, f32[16,256]{1,0:T(8,128)S(1)}, u32[]{:S(2)}, u32[]{:S(2)}) collective-permute-start(f32[16,256]{1,0:T(8,128)S(1)} %total.1.x_ref), channel_id=1, source_target_pairs={{0,128},{128,0},{1,129},{129,1},{2,130},{130,2},{3,131},{131,3},{4... | collective-permute-start | bytes 49160 | tf_op jit(solution)/shard_map/ppermute | solution.py:315
  127.1 2.3 %collective-permute-done.4.y_ref = f32[16,256]{1,0:T(8,128)S(1)} collective-permute-done((f32[16,256]{1,0:T(8,128)S(1)}, f32[16,256]{1,0:T(8,128)S(1)}, u32[]{:S(2)}, u32[]{:S(2)}) %collective-permute-start.4) | collective-permute-done | bytes 16416 | tf_op jit(solution)/shard_map/ppermute | solution.py:315
  129.3 1.2 back_outer.1
  130.5 3.3 %collective-permute-start.5 = (f32[16,16,256]{2,1,0:T(8,128)S(1)}, f32[16,16,256]{2,1,0:T(8,128)S(1)}, u32[]{:S(2)}, u32[]{:S(2)}) collective-permute-start(f32[16,16,256]{2,1,0:T(8,128)S(1)} %get-tuple-element.18), channel_id=1, source_target_pairs={{0,1},{1,0},{2,3},{3,2},{4,5},{5,4},{6,7},{7,6},{8,9},{9,8},{10,11... | collective-permute-start | bytes 786440 | tf_op jit(solution)/shard_map/ppermute | solution.py:273
  135.0 12.8 %all_to_all.44.x_ref = f32[16,16,256]{2,1,0:T(8,128)S(1)} all-to-all(f32[16,16,256]{2,1,0:T(8,128)S(1)} %add.6), channel_id=1, replica_groups=mesh['zh'=2,'y'=4,'zl'=4,'x'=4,'c'=2] {'zl','x'}, dimensions={0} | all-to-all | bytes 524288 | tf_op jit(solution)/shard_map/all_to_all | solution.py:40
  147.8 1.2 back_inner.1
  149.0 1.6 collective-permute-start.6
  150.6 1.3 collective-permute-done.6.b_ref
  151.9 14.2 %all_to_all.45.x_ref = f32[16,8,640]{2,1,0:T(8,128)S(1)} all-to-all(f32[16,8,640]{2,1,0:T(8,128)S(1)} %add.7), channel_id=1, replica_groups=mesh['zh'=2,'y'=4,'zl'=4,'x'=4,'c'=2] {'zl','x'}, dimensions={0} | all-to-all | bytes 655360 | tf_op jit(solution)/shard_map/all_to_all | solution.py:40
  167.0 14.2 %all_to_all.46.x_ref = f32[32,8,128]{2,1,0:T(8,128)S(1)} all-to-all(f32[32,8,128]{2,1,0:T(8,128)S(1)} %get-tuple-element.23), channel_id=1, replica_groups=mesh['zh'=2,'y'=4,'zl'=4,'x'=4,'c'=2] {'zl','x','c'}, dimensions={0} | all-to-all | bytes 262144 | tf_op jit(solution)/shard_map/all_to_all | solution.py:40
  181.3 6.9 %all_to_all.47.x_ref = f32[4,8,640]{2,1,0:T(8,128)S(1)} all-to-all(f32[4,8,640]{2,1,0:T(8,128)S(1)} %beta.1), channel_id=1, replica_groups=mesh['zh'=2,'y'=4,'zl'=4,'x'=4,'c'=2] {'y'}, dimensions={0} | all-to-all | bytes 163840 | tf_op jit(solution)/shard_map/all_to_all | solution.py:40
  (30 shorter events, 7.5 us)
Async XLA Ops:
  0.6 41.3 %copy-start = (bf16[256,8192]{1,0:T(8,128)(2,1)S(1)}, bf16[256,8192]{1,0:T(8,128)(2,1)}, u32[]{:S(2)}) copy-start(bf16[256,8192]{1,0:T(8,128)(2,1)} %f_ref.6) | copy-start | bytes 12582916
  0.7 1.0 copy-start.6
  20.7 3.2 %collective-permute-start = (bf16[16,32,256]{2,1,0:T(8,128)(2,1)S(1)}, bf16[16,32,256]{2,1,0:T(8,128)(2,1)S(1)}, u32[]{:S(2)}, u32[]{:S(2)}) collective-permute-start(bf16[16,32,256]{2,1,0:T(8,128)(2,1)S(1)} %all_to_all.40.x_ref), channel_id=1, source_target_pairs={{0,1},{1,0},{2,3},{3,2},{4,5},{5,4},{6,7},{7,6},{8,9},{9,8},{10,11... | collective-permute-start | bytes 786440 | tf_op jit(solution)/shard_map/ppermute | solution.py:273
  23.9 2.2 %copy-start.1 = (bf16[256,8192]{1,0:T(8,128)(2,1)S(1)}, bf16[256,8192]{1,0:T(8,128)(2,1)}, u32[]{:S(2)}) copy-start(bf16[256,8192]{1,0:T(8,128)(2,1)} %f_ref.7) | copy-start | bytes 12582916
  28.0 42.7 %copy-start.3 = (bf16[8192,128]{1,0:T(8,128)(2,1)S(1)}, bf16[8192,128]{1,0:T(8,128)(2,1)}, u32[]{:S(2)}) copy-start(bf16[8192,128]{1,0:T(8,128)(2,1)} %cen_ref.1) | copy-start | bytes 6291460
  28.0 42.7 %copy-start.4 = (bf16[2048,128]{1,0:T(8,128)(2,1)S(1)}, bf16[2048,128]{1,0:T(8,128)(2,1)}, u32[]{:S(2)}) copy-start(bf16[2048,128]{1,0:T(8,128)(2,1)} %p_ref.1) | copy-start | bytes 1572868
  39.2 2.8 %collective-permute-start.1 = (bf16[16,16,256]{2,1,0:T(8,128)(2,1)S(1)}, bf16[16,16,256]{2,1,0:T(8,128)(2,1)S(1)}, u32[]{:S(2)}, u32[]{:S(2)}) collective-permute-start(bf16[16,16,256]{2,1,0:T(8,128)(2,1)S(1)} %all_to_all.41.x_ref), channel_id=1, source_target_pairs={{0,1},{1,0},{2,3},{3,2},{4,5},{5,4},{6,7},{7,6},{8,9},{9,8},{10,11... | collective-permute-start | bytes 393224 | tf_op jit(solution)/shard_map/ppermute | solution.py:273
  67.3 3.4 %collective-permute-start.2 = (bf16[4,16,16,256]{3,2,1,0:T(8,128)(2,1)S(1)}, bf16[4,16,16,256]{3,2,1,0:T(8,128)(2,1)S(1)}, u32[]{:S(2)}, u32[]{:S(2)}) collective-permute-start(bf16[4,16,16,256]{3,2,1,0:T(8,128)(2,1)S(1)} %bitcast.5), channel_id=1, source_target_pairs={{0,1},{1,0},{2,3},{3,2},{4,5},{5,4},{6,7},{7,6},{8,9},{9,8},{10,11... | collective-permute-start | bytes 1572872 | tf_op jit(solution)/shard_map/ppermute | solution.py:273
  97.8 2.8 %collective-permute-start.3 = (f32[4,16,16,256]{3,2,1,0:T(8,128)S(1)}, f32[4,16,16,256]{3,2,1,0:T(8,128)S(1)}, u32[]{:S(2)}, u32[]{:S(2)}) collective-permute-start(f32[4,16,16,256]{3,2,1,0:T(8,128)S(1)} %get-tuple-element.16), channel_id=1, source_target_pairs={{0,1},{1,0},{2,3},{3,2},{4,5},{5,4},{6,7},{7,6},{8,9},{9,8},{10,11... | collective-permute-start | bytes 3145736 | tf_op jit(solution)/shard_map/ppermute | solution.py:273
  100.7 47.1 %copy-start.2 = (bf16[256,8192]{1,0:T(8,128)(2,1)S(1)}, bf16[256,8192]{1,0:T(8,128)(2,1)}, u32[]{:S(2)}) copy-start(bf16[256,8192]{1,0:T(8,128)(2,1)} %f_ref.7) | copy-start | bytes 12582916
  100.7 47.1 %copy-start.5 = (f32[64,256]{1,0:T(8,128)S(1)}, f32[64,256]{1,0:T(8,128)}, u32[]{:S(2)}) copy-start(f32[64,256]{1,0:T(8,128)} %res_ref.3) | copy-start | bytes 196612
  122.8 6.6 %collective-permute-start.4 = (f32[16,256]{1,0:T(8,128)S(1)}, f32[16,256]{1,0:T(8,128)S(1)}, u32[]{:S(2)}, u32[]{:S(2)}) collective-permute-start(f32[16,256]{1,0:T(8,128)S(1)} %total.1.x_ref), channel_id=1, source_target_pairs={{0,128},{128,0},{1,129},{129,1},{2,130},{130,2},{3,131},{131,3},{4... | collective-permute-start | bytes 49160 | tf_op jit(solution)/shard_map/ppermute | solution.py:315
  130.5 4.4 %collective-permute-start.5 = (f32[16,16,256]{2,1,0:T(8,128)S(1)}, f32[16,16,256]{2,1,0:T(8,128)S(1)}, u32[]{:S(2)}, u32[]{:S(2)}) collective-permute-start(f32[16,16,256]{2,1,0:T(8,128)S(1)} %get-tuple-element.18), channel_id=1, source_target_pairs={{0,1},{1,0},{2,3},{3,2},{4,5},{5,4},{6,7},{7,6},{8,9},{9,8},{10,11... | collective-permute-start | bytes 786440 | tf_op jit(solution)/shard_map/ppermute | solution.py:273
  135.0 53.3 %copy-start.7 = (f32[64,256]{1,0:T(8,128)S(1)}, f32[64,256]{1,0:T(8,128)}, u32[]{:S(2)}) copy-start(f32[64,256]{1,0:T(8,128)} %d_ref.3) | copy-start | bytes 196612
  135.0 53.3 %copy-start.8 = (f32[64,256]{1,0:T(8,128)S(1)}, f32[64,256]{1,0:T(8,128)}, u32[]{:S(2)}) copy-start(f32[64,256]{1,0:T(8,128)} %it_ref.1) | copy-start | bytes 196612
  149.0 2.9 %collective-permute-start.6 = (f32[16,8,640]{2,1,0:T(8,128)S(1)}, f32[16,8,640]{2,1,0:T(8,128)S(1)}, u32[]{:S(2)}, u32[]{:S(2)}) collective-permute-start(f32[16,8,640]{2,1,0:T(8,128)S(1)} %get-tuple-element.22), channel_id=1, source_target_pairs={{0,1},{1,0},{2,3},{3,2},{4,5},{5,4},{6,7},{7,6},{8,9},{9,8},{10,11... | collective-permute-start | bytes 983048 | tf_op jit(solution)/shard_map/ppermute | solution.py:273

commit v4 on v3

v4 whole, which is shorter than its diff:
```python
import functools
import jax
import jax.numpy as jnp
from jax import lax
from jax.sharding import Mesh, PartitionSpec as P
from jax.experimental import pallas as pl
from jax.experimental.pallas import tpu as pltpu

ridge_weight = 0.5
bf16, f32 = jnp.bfloat16, jnp.float32
ROW = ("zl", "x", "c")
LINE = ("zl", "x")
SIDE = ("y", "zl")
FACE = ("zh", "y", "zl")
HALVES = ("zh", "zl", "x", "c")
ALL = ("zh", "y") + ROW
SWAP = [(0, 1), (1, 0)]
LOG2E = 1.4426950408889634
MIB = 1024 * 1024
FILL = 4_000_000_000
LAST = (((1,), (1,)), ((), ()))
VM = pl.BlockSpec(memory_space=pltpu.VMEM)
SM = pl.BlockSpec(memory_space=pltpu.SMEM)


def call(body, outs, args, specs=None, scratch=(), vmem=10, name=None, flops=0):
    return pl.pallas_call(
        body,
        out_shape=outs,
        in_specs=specs or [VM] * len(args),
        out_specs=jax.tree.map(lambda _: VM, outs),
        scratch_shapes=scratch,
        compiler_params=pltpu.CompilerParams(vmem_limit_bytes=vmem * MIB),
        cost_estimate=pl.CostEstimate(flops=flops, bytes_accessed=0, transcendentals=0),
        name=name,
    )(*args)


def sds(shape, dtype):
    return jax.ShapeDtypeStruct(shape, dtype)


def exchange(v, axes):
    return lax.all_to_all(v, axes, 0, 0, tiled=True)


def own_rows(at_ref, ref):
    return ref[pl.ds(pl.multiple_of(at_ref[0] * 16, 16), 16), :]


def eight_rows(at_ref, ref):
    start = at_ref[0] * 16 + at_ref[3] * 8
    return ref[pl.ds(pl.multiple_of(start, 8), 8), :]


def columns(at_ref, z, which):
    c = at_ref[1]
    return pl.ds(pl.multiple_of((2 * z + (c if which == 0 else 1 - c)) * 256, 256), 256)


def spread(value, ref):
    for r in range(ref.shape[0]):
        ref[r] = value


def prep_body(at_ref, d_ref, out_ref):
    d = own_rows(at_ref, d_ref)
    hi = d.astype(bf16)
    lo = (d - hi.astype(f32)).astype(bf16)
    spread(jnp.concatenate([hi, lo], axis=0), out_ref)


def rows_dot(at_ref, x_ref, y_ref, f_ref):
    acc = None
    for which, ref in ((0, x_ref), (1, y_ref)):
        for z in range(ref.shape[0]):
            part = lax.dot_general(
                ref[z], f_ref[:, columns(at_ref, z, which)], LAST, preferred_element_type=f32
            )
            acc = part if acc is None else acc + part
    return acc


def inner_body(at_ref, x_ref, y_ref, f_ref, term_ref, full_ref, out_ref):
    acc = rows_dot(at_ref, x_ref, y_ref, f_ref)
    term_ref[...] = acc[:16]
    full_ref[...] = acc[:16] + acc[16:]
    spread(acc[:16].astype(bf16), out_ref)


def outer_body(at_ref, x_ref, y_ref, f_ref, out_ref):
    spread(rows_dot(at_ref, x_ref, y_ref, f_ref).astype(bf16), out_ref)


def norm_lanes(rows, first):
    wide = rows.astype(f32)
    lane = lax.broadcasted_iota(jnp.int32, (1, 128), 1)
    norm = jnp.sum(wide * wide, axis=1, keepdims=True) * -0.5
    one = norm.astype(bf16).astype(f32)
    rest = norm - one
    two = rest.astype(bf16).astype(f32)
    three = rest - two
    a, b = (0, 3) if first else (3, 0)
    ones = jnp.where((lane >= b) & (lane < b + 3), 1.0, 0.0)
    out = jnp.where(lane == a + 2, three, ones)
    out = jnp.where(lane == a + 1, two, out)
    return jnp.where(lane == a, one, out).astype(bf16)


def fill(at_ref, shift, i, pa_ref, cen_ref, ca_ref, k_ref, fit=None):
    z = i * 4 + (at_ref[2] + shift) % 4
    step = 256
    for h in range(2):
        cols = slice(h * 256, h * 256 + 256)
        block = cen_ref[columns(at_ref, z, h), :]
        ca_ref[cols, :128] = block
        ca_ref[cols, 128:] = norm_lanes(block, False)
    for r in range(pa_ref.shape[0] // step):
        rows = pl.ds(r * step, step)
        if fit is not None:
            fit(i, rows)
        for h in range(2):
            cols = slice(h * 256, h * 256 + 256)
            d = lax.dot_general(pa_ref[rows, :], ca_ref[cols, :], LAST, preferred_element_type=f32)
            k_ref[i, rows, cols] = jnp.exp2(d * (LOG2E * 8.0 / 128.0)).astype(bf16)


def fill_body(at_ref, p_ref, cen_ref, pa_ref, k_ref, ca_ref):
    pa_ref[:, :128] = p_ref[...]
    for r in range(p_ref.shape[0] // 256):
        rows = pl.ds(r * 256, 256)
        pa_ref[rows, 128:] = norm_lanes(p_ref[rows, :], True)

    def chunk(i, carry):
        fill(at_ref, 0, i, pa_ref, cen_ref, ca_ref, k_ref)
        return carry

    lax.fori_loop(0, k_ref.shape[0], chunk, 0)


def fitter(v_ref, u_ref, k_ref, sum_ref):
    def fit(i, rows):
        w = jnp.concatenate(
            [v_ref[:, i, :, :].reshape(64, 256), u_ref[:, i, :, :].reshape(64, 256)], axis=1
        )
        sum_ref[rows, :] += lax.dot_general(
            k_ref[i, rows, :], w, LAST, preferred_element_type=f32
        )

    return fit


def both_body(shift, at_ref, pa_ref, cen_ref, v_ref, u_ref, k_ref, old_ref, next_ref, sum_ref, ca_ref):
    sum_ref[...] = old_ref[...]
    fit = fitter(v_ref, u_ref, k_ref, sum_ref)

    def chunk(i, carry):
        fill(at_ref, shift + 1, i, pa_ref, cen_ref, ca_ref, next_ref, fit)
        return carry

    lax.fori_loop(0, k_ref.shape[0], chunk, 0)


def both_first_body(at_ref, pa_ref, cen_ref, v_ref, u_ref, k_ref, next_ref, sum_ref, ca_ref):
    sum_ref[...] = jnp.zeros_like(sum_ref)
    fit = fitter(v_ref, u_ref, k_ref, sum_ref)

    def chunk(i, carry):
        fill(at_ref, 1, i, pa_ref, cen_ref, ca_ref, next_ref, fit)
        return carry

    lax.fori_loop(0, k_ref.shape[0], chunk, 0)


def fit_body(v_ref, u_ref, k_ref, old_ref, out_ref, sum_ref):
    sum_ref[...] = old_ref[...]
    fit = fitter(v_ref, u_ref, k_ref, sum_ref)

    def chunk(i, carry):
        for r in range(8):
            fit(i, pl.ds(r * 256, 256))
        return carry

    lax.fori_loop(0, k_ref.shape[0], chunk, 0)
    out_ref[...] = sum_ref[...].T.astype(bf16)


def normal_body(fit_ref, k_ref, own_ref, oth_ref):
    fitted = fit_ref[...]

    def chunk(i, carry):
        for h, ref in ((0, own_ref), (1, oth_ref)):
            n = jnp.dot(fitted, k_ref[i, :, h * 256 : h * 256 + 256], preferred_element_type=f32)
            n = n.reshape(4, 2, 8, 256)
            ref[0, :, i, :, :] = n[:, 0]
            ref[1, :, i, :, :] = n[:, 1]
        return carry

    lax.fori_loop(0, k_ref.shape[0], chunk, 0, unroll=2)


def add_body(a_ref, b_ref, out_ref):
    out_ref[...] = (a_ref[...] + b_ref[...].astype(f32)).astype(out_ref.dtype)


def sum_blocks(ref):
    parts = [ref[r].astype(f32) for r in range(ref.shape[0])]
    while len(parts) > 1:
        parts = [a + b for a, b in zip(parts[::2], parts[1::2])]
    return parts[0]


def gather_body(a_ref, b_ref, c_ref, d_ref, e_ref, out_ref):
    out_ref[...] = (
        (a_ref[...] + b_ref[...])
        + (c_ref[...].astype(f32) + d_ref[...].astype(f32))
        + e_ref[...].astype(f32)
    )


def back_outer_body(at_ref, x_ref, f_ref, own_ref, oth_ref):
    half = sum_blocks(x_ref).astype(bf16)
    for which, ref in ((0, own_ref), (1, oth_ref)):
        for z in range(ref.shape[0]):
            ref[z] = jnp.dot(half, f_ref[:, columns(at_ref, z, which)], preferred_element_type=f32)


def back_inner_body(count, at_ref, x_ref, f_ref, term_ref, full_ref, res_ref, own_ref, oth_ref):
    mine = pl.ds(pl.multiple_of(at_ref[3] * 8, 8), 8)
    shaped = sum_blocks(x_ref) / count + ridge_weight * term_ref[mine, :]
    half = shaped.astype(bf16)
    curve = jnp.sum(half.astype(f32) * full_ref[mine, :], axis=1, keepdims=True)
    res = eight_rows(at_ref, res_ref)
    old = jnp.sum(res * res, axis=1, keepdims=True)
    lane = lax.broadcasted_iota(jnp.int32, (8, 128), 1)
    extra = jnp.where(lane == 0, curve, old)
    for which, ref in ((0, own_ref), (1, oth_ref)):
        for z in range(ref.shape[0]):
            ref[z, :, :256] = jnp.dot(
                half, f_ref[:, columns(at_ref, z, which)], preferred_element_type=f32
            )
            ref[z, :, 256:] = extra


def diagonal():
    lane = lax.broadcasted_iota(jnp.int32, (8, 128), 1)
    return lane == lax.broadcasted_iota(jnp.int32, (8, 128), 0)


def step_body(at_ref, x_ref, res_ref, keep_ref, out_ref):
    block = sum_blocks(x_ref)
    curve, old = block[:, 256:257], block[:, 257:258]
    alpha = old / curve
    new = eight_rows(at_ref, res_ref) - alpha * block[:, :256]
    lane = lax.broadcasted_iota(jnp.int32, (8, 128), 1)
    keep_ref[:, :256] = new
    keep_ref[:, 256:] = jnp.where(lane == 0, alpha, old)
    part = jnp.sum(new * new, axis=1, keepdims=True)
    row = jnp.sum(jnp.where(diagonal(), part, 0.0), axis=0, keepdims=True)
    out_ref[...] = jnp.broadcast_to(row, out_ref.shape)


def beta_body(at_ref, x_ref, keep_ref, far_ref, out_ref):
    lane = lax.broadcasted_iota(jnp.int32, (8, 128), 1)
    half = x_ref.shape[0] // 2
    for which, ref in ((0, keep_ref), (1, far_ref)):
        zh = at_ref[3] if which == 0 else 1 - at_ref[3]
        rows = x_ref[pl.ds(pl.multiple_of(zh * half, half), half), :]
        row = jnp.sum(rows, axis=0, keepdims=True)
        total = jnp.sum(jnp.where(diagonal(), row, 0.0), axis=1, keepdims=True)
        extra = ref[:, 256:]
        extra = jnp.where(lane == 0, extra, total / extra[:, 1:2])
        for r in range(out_ref.shape[0]):
            out_ref[r, zh, :, :256] = ref[:, :256]
            out_ref[r, zh, :, 256:] = extra


def final_body(x_ref, it_ref, d_ref, ni_ref, nr_ref, nd_ref):
    for g in range(x_ref.shape[0]):
        for h in range(2):
            rows = slice(g * 16 + h * 8, g * 16 + h * 8 + 8)
            new = x_ref[g, h, :, :256]
            d = d_ref[rows, :]
            ni_ref[rows, :] = it_ref[rows, :] + x_ref[g, h, :, 256:257] * d
            nr_ref[rows, :] = new
            nd_ref[rows, :] = new + x_ref[g, h, :, 257:258] * d


def local(points, centers, inner_factor, outer_factor, iterate, residual, direction):
    at = jnp.stack([lax.axis_index(n) for n in ("y", "c", "x", "zh")])
    here = points.shape[0]
    count = float(here * 256)

    def swap(v):
        return lax.ppermute(v, "c", SWAP)

    def fetch(v, k):
        return lax.ppermute(v, "x", [((i + k) % 4, i) for i in range(4)])

    def send(v, k):
        return lax.ppermute(v, "x", [(i, (i + k) % 4) for i in range(4)])

    x = call(prep_body, sds((16, 32, 256), bf16), (at, direction), [SM, VM], name="prep")
    x = exchange(x, LINE)
    term, full, x = call(
        inner_body,
        (sds((16, 256), f32), sds((16, 256), f32), sds((16, 16, 256), bf16)),
        (at, x, swap(x), inner_factor),
        [SM] + [VM] * 3,
        name="inner",
    )
    x = exchange(x, LINE)
    x = call(
        outer_body,
        sds((16, 16, 256), bf16),
        (at, x, swap(x), outer_factor),
        [SM] + [VM] * 3,
        name="outer",
    )
    v = exchange(x, SIDE).reshape(4, 4, 16, 256)
    vs = [v] + [fetch(v, k) for k in (1, 2, 3)]
    us = [swap(v) for v in vs]
    kernel = sds((4, here, 512), bf16)
    sums = sds((here, 64), f32)
    ca = pltpu.VMEM((512, 256), bf16)
    pa, k0 = call(
        fill_body,
        (sds((here, 256), bf16), kernel),
        (at, points, centers),
        [SM, VM, VM],
        scratch=[ca],
        name="fill",
        flops=FILL,
    )
    k1, fit = call(
        both_first_body,
        (kernel, sums),
        (at, pa, centers, vs[0], us[0], k0),
        [SM] + [VM] * 5,
        scratch=[ca],
        name="both0",
        flops=FILL,
    )
    ks = [k0, k1]
    for k in (1, 2):
        more, fit = call(
            functools.partial(both_body, k),
            (kernel, sums),
            (at, pa, centers, vs[k], us[k], ks[k], fit),
            [SM] + [VM] * 6,
            scratch=[ca],
            name=f"both{k}",
            flops=FILL,
        )
        ks.append(more)
    fitted = call(
        fit_body,
        sds((64, here), bf16),
        (vs[3], us[3], ks[3], fit),
        scratch=[pltpu.VMEM((here, 64), f32)],
        name="fit",
        flops=FILL // 2,
    )
    block = sds((2, 4, 4, 8, 256), f32)
    got = []
    for k in (2, 1, 3, 0):
        own, other = call(
            normal_body, (block, block), (fitted, ks[k]), name=f"normal{k}", flops=FILL // 2
        )
        other = swap(other)
        if k:
            x = call(add_body, sds(block.shape, bf16), (own, other), name="add")
            got.append(send(x, k))
    x = call(gather_body, block, (own, other, *got), name="gather")
    x = exchange(x.reshape(32, 8, 256), FACE)
    own, other = call(
        back_outer_body,
        (sds((16, 8, 256), f32), sds((16, 8, 256), f32)),
        (at, x, outer_factor),
        [SM] + [VM] * 2,
        name="back_outer",
    )
    x = call(add_body, sds((16, 8, 256), f32), (own, swap(other)), name="add")
    x = exchange(x, LINE)
    own, other = call(
        functools.partial(back_inner_body, count),
        (sds((16, 8, 384), f32), sds((16, 8, 384), f32)),
        (at, x, inner_factor, term, full, residual),
        [SM] + [VM] * 5,
        name="back_inner",
    )
    x = call(add_body, sds((16, 8, 384), f32), (own, swap(other)), name="add")
    x = exchange(x, LINE)
    keep, x = call(
        step_body,
        (sds((8, 384), f32), sds((64, 128), f32)),
        (at, x, residual),
        [SM, VM, VM],
        name="step",
    )
    far = lax.ppermute(keep, "zh", SWAP)
    x = exchange(x, HALVES)
    x = call(
        beta_body, sds((4, 2, 8, 384), f32), (at, x, keep, far), [SM, VM, VM, VM], name="beta"
    )
    x = exchange(x, ("y",))
    out = sds((64, 256), f32)
    return call(final_body, (out, out, out), (x, iterate, direction), name="final")


def solution(mesh):
    fine = Mesh(mesh.devices.reshape(2, 4, 4, 4, 2), ("zh", "y", "zl", "x", "c"))
    placed = (
        P(ALL, None),
        P(),
        P(ROW, None),
        P(ROW, None),
        P(None, ROW),
        P(None, ROW),
        P(None, ROW),
    )
    return jax.shard_map(
        local,
        mesh=fine,
        in_specs=placed,
        out_specs=(P(None, ROW),) * 3,
        check_vma=False,
    )
```

time: 190 us -> 183 us (0.963)
  blocking collectives: 123 us -> 87.8 us
  starting transfers between devices: 15.4 us -> 31.7 us
  Pallas kernels: 35.8 us -> 42.9 us
  waiting for transfers between devices: 10.7 us -> 15.9 us
    all_to_all x8 -> x7, blocking collectives: 123 us -> 87.8 us  [exchange(): return lax.all_to_all(v, axes, 0, 0, tiled=True)]
    pallas_call x13 -> x23, Pallas kernels: 35.8 us -> 42.9 us  [call(): pl.pallas_call(body, out_shape=outs, in_specs=specs or [VM] * len(args),...]
    ppermute x1 -> x7, waiting for transfers between devices: 2.28 us -> 9.17 us  [the longest x3 6.17 us: send(): return lax.ppermute(v, 'x', [(i, (i + k) % 4) for i in range(4)])]
    all_to_all x0 -> x1, starting transfers between devices: none -> 6.51 us  [exchange(): return lax.all_to_all(v, axes, 0, 0, tiled=True)]
    ppermute x1 -> x7, starting transfers between devices: 4.31 us -> 10.2 us  [the longest x1 5.45 us: local(): far = lax.ppermute(keep, 'zh', SWAP)]
    ppermute x6 -> x12, waiting for transfers between devices: 8.39 us -> 4.23 us  [swap(): return lax.ppermute(v, 'c', SWAP)]
    ppermute x6 -> x12, starting transfers between devices: 11.1 us -> 15 us  [swap(): return lax.ppermute(v, 'c', SWAP)]
    all_to_all x0 -> x1, waiting for transfers between devices: none -> 2.54 us  [exchange(): return lax.all_to_all(v, axes, 0, 0, tiled=True)]
  transfers between devices with their start and end apart: 7 -> 20, of which waited for: 7 -> 10; matrix products, arithmetic and copies ran while one was open for 0% -> 0% of each run, Pallas kernels for 0% -> 14%
where the time goes in v4:
time: 183 us
  blocking collectives  87.8 us (48%)
  Pallas kernels  42.9 us (23%)
  starting transfers between devices  31.7 us (17%)
  waiting for transfers between devices  15.9 us (9%)
  local copies, waits for them, and re-layouts  3.21 us (2%)
    all_to_all x7, blocking collectives, exchange(): return lax.all_to_all(v, axes, 0, 0, tiled=True)  87.8 us
    pallas_call x23, Pallas kernels, call(): pl.pallas_call(body, out_shape=outs, in_specs=specs or [VM] * len(args),...  42.9 us
    ppermute x12, starting transfers between devices, swap(): return lax.ppermute(v, 'c', SWAP)  15 us
    all_to_all x1, starting transfers between devices, exchange(): return lax.all_to_all(v, axes, 0, 0, tiled=True)  6.51 us
    ppermute x3, waiting for transfers between devices, send(): return lax.ppermute(v, 'x', [(i, (i + k) % 4) for i in range(4)])  6.17 us
    ppermute x1, starting transfers between devices, local(): far = lax.ppermute(keep, 'zh', SWAP)  5.45 us
    ppermute x12, waiting for transfers between devices, swap(): return lax.ppermute(v, 'c', SWAP)  4.23 us
  transfers between devices with their start and end apart: 20, of which 10 were waited for; matrix products, arithmetic and copies ran while one was open for 0% of the time, Pallas kernels for 14%

profile of v4, /device:TPU:1, one launch (start us, length us, event | category | flops | bytes accessed | tf_op | source)
XLA Modules:
  0.0 182.5 jit_solution(6132156125538742056)
XLA Ops:
  2.3 18.4 %all_to_all.46.x_ref = bf16[16,32,256]{2,1,0:T(8,128)(2,1)S(1)} all-to-all(bf16[16,32,256]{2,1,0:T(8,128)(2,1)S(1)} %prep.1), channel_id=1, replica_groups=mesh['zh'=2,'y'=4,'zl'=4,'x'=4,'c'=2] {'zl','x'}, dimensions={0} | all-to-all | bytes 524288 | tf_op jit(solution)/shard_map/all_to_all | solution.py:44
  20.7 2.1 %collective-permute-start = (bf16[16,32,256]{2,1,0:T(8,128)(2,1)S(1)}, bf16[16,32,256]{2,1,0:T(8,128)(2,1)S(1)}, u32[]{:S(2)}, u32[]{:S(2)}) collective-permute-start(bf16[16,32,256]{2,1,0:T(8,128)(2,1)S(1)} %all_to_all.46.x_ref), channel_id=1, source_target_pairs={{0,1},{1,0},{2,3},{3,2},{4,5},{5,4},{6,7},{7,6},{8,9},{9,8},{10,11... | collective-permute-start | bytes 786440 | tf_op jit(solution)/shard_map/ppermute | solution.py:295
  23.9 2.2 %copy-done.1 = bf16[256,8192]{1,0:T(8,128)(2,1)S(1)} copy-done((bf16[256,8192]{1,0:T(8,128)(2,1)S(1)}, bf16[256,8192]{1,0:T(8,128)(2,1)}, u32[]{:S(2)}) %copy-start.1) | copy-done | bytes 4194328
  26.1 1.9 %inner.1 = (f32[16,256]{1,0:T(8,128)S(1)}, f32[16,256]{1,0:T(8,128)S(1)}, bf16[16,16,256]{2,1,0:T(8,128)(2,1)S(1)}) custom-call(s32[4]{0:T(128)S(1)} %pad_add_fusion.at_ref, bf16[16,32,256]{2,1,0:T(8,128)(2,1)S(1)} %all_to_all.46.x_ref, bf16[16,32,256]{2,1,0:T(8,128)(2,1)S(1)} %collective-permute-done.y_ref, bf16[256,8192]{1,0:T(8,128)(2,1)S(1)} %copy-done.1), custom_call_target="tpu_custom_call" | custom-call | tf_op jit(solution)/shard_map/inner/pallas_call | solution.py:27
  28.0 11.1 %all_to_all.47.x_ref = bf16[16,16,256]{2,1,0:T(8,128)(2,1)S(1)} all-to-all(bf16[16,16,256]{2,1,0:T(8,128)(2,1)S(1)} %get-tuple-element.28), channel_id=1, replica_groups=mesh['zh'=2,'y'=4,'zl'=4,'x'=4,'c'=2] {'zl','x'}, dimensions={0} | all-to-all | bytes 262144 | tf_op jit(solution)/shard_map/all_to_all | solution.py:44
  39.0 1.8 collective-permute-start.1
  43.6 11.5 %all_to_all.48 = bf16[16,16,256]{2,1,0:T(8,128)(2,1)S(1)} all-to-all(bf16[16,16,256]{2,1,0:T(8,128)(2,1)S(1)} %outer.1), channel_id=1, replica_groups=mesh['zh'=2,'y'=4,'zl'=4,'x'=4,'c'=2] {'y','zl'}, dimensions={0} | all-to-all | bytes 262144 | tf_op jit(solution)/shard_map/all_to_all | solution.py:44
  55.1 1.9 %collective-permute-start.8 = (bf16[4,4,16,256]{3,2,1,0:T(8,128)(2,1)S(1)}, bf16[4,4,16,256]{3,2,1,0:T(8,128)(2,1)S(1)}, u32[]{:S(2)}, u32[]{:S(2)}) collective-permute-start(bf16[4,4,16,256]{3,2,1,0:T(8,128)(2,1)S(1)} %bitcast.12), channel_id=1, source_target_pairs={{0,1},{1,0},{2,3},{3,2},{4,5},{5,4},{6,7},{7,6},{8,9},{9,8},{10,11... | collective-permute-start | bytes 393224 | tf_op jit(solution)/shard_map/ppermute | solution.py:295
  59.1 4.6 %fill.1 = (bf16[2048,256]{1,0:T(8,128)(2,1)S(1)}, bf16[4,2048,512]{2,1,0:T(8,128)(2,1)S(1)}) custom-call(s32[4]{0:T(128)S(1)} %pad_add_fusion.at_ref, bf16[2048,128]{1,0:T(8,128)(2,1)S(1)} %copy-done.8, bf16[8192,128]{1,0:T(8,128)(2,1)S(1)} %copy-done.7), custom_call_target="tpu_custom_call" | custom-call | flops 4000000000 | tf_op jit(solution)/shard_map/fill/pallas_call | solution.py:27
  68.2 6.3 %both0.1 = (bf16[4,2048,512]{2,1,0:T(8,128)(2,1)S(1)}, f32[2048,64]{1,0:T(8,128)S(1)}) custom-call(s32[4]{0:T(128)S(1)} %pad_add_fusion.at_ref, bf16[2048,256]{1,0:T(8,128)(2,1)S(1)} %get-tuple-element.29.pa_ref, bf16[8192,128]{1,0:T(8,128)(2,1)S(1)} %copy-done.7, bf16[4,4,16,256]{3,2,1,0:T(8,128)(2,1)S(1)} %bitcast.16, ...), custom_call_target="tpu_custom_call" | custom-call | flops 4000000000 | tf_op jit(solution)/shard_map/both0/pallas_call | solution.py:27
  74.5 6.3 %both1.1 = (bf16[4,2048,512]{2,1,0:T(8,128)(2,1)S(1)}, f32[2048,64]{1,0:T(8,128)S(1)}) custom-call(s32[4]{0:T(128)S(1)} %pad_add_fusion.at_ref, bf16[2048,256]{1,0:T(8,128)(2,1)S(1)} %get-tuple-element.29.pa_ref, bf16[8192,128]{1,0:T(8,128)(2,1)S(1)} %copy-done.7, bf16[4,4,16,256]{3,2,1,0:T(8,128)(2,1)S(1)} %collective-permute-done.6.v_ref, ...), custom_call_target="tpu_custom_call" | custom-call | flops 4000000000 | tf_op jit(solution)/shard_map/both1/pallas_call | solution.py:27
  80.8 6.3 %both2.1 = (bf16[4,2048,512]{2,1,0:T(8,128)(2,1)S(1)}, f32[2048,64]{1,0:T(8,128)S(1)}) custom-call(s32[4]{0:T(128)S(1)} %pad_add_fusion.at_ref, bf16[2048,256]{1,0:T(8,128)(2,1)S(1)} %get-tuple-element.29.pa_ref, bf16[8192,128]{1,0:T(8,128)(2,1)S(1)} %copy-done.7, bf16[4,4,16,256]{3,2,1,0:T(8,128)(2,1)S(1)} %collective-permute-done.4.v_ref, ...), custom_call_target="tpu_custom_call" | custom-call | flops 4000000000 | tf_op jit(solution)/shard_map/both2/pallas_call | solution.py:27
  87.1 3.0 %fit.1.fit_ref = bf16[64,2048]{1,0:T(8,128)(2,1)S(1)} custom-call(bf16[4,4,16,256]{3,2,1,0:T(8,128)(2,1)S(1)} %collective-permute-done.2.v_ref, bf16[4,4,16,256]{3,2,1,0:T(8,128)(2,1)S(1)} %collective-permute-done.3.u_ref, bf16[4,2048,512]{2,1,0:T(8,128)(2,1)S(1)} %get-tuple-element.35.k_ref, f32[2048,64]{1,0:T(8,128)S(1)} %get-tuple-element.36.old_ref), custom_call_target="tpu_custom_call" | custom-call | flops 2000000000 | tf_op jit(solution)/shard_map/fit/pallas_call | solution.py:27
  100.9 2.4 %collective-permute-done.15.e_ref = bf16[2,4,4,8,256]{4,3,2,1,0:T(8,128)(2,1)S(1)} collective-permute-done((bf16[2,4,4,8,256]{4,3,2,1,0:T(8,128)(2,1)S(1)}, bf16[2,4,4,8,256]{4,3,2,1,0:T(8,128)(2,1)S(1)}, u32[]{:S(2)}, u32[]{:S(2)}) %collective-permute-start.15) | collective-permute-done | bytes 131104 | tf_op jit(solution)/shard_map/ppermute | solution.py:301
  104.9 2.2 %collective-permute-done.11.c_ref = bf16[2,4,4,8,256]{4,3,2,1,0:T(8,128)(2,1)S(1)} collective-permute-done((bf16[2,4,4,8,256]{4,3,2,1,0:T(8,128)(2,1)S(1)}, bf16[2,4,4,8,256]{4,3,2,1,0:T(8,128)(2,1)S(1)}, u32[]{:S(2)}, u32[]{:S(2)}) %collective-permute-start.11) | collective-permute-done | bytes 131104 | tf_op jit(solution)/shard_map/ppermute | solution.py:301
  107.2 17.5 %all_to_all.49.x_ref = f32[32,8,256]{2,1,0:T(8,128)S(1)} all-to-all(f32[32,8,256]{2,1,0:T(8,128)S(1)} %bitcast.10), channel_id=1, replica_groups=mesh['zh'=2,'y'=4,'zl'=4,'x'=4,'c'=2] {'zh','y','zl'}, dimensions={0} | all-to-all | bytes 524288 | tf_op jit(solution)/shard_map/all_to_all | solution.py:44
  125.9 3.4 %collective-permute-start.16 = (f32[16,8,256]{2,1,0:T(8,128)S(1)}, f32[16,8,256]{2,1,0:T(8,128)S(1)}, u32[]{:S(2)}, u32[]{:S(2)}) collective-permute-start(f32[16,8,256]{2,1,0:T(8,128)S(1)} %get-tuple-element.46), channel_id=1, source_target_pairs={{0,1},{1,0},{2,3},{3,2},{4,5},{5,4},{6,7},{7,6},{8,9},{9,8},{10,11... | collective-permute-start | bytes 393224 | tf_op jit(solution)/shard_map/ppermute | solution.py:295
  130.3 10.8 %all_to_all.50.x_ref = f32[16,8,256]{2,1,0:T(8,128)S(1)} all-to-all(f32[16,8,256]{2,1,0:T(8,128)S(1)} %add.14), channel_id=1, replica_groups=mesh['zh'=2,'y'=4,'zl'=4,'x'=4,'c'=2] {'zl','x'}, dimensions={0} | all-to-all | bytes 262144 | tf_op jit(solution)/shard_map/all_to_all | solution.py:44
  142.3 1.8 collective-permute-start.17
  145.2 11.5 %all_to_all.51.x_ref = f32[16,8,384]{2,1,0:T(8,128)S(1)} all-to-all(f32[16,8,384]{2,1,0:T(8,128)S(1)} %add.15), channel_id=1, replica_groups=mesh['zh'=2,'y'=4,'zl'=4,'x'=4,'c'=2] {'zl','x'}, dimensions={0} | all-to-all | bytes 393216 | tf_op jit(solution)/shard_map/all_to_all | solution.py:44
  158.1 6.5 %all-to-all-start.6 = ((f32[64,1,128]{2,1,0:T(1,128)}), f32[64,1,128]{2,1,0:T(1,128)S(1)}, u32[]{:S(2)}, u32[]{:S(2)}) async-start(f32[64,1,128]{2,1,0:T(1,128)} %bitcast.7), calls=%async_computation.6 | async-start | bytes 65536 | tf_op jit(solution)/shard_map/all_to_all | solution.py:44
  164.7 5.5 %collective-permute-start.18 = (f32[8,384]{1,0:T(8,128)S(1)}, f32[8,384]{1,0:T(8,128)S(1)}, u32[]{:S(2)}, u32[]{:S(2)}) collective-permute-start(f32[8,384]{1,0:T(8,128)S(1)} %get-tuple-element.52.keep_ref), channel_id=1, source_target_pairs={{0,128},{128,0},{1,129},{129,1},{2,130},{130,2},{3,131},{131,3},{4... | collective-permute-start | bytes 36872 | tf_op jit(solution)/shard_map/ppermute | solution.py:401
  171.5 2.5 %all-to-all-done.6 = f32[64,1,128]{2,1,0:T(1,128)S(1)} async-done(((f32[64,1,128]{2,1,0:T(1,128)}), f32[64,1,128]{2,1,0:T(1,128)S(1)}, u32[]{:S(2)}, u32[]{:S(2)}) %all-to-all-start.6) | async-done | bytes 32800 | tf_op jit(solution)/shard_map/all_to_all | solution.py:44
  174.8 7.0 %all_to_all.52.x_ref = f32[4,2,8,384]{3,2,1,0:T(8,128)S(1)} all-to-all(f32[4,2,8,384]{3,2,1,0:T(8,128)S(1)} %beta.1), channel_id=1, replica_groups=mesh['zh'=2,'y'=4,'zl'=4,'x'=4,'c'=2] {'y'}, dimensions={0} | all-to-all | bytes 196608 | tf_op jit(solution)/shard_map/all_to_all | solution.py:44
  (65 shorter events, 33.4 us)
Async XLA Ops:
  20.7 3.2 %collective-permute-start = (bf16[16,32,256]{2,1,0:T(8,128)(2,1)S(1)}, bf16[16,32,256]{2,1,0:T(8,128)(2,1)S(1)}, u32[]{:S(2)}, u32[]{:S(2)}) collective-permute-start(bf16[16,32,256]{2,1,0:T(8,128)(2,1)S(1)} %all_to_all.46.x_ref), channel_id=1, source_target_pairs={{0,1},{1,0},{2,3},{3,2},{4,5},{5,4},{6,7},{7,6},{8,9},{9,8},{10,11... | collective-permute-start | bytes 786440 | tf_op jit(solution)/shard_map/ppermute | solution.py:295
  39.0 2.8 %collective-permute-start.1 = (bf16[16,16,256]{2,1,0:T(8,128)(2,1)S(1)}, bf16[16,16,256]{2,1,0:T(8,128)(2,1)S(1)}, u32[]{:S(2)}, u32[]{:S(2)}) collective-permute-start(bf16[16,16,256]{2,1,0:T(8,128)(2,1)S(1)} %all_to_all.47.x_ref), channel_id=1, source_target_pairs={{0,1},{1,0},{2,3},{3,2},{4,5},{5,4},{6,7},{7,6},{8,9},{9,8},{10,11... | collective-permute-start | bytes 393224 | tf_op jit(solution)/shard_map/ppermute | solution.py:295
  55.1 13.1 %collective-permute-start.8 = (bf16[4,4,16,256]{3,2,1,0:T(8,128)(2,1)S(1)}, bf16[4,4,16,256]{3,2,1,0:T(8,128)(2,1)S(1)}, u32[]{:S(2)}, u32[]{:S(2)}) collective-permute-start(bf16[4,4,16,256]{3,2,1,0:T(8,128)(2,1)S(1)} %bitcast.12), channel_id=1, source_target_pairs={{0,1},{1,0},{2,3},{3,2},{4,5},{5,4},{6,7},{7,6},{8,9},{9,8},{10,11... | collective-permute-start | bytes 393224 | tf_op jit(solution)/shard_map/ppermute | solution.py:295
  57.0 6.8 %collective-permute-start.6 = (bf16[4,4,16,256]{3,2,1,0:T(8,128)(2,1)S(1)}, bf16[4,4,16,256]{3,2,1,0:T(8,128)(2,1)S(1)}, u32[]{:S(2)}, u32[]{:S(2)}) collective-permute-start(bf16[4,4,16,256]{3,2,1,0:T(8,128)(2,1)S(1)} %bitcast.13), channel_id=1, source_target_pairs={{2,0},{4,2},{6,4},{0,6},{3,1},{5,3},{7,5},{1,7},{10,8},{12,10},{14... | collective-permute-start | bytes 393224 | tf_op jit(solution)/shard_map/ppermute | solution.py:298
  58.0 6.7 %collective-permute-start.4 = (bf16[4,4,16,256]{3,2,1,0:T(8,128)(2,1)S(1)}, bf16[4,4,16,256]{3,2,1,0:T(8,128)(2,1)S(1)}, u32[]{:S(2)}, u32[]{:S(2)}) collective-permute-start(bf16[4,4,16,256]{3,2,1,0:T(8,128)(2,1)S(1)} %bitcast.14), channel_id=1, source_target_pairs={{4,0},{6,2},{0,4},{2,6},{5,1},{7,3},{1,5},{3,7},{12,8},{14,10},{8,... | collective-permute-start | bytes 393224 | tf_op jit(solution)/shard_map/ppermute | solution.py:298
  58.9 8.8 %collective-permute-start.2 = (bf16[4,4,16,256]{3,2,1,0:T(8,128)(2,1)S(1)}, bf16[4,4,16,256]{3,2,1,0:T(8,128)(2,1)S(1)}, u32[]{:S(2)}, u32[]{:S(2)}) collective-permute-start(bf16[4,4,16,256]{3,2,1,0:T(8,128)(2,1)S(1)} %bitcast.15), channel_id=1, source_target_pairs={{6,0},{0,2},{2,4},{4,6},{7,1},{1,3},{3,5},{5,7},{14,8},{8,10},{10,... | collective-permute-start | bytes 393224 | tf_op jit(solution)/shard_map/ppermute | solution.py:298
  63.8 10.7 %collective-permute-start.7 = (bf16[4,4,16,256]{3,2,1,0:T(8,128)(2,1)S(1)}, bf16[4,4,16,256]{3,2,1,0:T(8,128)(2,1)S(1)}, u32[]{:S(2)}, u32[]{:S(2)}) collective-permute-start(bf16[4,4,16,256]{3,2,1,0:T(8,128)(2,1)S(1)} %collective-permute-done.6.v_ref), channel_id=1, source_target_pairs={{0,1},{1,0},{2,3},{3,2},{4,5},{5,4},{6,7},{7,6},{8,9},{9,8},{10,11... | collective-permute-start | bytes 393224 | tf_op jit(solution)/shard_map/ppermute | solution.py:295
  64.7 16.1 %collective-permute-start.5 = (bf16[4,4,16,256]{3,2,1,0:T(8,128)(2,1)S(1)}, bf16[4,4,16,256]{3,2,1,0:T(8,128)(2,1)S(1)}, u32[]{:S(2)}, u32[]{:S(2)}) collective-permute-start(bf16[4,4,16,256]{3,2,1,0:T(8,128)(2,1)S(1)} %collective-permute-done.4.v_ref), channel_id=1, source_target_pairs={{0,1},{1,0},{2,3},{3,2},{4,5},{5,4},{6,7},{7,6},{8,9},{9,8},{10,11... | collective-permute-start | bytes 393224 | tf_op jit(solution)/shard_map/ppermute | solution.py:295
  67.7 19.3 %collective-permute-start.3 = (bf16[4,4,16,256]{3,2,1,0:T(8,128)(2,1)S(1)}, bf16[4,4,16,256]{3,2,1,0:T(8,128)(2,1)S(1)}, u32[]{:S(2)}, u32[]{:S(2)}) collective-permute-start(bf16[4,4,16,256]{3,2,1,0:T(8,128)(2,1)S(1)} %collective-permute-done.2.v_ref), channel_id=1, source_target_pairs={{0,1},{1,0},{2,3},{3,2},{4,5},{5,4},{6,7},{7,6},{8,9},{9,8},{10,11... | collective-permute-start | bytes 393224 | tf_op jit(solution)/shard_map/ppermute | solution.py:295
  95.3 3.0 %collective-permute-start.14 = (f32[2,4,4,8,256]{4,3,2,1,0:T(8,128)S(1)}, f32[2,4,4,8,256]{4,3,2,1,0:T(8,128)S(1)}, u32[]{:S(2)}, u32[]{:S(2)}) collective-permute-start(f32[2,4,4,8,256]{4,3,2,1,0:T(8,128)S(1)} %get-tuple-element.44), channel_id=1, source_target_pairs={{0,1},{1,0},{2,3},{3,2},{4,5},{5,4},{6,7},{7,6},{8,9},{9,8},{10,11... | collective-permute-start | bytes 786440 | tf_op jit(solution)/shard_map/ppermute | solution.py:295
  95.4 3.2 %collective-permute-start.12 = (f32[2,4,4,8,256]{4,3,2,1,0:T(8,128)S(1)}, f32[2,4,4,8,256]{4,3,2,1,0:T(8,128)S(1)}, u32[]{:S(2)}, u32[]{:S(2)}) collective-permute-start(f32[2,4,4,8,256]{4,3,2,1,0:T(8,128)S(1)} %get-tuple-element.42), channel_id=1, source_target_pairs={{0,1},{1,0},{2,3},{3,2},{4,5},{5,4},{6,7},{7,6},{8,9},{9,8},{10,11... | collective-permute-start | bytes 786440 | tf_op jit(solution)/shard_map/ppermute | solution.py:295
  95.9 45.2 %copy-start.2 = (bf16[256,8192]{1,0:T(8,128)(2,1)S(1)}, bf16[256,8192]{1,0:T(8,128)(2,1)}, u32[]{:S(2)}) copy-start(bf16[256,8192]{1,0:T(8,128)(2,1)} %f_ref.7) | copy-start | bytes 12582916
  95.9 45.2 %copy-start.3 = (f32[64,256]{1,0:T(8,128)S(1)}, f32[64,256]{1,0:T(8,128)}, u32[]{:S(2)}) copy-start(f32[64,256]{1,0:T(8,128)} %res_ref.3) | copy-start | bytes 196612
  95.9 4.0 %collective-permute-start.10 = (f32[2,4,4,8,256]{4,3,2,1,0:T(8,128)S(1)}, f32[2,4,4,8,256]{4,3,2,1,0:T(8,128)S(1)}, u32[]{:S(2)}, u32[]{:S(2)}) collective-permute-start(f32[2,4,4,8,256]{4,3,2,1,0:T(8,128)S(1)} %get-tuple-element.40), channel_id=1, source_target_pairs={{0,1},{1,0},{2,3},{3,2},{4,5},{5,4},{6,7},{7,6},{8,9},{9,8},{10,11... | collective-permute-start | bytes 786440 | tf_op jit(solution)/shard_map/ppermute | solution.py:295
  97.7 84.1 %copy-start.5 = (f32[64,256]{1,0:T(8,128)S(1)}, f32[64,256]{1,0:T(8,128)}, u32[]{:S(2)}) copy-start(f32[64,256]{1,0:T(8,128)} %d_ref.3) | copy-start | bytes 196612
  97.7 84.1 %copy-start.6 = (f32[64,256]{1,0:T(8,128)S(1)}, f32[64,256]{1,0:T(8,128)}, u32[]{:S(2)}) copy-start(f32[64,256]{1,0:T(8,128)} %it_ref.1) | copy-start | bytes 196612
  97.7 3.2 %collective-permute-start.9 = (f32[2,4,4,8,256]{4,3,2,1,0:T(8,128)S(1)}, f32[2,4,4,8,256]{4,3,2,1,0:T(8,128)S(1)}, u32[]{:S(2)}, u32[]{:S(2)}) collective-permute-start(f32[2,4,4,8,256]{4,3,2,1,0:T(8,128)S(1)} %get-tuple-element.38), channel_id=1, source_target_pairs={{0,1},{1,0},{2,3},{3,2},{4,5},{5,4},{6,7},{7,6},{8,9},{9,8},{10,11... | collective-permute-start | bytes 786440 | tf_op jit(solution)/shard_map/ppermute | solution.py:295
  98.3 5.0 %collective-permute-start.15 = (bf16[2,4,4,8,256]{4,3,2,1,0:T(8,128)(2,1)S(1)}, bf16[2,4,4,8,256]{4,3,2,1,0:T(8,128)(2,1)S(1)}, u32[]{:S(2)}, u32[]{:S(2)}) collective-permute-start(bf16[2,4,4,8,256]{4,3,2,1,0:T(8,128)(2,1)S(1)} %add.13), channel_id=1, source_target_pairs={{0,6},{2,0},{4,2},{6,4},{1,7},{3,1},{5,3},{7,5},{8,14},{10,8},{12,... | collective-permute-start | bytes 393224 | tf_op jit(solution)/shard_map/ppermute | solution.py:301
  98.7 6.3 %collective-permute-start.13 = (bf16[2,4,4,8,256]{4,3,2,1,0:T(8,128)(2,1)S(1)}, bf16[2,4,4,8,256]{4,3,2,1,0:T(8,128)(2,1)S(1)}, u32[]{:S(2)}, u32[]{:S(2)}) collective-permute-start(bf16[2,4,4,8,256]{4,3,2,1,0:T(8,128)(2,1)S(1)} %add.12), channel_id=1, source_target_pairs={{0,2},{2,4},{4,6},{6,0},{1,3},{3,5},{5,7},{7,1},{8,10},{10,12},{12... | collective-permute-start | bytes 393224 | tf_op jit(solution)/shard_map/ppermute | solution.py:301
  100.0 7.2 %collective-permute-start.11 = (bf16[2,4,4,8,256]{4,3,2,1,0:T(8,128)(2,1)S(1)}, bf16[2,4,4,8,256]{4,3,2,1,0:T(8,128)(2,1)S(1)}, u32[]{:S(2)}, u32[]{:S(2)}) collective-permute-start(bf16[2,4,4,8,256]{4,3,2,1,0:T(8,128)(2,1)S(1)} %add.11), channel_id=1, source_target_pairs={{0,4},{2,6},{4,0},{6,2},{1,5},{3,7},{5,1},{7,3},{8,12},{10,14},{12... | collective-permute-start | bytes 393224 | tf_op jit(solution)/shard_map/ppermute | solution.py:301
  125.9 4.4 %collective-permute-start.16 = (f32[16,8,256]{2,1,0:T(8,128)S(1)}, f32[16,8,256]{2,1,0:T(8,128)S(1)}, u32[]{:S(2)}, u32[]{:S(2)}) collective-permute-start(f32[16,8,256]{2,1,0:T(8,128)S(1)} %get-tuple-element.46), channel_id=1, source_target_pairs={{0,1},{1,0},{2,3},{3,2},{4,5},{5,4},{6,7},{7,6},{8,9},{9,8},{10,11... | collective-permute-start | bytes 393224 | tf_op jit(solution)/shard_map/ppermute | solution.py:295
  142.3 2.9 %collective-permute-start.17 = (f32[16,8,384]{2,1,0:T(8,128)S(1)}, f32[16,8,384]{2,1,0:T(8,128)S(1)}, u32[]{:S(2)}, u32[]{:S(2)}) collective-permute-start(f32[16,8,384]{2,1,0:T(8,128)S(1)} %get-tuple-element.50), channel_id=1, source_target_pairs={{0,1},{1,0},{2,3},{3,2},{4,5},{5,4},{6,7},{7,6},{8,9},{9,8},{10,11... | collective-permute-start | bytes 589832 | tf_op jit(solution)/shard_map/ppermute | solution.py:295
  158.1 15.9 %all-to-all-start.6 = ((f32[64,1,128]{2,1,0:T(1,128)}), f32[64,1,128]{2,1,0:T(1,128)S(1)}, u32[]{:S(2)}, u32[]{:S(2)}) async-start(f32[64,1,128]{2,1,0:T(1,128)} %bitcast.7), calls=%async_computation.6 | async-start | bytes 65536 | tf_op jit(solution)/shard_map/all_to_all | solution.py:44
  164.7 6.9 %collective-permute-start.18 = (f32[8,384]{1,0:T(8,128)S(1)}, f32[8,384]{1,0:T(8,128)S(1)}, u32[]{:S(2)}, u32[]{:S(2)}) collective-permute-start(f32[8,384]{1,0:T(8,128)S(1)} %get-tuple-element.52.keep_ref), channel_id=1, source_target_pairs={{0,128},{128,0},{1,129},{129,1},{2,130},{130,2},{3,131},{131,3},{4... | collective-permute-start | bytes 36872 | tf_op jit(solution)/shard_map/ppermute | solution.py:401
  (5 other events, 110.5 us)

commit v5 on v4

--- a/solution.py
+++ b/solution.py
@@ -23,7 +23,7 @@
 SM = pl.BlockSpec(memory_space=pltpu.SMEM)
 
 
-def call(body, outs, args, specs=None, scratch=(), vmem=10, name=None, flops=0):
+def call(body, outs, args, specs=None, scratch=(), vmem=10, flops=0):
     return pl.pallas_call(
         body,
         out_shape=outs,
@@ -32,7 +32,6 @@
         scratch_shapes=scratch,
         compiler_params=pltpu.CompilerParams(vmem_limit_bytes=vmem * MIB),
         cost_estimate=pl.CostEstimate(flops=flops, bytes_accessed=0, transcendentals=0),
-        name=name,
     )(*args)
 
 
@@ -81,8 +80,27 @@
     return acc
 
 
-def inner_body(at_ref, x_ref, y_ref, f_ref, term_ref, full_ref, out_ref):
-    acc = rows_dot(at_ref, x_ref, y_ref, f_ref)
+def inner_body(at_ref, x_ref, y_ref, hbm_ref, term_ref, full_ref, out_ref, f_ref, sem):
+    parts = sem.shape[0]
+    width = hbm_ref.shape[1] // parts
+    copies = [
+        pltpu.make_async_copy(
+            hbm_ref.at[:, pl.ds(q * width, width)], f_ref.at[:, pl.ds(q * width, width)], sem.at[q]
+        )
+        for q in range(parts)
+    ]
+    for copy in copies:
+        copy.start()
+    acc = None
+    count = x_ref.shape[0] // parts
+    for q in range(parts):
+        copies[q].wait()
+        for z in range(q * count, q * count + count):
+            for which, ref in ((0, x_ref), (1, y_ref)):
+                part = lax.dot_general(
+                    ref[z], f_ref[:, columns(at_ref, z, which)], LAST, preferred_element_type=f32
+                )
+                acc = part if acc is None else acc + part
     term_ref[...] = acc[:16]
     full_ref[...] = acc[:16] + acc[16:]
     spread(acc[:16].astype(bf16), out_ref)
@@ -107,22 +125,37 @@
     return jnp.where(lane == a, one, out).astype(bf16)
 
 
-def fill(at_ref, shift, i, pa_ref, cen_ref, ca_ref, k_ref, fit=None):
-    z = i * 4 + (at_ref[2] + shift) % 4
+def chunks(at_ref, shift, pa_ref, cen_ref, ca_ref, k_ref, fit=None):
     step = 256
-    for h in range(2):
-        cols = slice(h * 256, h * 256 + 256)
-        block = cen_ref[columns(at_ref, z, h), :]
-        ca_ref[cols, :128] = block
-        ca_ref[cols, 128:] = norm_lanes(block, False)
-    for r in range(pa_ref.shape[0] // step):
-        rows = pl.ds(r * step, step)
-        if fit is not None:
-            fit(i, rows)
+
+    def load(i, slot):
+        z = i * 4 + (at_ref[2] + shift) % 4
         for h in range(2):
             cols = slice(h * 256, h * 256 + 256)
-            d = lax.dot_general(pa_ref[rows, :], ca_ref[cols, :], LAST, preferred_element_type=f32)
-            k_ref[i, rows, cols] = jnp.exp2(d * (LOG2E * 8.0 / 128.0)).astype(bf16)
+            block = cen_ref[columns(at_ref, z, h), :]
+            ca_ref[slot, cols, :128] = block
+            ca_ref[slot, cols, 128:] = norm_lanes(block, False)
+
+    load(0, 0)
+
+    def two(j, carry):
+        for slot in range(2):
+            i = j * 2 + slot
+            load(jnp.minimum(i + 1, 3), 1 - slot)
+            w = None if fit is None else fit.weights(i)
+            for r in range(pa_ref.shape[0] // step):
+                rows = pl.ds(r * step, step)
+                if fit is not None:
+                    fit.add(w, i, rows)
+                for h in range(2):
+                    cols = slice(h * 256, h * 256 + 256)
+                    d = lax.dot_general(
+                        pa_ref[rows, :], ca_ref[slot, cols, :], LAST, preferred_element_type=f32
+                    )
+                    k_ref[i, rows, cols] = jnp.exp2(d * (LOG2E * 8.0 / 128.0)).astype(bf16)
+        return carry
+
+    lax.fori_loop(0, 2, two, 0)
 
 
 def fill_body(at_ref, p_ref, cen_ref, pa_ref, k_ref, ca_ref):
@@ -130,55 +163,46 @@
     for r in range(p_ref.shape[0] // 256):
         rows = pl.ds(r * 256, 256)
         pa_ref[rows, 128:] = norm_lanes(p_ref[rows, :], True)
-
-    def chunk(i, carry):
-        fill(at_ref, 0, i, pa_ref, cen_ref, ca_ref, k_ref)
-        return carry
-
-    lax.fori_loop(0, k_ref.shape[0], chunk, 0)
-
-
-def fitter(v_ref, u_ref, k_ref, sum_ref):
-    def fit(i, rows):
-        w = jnp.concatenate(
+    chunks(at_ref, 0, pa_ref, cen_ref, ca_ref, k_ref)
+
+
+class Fitter:
+    def __init__(self, v_ref, u_ref, k_ref, sum_ref):
+        self.refs = v_ref, u_ref, k_ref, sum_ref
+
+    def weights(self, i):
+        v_ref, u_ref = self.refs[:2]
+        return jnp.concatenate(
             [v_ref[:, i, :, :].reshape(64, 256), u_ref[:, i, :, :].reshape(64, 256)], axis=1
         )
+
+    def add(self, w, i, rows):
+        k_ref, sum_ref = self.refs[2:]
         sum_ref[rows, :] += lax.dot_general(
             k_ref[i, rows, :], w, LAST, preferred_element_type=f32
         )
 
-    return fit
-
 
 def both_body(shift, at_ref, pa_ref, cen_ref, v_ref, u_ref, k_ref, old_ref, next_ref, sum_ref, ca_ref):
     sum_ref[...] = old_ref[...]
-    fit = fitter(v_ref, u_ref, k_ref, sum_ref)
-
-    def chunk(i, carry):
-        fill(at_ref, shift + 1, i, pa_ref, cen_ref, ca_ref, next_ref, fit)
-        return carry
-
-    lax.fori_loop(0, k_ref.shape[0], chunk, 0)
+    fit = Fitter(v_ref, u_ref, k_ref, sum_ref)
+    chunks(at_ref, shift + 1, pa_ref, cen_ref, ca_ref, next_ref, fit)
 
 
 def both_first_body(at_ref, pa_ref, cen_ref, v_ref, u_ref, k_ref, next_ref, sum_ref, ca_ref):
     sum_ref[...] = jnp.zeros_like(sum_ref)
-    fit = fitter(v_ref, u_ref, k_ref, sum_ref)
-
-    def chunk(i, carry):
-        fill(at_ref, 1, i, pa_ref, cen_ref, ca_ref, next_ref, fit)
-        return carry
-
-    lax.fori_loop(0, k_ref.shape[0], chunk, 0)
+    fit = Fitter(v_ref, u_ref, k_ref, sum_ref)
+    chunks(at_ref, 1, pa_ref, cen_ref, ca_ref, next_ref, fit)
 
 
 def fit_body(v_ref, u_ref, k_ref, old_ref, out_ref, sum_ref):
     sum_ref[...] = old_ref[...]
-    fit = fitter(v_ref, u_ref, k_ref, sum_ref)
+    fit = Fitter(v_ref, u_ref, k_ref, sum_ref)
 
     def chunk(i, carry):
-        for r in range(8):
-            fit(i, pl.ds(r * 256, 256))
+        w = fit.weights(i)
+        for r in range(k_ref.shape[1] // 256):
+            fit.add(w, i, pl.ds(r * 256, 256))
         return carry
 
     lax.fori_loop(0, k_ref.shape[0], chunk, 0)
@@ -211,11 +235,12 @@
 
 
 def gather_body(a_ref, b_ref, c_ref, d_ref, e_ref, out_ref):
-    out_ref[...] = (
+    total = (
         (a_ref[...] + b_ref[...])
         + (c_ref[...].astype(f32) + d_ref[...].astype(f32))
         + e_ref[...].astype(f32)
     )
+    out_ref[...] = total.astype(out_ref.dtype)
 
 
 def back_outer_body(at_ref, x_ref, f_ref, own_ref, oth_ref):
@@ -286,7 +311,7 @@
             nd_ref[rows, :] = new + x_ref[g, h, :, 257:258] * d
 
 
-def local(points, centers, inner_factor, outer_factor, iterate, residual, direction):
+def iteration(points, centers, inner_factor, outer_factor, iterate, residual, direction):
     at = jnp.stack([lax.axis_index(n) for n in ("y", "c", "x", "zh")])
     here = points.shape[0]
     count = float(here * 256)
@@ -300,36 +325,29 @@
     def send(v, k):
         return lax.ppermute(v, "x", [(i, (i + k) % 4) for i in range(4)])
 
-    x = call(prep_body, sds((16, 32, 256), bf16), (at, direction), [SM, VM], name="prep")
+    x = call(prep_body, sds((16, 32, 256), bf16), (at, direction), [SM, VM])
     x = exchange(x, LINE)
     term, full, x = call(
         inner_body,
         (sds((16, 256), f32), sds((16, 256), f32), sds((16, 16, 256), bf16)),
-        (at, x, swap(x), inner_factor),
-        [SM] + [VM] * 3,
-        name="inner",
+        (at, x, swap(x), pltpu.with_memory_space_constraint(inner_factor, pltpu.HBM)),
+        [SM, VM, VM, pl.BlockSpec(memory_space=pltpu.HBM)],
+        scratch=[pltpu.VMEM(inner_factor.shape, bf16), pltpu.SemaphoreType.DMA((4,))],
     )
     x = exchange(x, LINE)
-    x = call(
-        outer_body,
-        sds((16, 16, 256), bf16),
-        (at, x, swap(x), outer_factor),
-        [SM] + [VM] * 3,
-        name="outer",
-    )
+    x = call(outer_body, sds((16, 16, 256), bf16), (at, x, swap(x), outer_factor), [SM] + [VM] * 3)
     v = exchange(x, SIDE).reshape(4, 4, 16, 256)
     vs = [v] + [fetch(v, k) for k in (1, 2, 3)]
     us = [swap(v) for v in vs]
     kernel = sds((4, here, 512), bf16)
     sums = sds((here, 64), f32)
-    ca = pltpu.VMEM((512, 256), bf16)
+    ca = pltpu.VMEM((2, 512, 256), bf16)
     pa, k0 = call(
         fill_body,
         (sds((here, 256), bf16), kernel),
         (at, points, centers),
         [SM, VM, VM],
         scratch=[ca],
-        name="fill",
         flops=FILL,
     )
     k1, fit = call(
@@ -338,7 +356,6 @@
         (at, pa, centers, vs[0], us[0], k0),
         [SM] + [VM] * 5,
         scratch=[ca],
-        name="both0",
         flops=FILL,
     )
     ks = [k0, k1]
@@ -349,7 +366,6 @@
             (at, pa, centers, vs[k], us[k], ks[k], fit),
             [SM] + [VM] * 6,
             scratch=[ca],
-            name=f"both{k}",
             flops=FILL,
         )
         ks.append(more)
@@ -358,54 +374,43 @@
         sds((64, here), bf16),
         (vs[3], us[3], ks[3], fit),
         scratch=[pltpu.VMEM((here, 64), f32)],
-        name="fit",
         flops=FILL // 2,
     )
     block = sds((2, 4, 4, 8, 256), f32)
     got = []
     for k in (2, 1, 3, 0):
-        own, other = call(
-            normal_body, (block, block), (fitted, ks[k]), name=f"normal{k}", flops=FILL // 2
-        )
+        own, other = call(normal_body, (block, block), (fitted, ks[k]), flops=FILL // 2)
         other = swap(other)
         if k:
-            x = call(add_body, sds(block.shape, bf16), (own, other), name="add")
+            x = call(add_body, sds(block.shape, bf16), (own, other))
             got.append(send(x, k))
-    x = call(gather_body, block, (own, other, *got), name="gather")
+    x = call(gather_body, sds(block.shape, bf16), (own, other, *got))
     x = exchange(x.reshape(32, 8, 256), FACE)
     own, other = call(
         back_outer_body,
         (sds((16, 8, 256), f32), sds((16, 8, 256), f32)),
         (at, x, outer_factor),
         [SM] + [VM] * 2,
-        name="back_outer",
-    )
-    x = call(add_body, sds((16, 8, 256), f32), (own, swap(other)), name="add")
+    )
+    x = call(add_body, sds((16, 8, 256), f32), (own, swap(other)))
     x = exchange(x, LINE)
     own, other = call(
         functools.partial(back_inner_body, count),
         (sds((16, 8, 384), f32), sds((16, 8, 384), f32)),
         (at, x, inner_factor, term, full, residual),
         [SM] + [VM] * 5,
-        name="back_inner",
-    )
-    x = call(add_body, sds((16, 8, 384), f32), (own, swap(other)), name="add")
+    )
+    x = call(add_body, sds((16, 8, 384), f32), (own, swap(other)))
     x = exchange(x, LINE)
     keep, x = call(
-        step_body,
-        (sds((8, 384), f32), sds((64, 128), f32)),
-        (at, x, residual),
-        [SM, VM, VM],
-        name="step",
+        step_body, (sds((8, 384), f32), sds((64, 128), f32)), (at, x, residual), [SM, VM, VM]
     )
     far = lax.ppermute(keep, "zh", SWAP)
     x = exchange(x, HALVES)
-    x = call(
-        beta_body, sds((4, 2, 8, 384), f32), (at, x, keep, far), [SM, VM, VM, VM], name="beta"
-    )
+    x = call(beta_body, sds((4, 2, 8, 384), f32), (at, x, keep, far), [SM, VM, VM, VM])
     x = exchange(x, ("y",))
     out = sds((64, 256), f32)
-    return call(final_body, (out, out, out), (x, iterate, direction), name="final")
+    return call(final_body, (out, out, out), (x, iterate, direction))
 
 
 def solution(mesh):
@@ -420,7 +425,7 @@
         P(None, ROW),
     )
     return jax.shard_map(
-        local,
+        iteration,
         mesh=fine,
         in_specs=placed,
         out_specs=(P(None, ROW),) * 3,

time: 183 us -> 179 us (0.978)
  local copies, waits for them, and re-layouts: 3.21 us -> 1.02 us
    unnamed x18 -> x16, local copies, waits for them, and re-layouts: 3.21 us -> 1.02 us
  transfers between devices with their start and end apart: 20 -> 20, of which waited for: 10 -> 11; matrix products, arithmetic and copies ran while one was open for 0% -> 0% of each run, Pallas kernels for 14% -> 13%
where the time goes in v5:
time: 179 us
  blocking collectives  86.4 us (48%)
  Pallas kernels  42.6 us (24%)
  starting transfers between devices  32 us (18%)
  waiting for transfers between devices  16.1 us (9%)
    all_to_all x7, blocking collectives, exchange(): return lax.all_to_all(v, axes, 0, 0, tiled=True)  86.4 us
    pallas_call x23, Pallas kernels, call(): pl.pallas_call(body, out_shape=outs, in_specs=specs or [VM] * len(args),...  42.6 us
    ppermute x12, starting transfers between devices, swap(): return lax.ppermute(v, 'c', SWAP)  15.1 us
    all_to_all x1, starting transfers between devices, exchange(): return lax.all_to_all(v, axes, 0, 0, tiled=True)  6.79 us
    ppermute x3, waiting for transfers between devices, send(): return lax.ppermute(v, 'x', [(i, (i + k) % 4) for i in range(4)])  6.16 us
    ppermute x1, starting transfers between devices, iteration(): far = lax.ppermute(keep, 'zh', SWAP)  5.45 us
    ppermute x12, waiting for transfers between devices, swap(): return lax.ppermute(v, 'c', SWAP)  4.23 us
  transfers between devices with their start and end apart: 20, of which 11 were waited for; matrix products, arithmetic and copies ran while one was open for 0% of the time, Pallas kernels for 13%

profile of v5, /device:TPU:1, one launch (start us, length us, event | category | flops | bytes accessed | tf_op | source)
XLA Modules:
  0.0 179.0 jit_solution(1553237367699649168)
XLA Ops:
  2.3 18.5 %all_to_all.46.x_ref = bf16[16,32,256]{2,1,0:T(8,128)(2,1)S(1)} all-to-all(bf16[16,32,256]{2,1,0:T(8,128)(2,1)S(1)} %shard_map.94), channel_id=1, replica_groups=mesh['zh'=2,'y'=4,'zl'=4,'x'=4,'c'=2] {'zl','x'}, dimensions={0} | all-to-all | bytes 524288 | tf_op jit(solution)/shard_map/all_to_all | solution.py:43
  20.8 2.1 %collective-permute-start = (bf16[16,32,256]{2,1,0:T(8,128)(2,1)S(1)}, bf16[16,32,256]{2,1,0:T(8,128)(2,1)S(1)}, u32[]{:S(2)}, u32[]{:S(2)}) collective-permute-start(bf16[16,32,256]{2,1,0:T(8,128)(2,1)S(1)} %all_to_all.46.x_ref), channel_id=1, source_target_pairs={{0,1},{1,0},{2,3},{3,2},{4,5},{5,4},{6,7},{7,6},{8,9},{9,8},{10,11... | collective-permute-start | bytes 786440 | tf_op jit(solution)/shard_map/ppermute | solution.py:320
  24.0 4.2 %shard_map.95 = (f32[16,256]{1,0:T(8,128)S(1)}, f32[16,256]{1,0:T(8,128)S(1)}, bf16[16,16,256]{2,1,0:T(8,128)(2,1)S(1)}) custom-call(s32[4]{0:T(128)S(1)} %pad_add_fusion.at_ref, bf16[16,32,256]{2,1,0:T(8,128)(2,1)S(1)} %all_to_all.46.x_ref, bf16[16,32,256]{2,1,0:T(8,128)(2,1)S(1)} %collective-permute-done.y_ref, bf16[256,8192]{1,0:T(8,128)(2,1)} %f_ref.5), custom_call_target="tpu_custom_call" | custom-call | tf_op jit(solution)/shard_map/pallas_call | solution.py:27
  28.3 11.1 %all_to_all.47.x_ref = bf16[16,16,256]{2,1,0:T(8,128)(2,1)S(1)} all-to-all(bf16[16,16,256]{2,1,0:T(8,128)(2,1)S(1)} %get-tuple-element.28), channel_id=1, replica_groups=mesh['zh'=2,'y'=4,'zl'=4,'x'=4,'c'=2] {'zl','x'}, dimensions={0} | all-to-all | bytes 262144 | tf_op jit(solution)/shard_map/all_to_all | solution.py:43
  39.3 1.8 %collective-permute-start.1 = (bf16[16,16,256]{2,1,0:T(8,128)(2,1)S(1)}, bf16[16,16,256]{2,1,0:T(8,128)(2,1)S(1)}, u32[]{:S(2)}, u32[]{:S(2)}) collective-permute-start(bf16[16,16,256]{2,1,0:T(8,128)(2,1)S(1)} %all_to_all.47.x_ref), channel_id=1, source_target_pairs={{0,1},{1,0},{2,3},{3,2},{4,5},{5,4},{6,7},{7,6},{8,9},{9,8},{10,11... | collective-permute-start | bytes 393224 | tf_op jit(solution)/shard_map/ppermute | solution.py:320
  43.9 11.5 %all_to_all.48 = bf16[16,16,256]{2,1,0:T(8,128)(2,1)S(1)} all-to-all(bf16[16,16,256]{2,1,0:T(8,128)(2,1)S(1)} %shard_map.96), channel_id=1, replica_groups=mesh['zh'=2,'y'=4,'zl'=4,'x'=4,'c'=2] {'y','zl'}, dimensions={0} | all-to-all | bytes 262144 | tf_op jit(solution)/shard_map/all_to_all | solution.py:43
  55.4 1.9 %collective-permute-start.8 = (bf16[4,4,16,256]{3,2,1,0:T(8,128)(2,1)S(1)}, bf16[4,4,16,256]{3,2,1,0:T(8,128)(2,1)S(1)}, u32[]{:S(2)}, u32[]{:S(2)}) collective-permute-start(bf16[4,4,16,256]{3,2,1,0:T(8,128)(2,1)S(1)} %bitcast.12), channel_id=1, source_target_pairs={{0,1},{1,0},{2,3},{3,2},{4,5},{5,4},{6,7},{7,6},{8,9},{9,8},{10,11... | collective-permute-start | bytes 393224 | tf_op jit(solution)/shard_map/ppermute | solution.py:320
  59.4 4.1 %shard_map.97 = (bf16[2048,256]{1,0:T(8,128)(2,1)S(1)}, bf16[4,2048,512]{2,1,0:T(8,128)(2,1)S(1)}) custom-call(s32[4]{0:T(128)S(1)} %pad_add_fusion.at_ref, bf16[2048,128]{1,0:T(8,128)(2,1)S(1)} %copy-done.7, bf16[8192,128]{1,0:T(8,128)(2,1)S(1)} %copy-done.6), custom_call_target="tpu_custom_call" | custom-call | flops 4000000000 | tf_op jit(solution)/shard_map/pallas_call | solution.py:27
  64.6 1.9 %collective-permute-start.5 = (bf16[4,4,16,256]{3,2,1,0:T(8,128)(2,1)S(1)}, bf16[4,4,16,256]{3,2,1,0:T(8,128)(2,1)S(1)}, u32[]{:S(2)}, u32[]{:S(2)}) collective-permute-start(bf16[4,4,16,256]{3,2,1,0:T(8,128)(2,1)S(1)} %collective-permute-done.4.v_ref), channel_id=1, source_target_pairs={{0,1},{1,0},{2,3},{3,2},{4,5},{5,4},{6,7},{7,6},{8,9},{9,8},{10,11... | collective-permute-start | bytes 393224 | tf_op jit(solution)/shard_map/ppermute | solution.py:320
  68.5 5.5 %shard_map.98 = (bf16[4,2048,512]{2,1,0:T(8,128)(2,1)S(1)}, f32[2048,64]{1,0:T(8,128)S(1)}) custom-call(s32[4]{0:T(128)S(1)} %pad_add_fusion.at_ref, bf16[2048,256]{1,0:T(8,128)(2,1)S(1)} %get-tuple-element.29.pa_ref, bf16[8192,128]{1,0:T(8,128)(2,1)S(1)} %copy-done.6, bf16[4,4,16,256]{3,2,1,0:T(8,128)(2,1)S(1)} %bitcast.16, ...), custom_call_target="tpu_custom_call" | custom-call | flops 4000000000 | tf_op jit(solution)/shard_map/pallas_call | solution.py:27
  74.0 5.6 %shard_map.99 = (bf16[4,2048,512]{2,1,0:T(8,128)(2,1)S(1)}, f32[2048,64]{1,0:T(8,128)S(1)}) custom-call(s32[4]{0:T(128)S(1)} %pad_add_fusion.at_ref, bf16[2048,256]{1,0:T(8,128)(2,1)S(1)} %get-tuple-element.29.pa_ref, bf16[8192,128]{1,0:T(8,128)(2,1)S(1)} %copy-done.6, bf16[4,4,16,256]{3,2,1,0:T(8,128)(2,1)S(1)} %collective-permute-done.6.v_ref, ...), custom_call_target="tpu_custom_call" | custom-call | flops 4000000000 | tf_op jit(solution)/shard_map/pallas_call | solution.py:27
  79.6 5.6 %shard_map.100 = (bf16[4,2048,512]{2,1,0:T(8,128)(2,1)S(1)}, f32[2048,64]{1,0:T(8,128)S(1)}) custom-call(s32[4]{0:T(128)S(1)} %pad_add_fusion.at_ref, bf16[2048,256]{1,0:T(8,128)(2,1)S(1)} %get-tuple-element.29.pa_ref, bf16[8192,128]{1,0:T(8,128)(2,1)S(1)} %copy-done.6, bf16[4,4,16,256]{3,2,1,0:T(8,128)(2,1)S(1)} %collective-permute-done.4.v_ref, ...), custom_call_target="tpu_custom_call" | custom-call | flops 4000000000 | tf_op jit(solution)/shard_map/pallas_call | solution.py:27
  85.3 3.0 %shard_map.101.fit_ref = bf16[64,2048]{1,0:T(8,128)(2,1)S(1)} custom-call(bf16[4,4,16,256]{3,2,1,0:T(8,128)(2,1)S(1)} %collective-permute-done.2.v_ref, bf16[4,4,16,256]{3,2,1,0:T(8,128)(2,1)S(1)} %collective-permute-done.3.u_ref, bf16[4,2048,512]{2,1,0:T(8,128)(2,1)S(1)} %get-tuple-element.35.k_ref, f32[2048,64]{1,0:T(8,128)S(1)} %get-tuple-element.36.old_ref), custom_call_target="tpu_custom_call" | custom-call | flops 2000000000 | tf_op jit(solution)/shard_map/pallas_call | solution.py:27
  99.1 2.2 %collective-permute-done.15.e_ref = bf16[2,4,4,8,256]{4,3,2,1,0:T(8,128)(2,1)S(1)} collective-permute-done((bf16[2,4,4,8,256]{4,3,2,1,0:T(8,128)(2,1)S(1)}, bf16[2,4,4,8,256]{4,3,2,1,0:T(8,128)(2,1)S(1)}, u32[]{:S(2)}, u32[]{:S(2)}) %collective-permute-start.15) | collective-permute-done | bytes 131104 | tf_op jit(solution)/shard_map/ppermute | solution.py:326
  102.9 2.4 %collective-permute-done.11.c_ref = bf16[2,4,4,8,256]{4,3,2,1,0:T(8,128)(2,1)S(1)} collective-permute-done((bf16[2,4,4,8,256]{4,3,2,1,0:T(8,128)(2,1)S(1)}, bf16[2,4,4,8,256]{4,3,2,1,0:T(8,128)(2,1)S(1)}, u32[]{:S(2)}, u32[]{:S(2)}) %collective-permute-start.11) | collective-permute-done | bytes 131104 | tf_op jit(solution)/shard_map/ppermute | solution.py:326
  105.4 16.2 %all_to_all.49.x_ref = bf16[32,8,256]{2,1,0:T(8,128)(2,1)S(1)} all-to-all(bf16[32,8,256]{2,1,0:T(8,128)(2,1)S(1)} %bitcast.10), channel_id=1, replica_groups=mesh['zh'=2,'y'=4,'zl'=4,'x'=4,'c'=2] {'zh','y','zl'}, dimensions={0} | all-to-all | bytes 262144 | tf_op jit(solution)/shard_map/all_to_all | solution.py:43
  122.8 3.0 %collective-permute-start.16 = (f32[16,8,256]{2,1,0:T(8,128)S(1)}, f32[16,8,256]{2,1,0:T(8,128)S(1)}, u32[]{:S(2)}, u32[]{:S(2)}) collective-permute-start(f32[16,8,256]{2,1,0:T(8,128)S(1)} %get-tuple-element.46), channel_id=1, source_target_pairs={{0,1},{1,0},{2,3},{3,2},{4,5},{5,4},{6,7},{7,6},{8,9},{9,8},{10,11... | collective-permute-start | bytes 393224 | tf_op jit(solution)/shard_map/ppermute | solution.py:320
  126.7 10.6 %all_to_all.50.x_ref = f32[16,8,256]{2,1,0:T(8,128)S(1)} all-to-all(f32[16,8,256]{2,1,0:T(8,128)S(1)} %shard_map.111), channel_id=1, replica_groups=mesh['zh'=2,'y'=4,'zl'=4,'x'=4,'c'=2] {'zl','x'}, dimensions={0} | all-to-all | bytes 262144 | tf_op jit(solution)/shard_map/all_to_all | solution.py:43
  138.5 1.8 %collective-permute-start.17 = (f32[16,8,384]{2,1,0:T(8,128)S(1)}, f32[16,8,384]{2,1,0:T(8,128)S(1)}, u32[]{:S(2)}, u32[]{:S(2)}) collective-permute-start(f32[16,8,384]{2,1,0:T(8,128)S(1)} %get-tuple-element.50), channel_id=1, source_target_pairs={{0,1},{1,0},{2,3},{3,2},{4,5},{5,4},{6,7},{7,6},{8,9},{9,8},{10,11... | collective-permute-start | bytes 589832 | tf_op jit(solution)/shard_map/ppermute | solution.py:320
  141.4 11.5 %all_to_all.51.x_ref = f32[16,8,384]{2,1,0:T(8,128)S(1)} all-to-all(f32[16,8,384]{2,1,0:T(8,128)S(1)} %shard_map.113), channel_id=1, replica_groups=mesh['zh'=2,'y'=4,'zl'=4,'x'=4,'c'=2] {'zl','x'}, dimensions={0} | all-to-all | bytes 393216 | tf_op jit(solution)/shard_map/all_to_all | solution.py:43
  154.3 6.8 %all-to-all-start.6 = ((f32[64,1,128]{2,1,0:T(1,128)}), f32[64,1,128]{2,1,0:T(1,128)S(1)}, u32[]{:S(2)}, u32[]{:S(2)}) async-start(f32[64,1,128]{2,1,0:T(1,128)} %bitcast.7), calls=%async_computation.6 | async-start | bytes 65536 | tf_op jit(solution)/shard_map/all_to_all | solution.py:43
  161.1 5.5 %collective-permute-start.18 = (f32[8,384]{1,0:T(8,128)S(1)}, f32[8,384]{1,0:T(8,128)S(1)}, u32[]{:S(2)}, u32[]{:S(2)}) collective-permute-start(f32[8,384]{1,0:T(8,128)S(1)} %get-tuple-element.52.keep_ref), channel_id=1, source_target_pairs={{0,128},{128,0},{1,129},{129,1},{2,130},{130,2},{3,131},{131,3},{4... | collective-permute-start | bytes 36872 | tf_op jit(solution)/shard_map/ppermute | solution.py:408
  168.0 2.5 %all-to-all-done.6 = f32[64,1,128]{2,1,0:T(1,128)S(1)} async-done(((f32[64,1,128]{2,1,0:T(1,128)}), f32[64,1,128]{2,1,0:T(1,128)S(1)}, u32[]{:S(2)}, u32[]{:S(2)}) %all-to-all-start.6) | async-done | bytes 32800 | tf_op jit(solution)/shard_map/all_to_all | solution.py:43
  171.3 7.0 %all_to_all.52.x_ref = f32[4,2,8,384]{3,2,1,0:T(8,128)S(1)} all-to-all(f32[4,2,8,384]{3,2,1,0:T(8,128)S(1)} %shard_map.115), channel_id=1, replica_groups=mesh['zh'=2,'y'=4,'zl'=4,'x'=4,'c'=2] {'y'}, dimensions={0} | all-to-all | bytes 196608 | tf_op jit(solution)/shard_map/all_to_all | solution.py:43
  (63 shorter events, 32.0 us)
Async XLA Ops:
  1.7 57.7 %copy-start.6 = (bf16[8192,128]{1,0:T(8,128)(2,1)S(1)}, bf16[8192,128]{1,0:T(8,128)(2,1)}, u32[]{:S(2)}) copy-start(bf16[8192,128]{1,0:T(8,128)(2,1)} %cen_ref.7) | copy-start | bytes 6291460
  1.7 57.7 %copy-start.7 = (bf16[2048,128]{1,0:T(8,128)(2,1)S(1)}, bf16[2048,128]{1,0:T(8,128)(2,1)}, u32[]{:S(2)}) copy-start(bf16[2048,128]{1,0:T(8,128)(2,1)} %p_ref.1) | copy-start | bytes 1572868
  20.8 3.2 %collective-permute-start = (bf16[16,32,256]{2,1,0:T(8,128)(2,1)S(1)}, bf16[16,32,256]{2,1,0:T(8,128)(2,1)S(1)}, u32[]{:S(2)}, u32[]{:S(2)}) collective-permute-start(bf16[16,32,256]{2,1,0:T(8,128)(2,1)S(1)} %all_to_all.46.x_ref), channel_id=1, source_target_pairs={{0,1},{1,0},{2,3},{3,2},{4,5},{5,4},{6,7},{7,6},{8,9},{9,8},{10,11... | collective-permute-start | bytes 786440 | tf_op jit(solution)/shard_map/ppermute | solution.py:320
  39.3 2.8 %collective-permute-start.1 = (bf16[16,16,256]{2,1,0:T(8,128)(2,1)S(1)}, bf16[16,16,256]{2,1,0:T(8,128)(2,1)S(1)}, u32[]{:S(2)}, u32[]{:S(2)}) collective-permute-start(bf16[16,16,256]{2,1,0:T(8,128)(2,1)S(1)} %all_to_all.47.x_ref), channel_id=1, source_target_pairs={{0,1},{1,0},{2,3},{3,2},{4,5},{5,4},{6,7},{7,6},{8,9},{9,8},{10,11... | collective-permute-start | bytes 393224 | tf_op jit(solution)/shard_map/ppermute | solution.py:320
  55.4 13.1 %collective-permute-start.8 = (bf16[4,4,16,256]{3,2,1,0:T(8,128)(2,1)S(1)}, bf16[4,4,16,256]{3,2,1,0:T(8,128)(2,1)S(1)}, u32[]{:S(2)}, u32[]{:S(2)}) collective-permute-start(bf16[4,4,16,256]{3,2,1,0:T(8,128)(2,1)S(1)} %bitcast.12), channel_id=1, source_target_pairs={{0,1},{1,0},{2,3},{3,2},{4,5},{5,4},{6,7},{7,6},{8,9},{9,8},{10,11... | collective-permute-start | bytes 393224 | tf_op jit(solution)/shard_map/ppermute | solution.py:320
  57.3 6.2 %collective-permute-start.6 = (bf16[4,4,16,256]{3,2,1,0:T(8,128)(2,1)S(1)}, bf16[4,4,16,256]{3,2,1,0:T(8,128)(2,1)S(1)}, u32[]{:S(2)}, u32[]{:S(2)}) collective-permute-start(bf16[4,4,16,256]{3,2,1,0:T(8,128)(2,1)S(1)} %bitcast.13), channel_id=1, source_target_pairs={{2,0},{4,2},{6,4},{0,6},{3,1},{5,3},{7,5},{1,7},{10,8},{12,10},{14... | collective-permute-start | bytes 393224 | tf_op jit(solution)/shard_map/ppermute | solution.py:323
  58.3 6.3 %collective-permute-start.4 = (bf16[4,4,16,256]{3,2,1,0:T(8,128)(2,1)S(1)}, bf16[4,4,16,256]{3,2,1,0:T(8,128)(2,1)S(1)}, u32[]{:S(2)}, u32[]{:S(2)}) collective-permute-start(bf16[4,4,16,256]{3,2,1,0:T(8,128)(2,1)S(1)} %bitcast.14), channel_id=1, source_target_pairs={{4,0},{6,2},{0,4},{2,6},{5,1},{7,3},{1,5},{3,7},{12,8},{14,10},{8,... | collective-permute-start | bytes 393224 | tf_op jit(solution)/shard_map/ppermute | solution.py:323
  59.2 8.8 %collective-permute-start.2 = (bf16[4,4,16,256]{3,2,1,0:T(8,128)(2,1)S(1)}, bf16[4,4,16,256]{3,2,1,0:T(8,128)(2,1)S(1)}, u32[]{:S(2)}, u32[]{:S(2)}) collective-permute-start(bf16[4,4,16,256]{3,2,1,0:T(8,128)(2,1)S(1)} %bitcast.15), channel_id=1, source_target_pairs={{6,0},{0,2},{2,4},{4,6},{7,1},{1,3},{3,5},{5,7},{14,8},{8,10},{10,... | collective-permute-start | bytes 393224 | tf_op jit(solution)/shard_map/ppermute | solution.py:323
  63.5 10.5 %collective-permute-start.7 = (bf16[4,4,16,256]{3,2,1,0:T(8,128)(2,1)S(1)}, bf16[4,4,16,256]{3,2,1,0:T(8,128)(2,1)S(1)}, u32[]{:S(2)}, u32[]{:S(2)}) collective-permute-start(bf16[4,4,16,256]{3,2,1,0:T(8,128)(2,1)S(1)} %collective-permute-done.6.v_ref), channel_id=1, source_target_pairs={{0,1},{1,0},{2,3},{3,2},{4,5},{5,4},{6,7},{7,6},{8,9},{9,8},{10,11... | collective-permute-start | bytes 393224 | tf_op jit(solution)/shard_map/ppermute | solution.py:320
  64.6 15.1 %collective-permute-start.5 = (bf16[4,4,16,256]{3,2,1,0:T(8,128)(2,1)S(1)}, bf16[4,4,16,256]{3,2,1,0:T(8,128)(2,1)S(1)}, u32[]{:S(2)}, u32[]{:S(2)}) collective-permute-start(bf16[4,4,16,256]{3,2,1,0:T(8,128)(2,1)S(1)} %collective-permute-done.4.v_ref), channel_id=1, source_target_pairs={{0,1},{1,0},{2,3},{3,2},{4,5},{5,4},{6,7},{7,6},{8,9},{9,8},{10,11... | collective-permute-start | bytes 393224 | tf_op jit(solution)/shard_map/ppermute | solution.py:320
  68.0 17.2 %collective-permute-start.3 = (bf16[4,4,16,256]{3,2,1,0:T(8,128)(2,1)S(1)}, bf16[4,4,16,256]{3,2,1,0:T(8,128)(2,1)S(1)}, u32[]{:S(2)}, u32[]{:S(2)}) collective-permute-start(bf16[4,4,16,256]{3,2,1,0:T(8,128)(2,1)S(1)} %collective-permute-done.2.v_ref), channel_id=1, source_target_pairs={{0,1},{1,0},{2,3},{3,2},{4,5},{5,4},{6,7},{7,6},{8,9},{9,8},{10,11... | collective-permute-start | bytes 393224 | tf_op jit(solution)/shard_map/ppermute | solution.py:320
  93.5 3.0 %collective-permute-start.14 = (f32[2,4,4,8,256]{4,3,2,1,0:T(8,128)S(1)}, f32[2,4,4,8,256]{4,3,2,1,0:T(8,128)S(1)}, u32[]{:S(2)}, u32[]{:S(2)}) collective-permute-start(f32[2,4,4,8,256]{4,3,2,1,0:T(8,128)S(1)} %get-tuple-element.44), channel_id=1, source_target_pairs={{0,1},{1,0},{2,3},{3,2},{4,5},{5,4},{6,7},{7,6},{8,9},{9,8},{10,11... | collective-permute-start | bytes 786440 | tf_op jit(solution)/shard_map/ppermute | solution.py:320
  93.6 3.2 %collective-permute-start.12 = (f32[2,4,4,8,256]{4,3,2,1,0:T(8,128)S(1)}, f32[2,4,4,8,256]{4,3,2,1,0:T(8,128)S(1)}, u32[]{:S(2)}, u32[]{:S(2)}) collective-permute-start(f32[2,4,4,8,256]{4,3,2,1,0:T(8,128)S(1)} %get-tuple-element.42), channel_id=1, source_target_pairs={{0,1},{1,0},{2,3},{3,2},{4,5},{5,4},{6,7},{7,6},{8,9},{9,8},{10,11... | collective-permute-start | bytes 786440 | tf_op jit(solution)/shard_map/ppermute | solution.py:320
  94.1 4.0 %collective-permute-start.10 = (f32[2,4,4,8,256]{4,3,2,1,0:T(8,128)S(1)}, f32[2,4,4,8,256]{4,3,2,1,0:T(8,128)S(1)}, u32[]{:S(2)}, u32[]{:S(2)}) collective-permute-start(f32[2,4,4,8,256]{4,3,2,1,0:T(8,128)S(1)} %get-tuple-element.40), channel_id=1, source_target_pairs={{0,1},{1,0},{2,3},{3,2},{4,5},{5,4},{6,7},{7,6},{8,9},{9,8},{10,11... | collective-permute-start | bytes 786440 | tf_op jit(solution)/shard_map/ppermute | solution.py:320
  96.0 82.3 %copy-start.4 = (f32[64,256]{1,0:T(8,128)S(1)}, f32[64,256]{1,0:T(8,128)}, u32[]{:S(2)}) copy-start(f32[64,256]{1,0:T(8,128)} %d_ref.3) | copy-start | bytes 196612
  96.0 82.3 %copy-start.5 = (f32[64,256]{1,0:T(8,128)S(1)}, f32[64,256]{1,0:T(8,128)}, u32[]{:S(2)}) copy-start(f32[64,256]{1,0:T(8,128)} %it_ref.1) | copy-start | bytes 196612
  96.0 3.1 %collective-permute-start.9 = (f32[2,4,4,8,256]{4,3,2,1,0:T(8,128)S(1)}, f32[2,4,4,8,256]{4,3,2,1,0:T(8,128)S(1)}, u32[]{:S(2)}, u32[]{:S(2)}) collective-permute-start(f32[2,4,4,8,256]{4,3,2,1,0:T(8,128)S(1)} %get-tuple-element.38), channel_id=1, source_target_pairs={{0,1},{1,0},{2,3},{3,2},{4,5},{5,4},{6,7},{7,6},{8,9},{9,8},{10,11... | collective-permute-start | bytes 786440 | tf_op jit(solution)/shard_map/ppermute | solution.py:320
  96.4 4.9 %collective-permute-start.15 = (bf16[2,4,4,8,256]{4,3,2,1,0:T(8,128)(2,1)S(1)}, bf16[2,4,4,8,256]{4,3,2,1,0:T(8,128)(2,1)S(1)}, u32[]{:S(2)}, u32[]{:S(2)}) collective-permute-start(bf16[2,4,4,8,256]{4,3,2,1,0:T(8,128)(2,1)S(1)} %shard_map.108), channel_id=1, source_target_pairs={{0,6},{2,0},{4,2},{6,4},{1,7},{3,1},{5,3},{7,5},{8,14},{10,8},{12,... | collective-permute-start | bytes 393224 | tf_op jit(solution)/shard_map/ppermute | solution.py:326
  96.8 6.1 %collective-permute-start.13 = (bf16[2,4,4,8,256]{4,3,2,1,0:T(8,128)(2,1)S(1)}, bf16[2,4,4,8,256]{4,3,2,1,0:T(8,128)(2,1)S(1)}, u32[]{:S(2)}, u32[]{:S(2)}) collective-permute-start(bf16[2,4,4,8,256]{4,3,2,1,0:T(8,128)(2,1)S(1)} %shard_map.106), channel_id=1, source_target_pairs={{0,2},{2,4},{4,6},{6,0},{1,3},{3,5},{5,7},{7,1},{8,10},{10,12},{12... | collective-permute-start | bytes 393224 | tf_op jit(solution)/shard_map/ppermute | solution.py:326
  98.1 7.2 %collective-permute-start.11 = (bf16[2,4,4,8,256]{4,3,2,1,0:T(8,128)(2,1)S(1)}, bf16[2,4,4,8,256]{4,3,2,1,0:T(8,128)(2,1)S(1)}, u32[]{:S(2)}, u32[]{:S(2)}) collective-permute-start(bf16[2,4,4,8,256]{4,3,2,1,0:T(8,128)(2,1)S(1)} %shard_map.104), channel_id=1, source_target_pairs={{0,4},{2,6},{4,0},{6,2},{1,5},{3,7},{5,1},{7,3},{8,12},{10,14},{12... | collective-permute-start | bytes 393224 | tf_op jit(solution)/shard_map/ppermute | solution.py:326
  122.8 4.0 %collective-permute-start.16 = (f32[16,8,256]{2,1,0:T(8,128)S(1)}, f32[16,8,256]{2,1,0:T(8,128)S(1)}, u32[]{:S(2)}, u32[]{:S(2)}) collective-permute-start(f32[16,8,256]{2,1,0:T(8,128)S(1)} %get-tuple-element.46), channel_id=1, source_target_pairs={{0,1},{1,0},{2,3},{3,2},{4,5},{5,4},{6,7},{7,6},{8,9},{9,8},{10,11... | collective-permute-start | bytes 393224 | tf_op jit(solution)/shard_map/ppermute | solution.py:320
  138.5 2.9 %collective-permute-start.17 = (f32[16,8,384]{2,1,0:T(8,128)S(1)}, f32[16,8,384]{2,1,0:T(8,128)S(1)}, u32[]{:S(2)}, u32[]{:S(2)}) collective-permute-start(f32[16,8,384]{2,1,0:T(8,128)S(1)} %get-tuple-element.50), channel_id=1, source_target_pairs={{0,1},{1,0},{2,3},{3,2},{4,5},{5,4},{6,7},{7,6},{8,9},{9,8},{10,11... | collective-permute-start | bytes 589832 | tf_op jit(solution)/shard_map/ppermute | solution.py:320
  154.3 16.2 %all-to-all-start.6 = ((f32[64,1,128]{2,1,0:T(1,128)}), f32[64,1,128]{2,1,0:T(1,128)S(1)}, u32[]{:S(2)}, u32[]{:S(2)}) async-start(f32[64,1,128]{2,1,0:T(1,128)} %bitcast.7), calls=%async_computation.6 | async-start | bytes 65536 | tf_op jit(solution)/shard_map/all_to_all | solution.py:43
  161.1 6.9 %collective-permute-start.18 = (f32[8,384]{1,0:T(8,128)S(1)}, f32[8,384]{1,0:T(8,128)S(1)}, u32[]{:S(2)}, u32[]{:S(2)}) collective-permute-start(f32[8,384]{1,0:T(8,128)S(1)} %get-tuple-element.52.keep_ref), channel_id=1, source_target_pairs={{0,128},{128,0},{1,129},{129,1},{2,130},{130,2},{3,131},{131,3},{4... | collective-permute-start | bytes 36872 | tf_op jit(solution)/shard_map/ppermute | solution.py:408
  (4 other events, 129.0 us)

commit v6 on v5

--- a/solution.py
+++ b/solution.py
@@ -12,7 +12,6 @@
 LINE = ("zl", "x")
 SIDE = ("y", "zl")
 FACE = ("zh", "y", "zl")
-HALVES = ("zh", "zl", "x", "c")
 ALL = ("zh", "y") + ROW
 SWAP = [(0, 1), (1, 0)]
 LOG2E = 1.4426950408889634
@@ -89,12 +88,14 @@
         )
         for q in range(parts)
     ]
-    for copy in copies:
+    for copy in copies[:2]:
         copy.start()
     acc = None
     count = x_ref.shape[0] // parts
     for q in range(parts):
         copies[q].wait()
+        if q + 2 < parts:
+            copies[q + 2].start()
         for z in range(q * count, q * count + count):
             for which, ref in ((0, x_ref), (1, y_ref)):
                 part = lax.dot_general(
@@ -129,7 +130,7 @@
     step = 256
 
     def load(i, slot):
-        z = i * 4 + (at_ref[2] + shift) % 4
+        z = i * 4 + (at_ref[2] ^ shift)
         for h in range(2):
             cols = slice(h * 256, h * 256 + 256)
             block = cen_ref[columns(at_ref, z, h), :]
@@ -285,30 +286,26 @@
     out_ref[...] = jnp.broadcast_to(row, out_ref.shape)
 
 
-def beta_body(at_ref, x_ref, keep_ref, far_ref, out_ref):
+def beta_body(x_ref, keep_ref, out_ref):
     lane = lax.broadcasted_iota(jnp.int32, (8, 128), 1)
-    half = x_ref.shape[0] // 2
-    for which, ref in ((0, keep_ref), (1, far_ref)):
-        zh = at_ref[3] if which == 0 else 1 - at_ref[3]
-        rows = x_ref[pl.ds(pl.multiple_of(zh * half, half), half), :]
-        row = jnp.sum(rows, axis=0, keepdims=True)
-        total = jnp.sum(jnp.where(diagonal(), row, 0.0), axis=1, keepdims=True)
-        extra = ref[:, 256:]
-        extra = jnp.where(lane == 0, extra, total / extra[:, 1:2])
-        for r in range(out_ref.shape[0]):
-            out_ref[r, zh, :, :256] = ref[:, :256]
-            out_ref[r, zh, :, 256:] = extra
+    row = jnp.sum(x_ref[...], axis=0, keepdims=True)
+    total = jnp.sum(jnp.where(diagonal(), row, 0.0), axis=1, keepdims=True)
+    extra = keep_ref[:, 256:]
+    extra = jnp.where(lane == 0, extra, total / extra[:, 1:2])
+    for r in range(out_ref.shape[0]):
+        out_ref[r, :, :256] = keep_ref[:, :256]
+        out_ref[r, :, 256:] = extra
 
 
 def final_body(x_ref, it_ref, d_ref, ni_ref, nr_ref, nd_ref):
     for g in range(x_ref.shape[0]):
-        for h in range(2):
-            rows = slice(g * 16 + h * 8, g * 16 + h * 8 + 8)
-            new = x_ref[g, h, :, :256]
-            d = d_ref[rows, :]
-            ni_ref[rows, :] = it_ref[rows, :] + x_ref[g, h, :, 256:257] * d
-            nr_ref[rows, :] = new
-            nd_ref[rows, :] = new + x_ref[g, h, :, 257:258] * d
+        start = (g % 4) * 16 + (g // 4) * 8
+        rows = slice(start, start + 8)
+        new = x_ref[g, :, :256]
+        d = d_ref[rows, :]
+        ni_ref[rows, :] = it_ref[rows, :] + x_ref[g, :, 256:257] * d
+        nr_ref[rows, :] = new
+        nd_ref[rows, :] = new + x_ref[g, :, 257:258] * d
 
 
 def iteration(points, centers, inner_factor, outer_factor, iterate, residual, direction):
@@ -319,11 +316,8 @@
     def swap(v):
         return lax.ppermute(v, "c", SWAP)
 
-    def fetch(v, k):
-        return lax.ppermute(v, "x", [((i + k) % 4, i) for i in range(4)])
-
-    def send(v, k):
-        return lax.ppermute(v, "x", [(i, (i + k) % 4) for i in range(4)])
+    def across(v, k):
+        return lax.ppermute(v, "x", [(i, i ^ k) for i in range(4)])
 
     x = call(prep_body, sds((16, 32, 256), bf16), (at, direction), [SM, VM])
     x = exchange(x, LINE)
@@ -332,12 +326,12 @@
         (sds((16, 256), f32), sds((16, 256), f32), sds((16, 16, 256), bf16)),
         (at, x, swap(x), pltpu.with_memory_space_constraint(inner_factor, pltpu.HBM)),
         [SM, VM, VM, pl.BlockSpec(memory_space=pltpu.HBM)],
-        scratch=[pltpu.VMEM(inner_factor.shape, bf16), pltpu.SemaphoreType.DMA((4,))],
+        scratch=[pltpu.VMEM(inner_factor.shape, bf16), pltpu.SemaphoreType.DMA((8,))],
     )
     x = exchange(x, LINE)
     x = call(outer_body, sds((16, 16, 256), bf16), (at, x, swap(x), outer_factor), [SM] + [VM] * 3)
     v = exchange(x, SIDE).reshape(4, 4, 16, 256)
-    vs = [v] + [fetch(v, k) for k in (1, 2, 3)]
+    vs = [v] + [across(v, k) for k in (1, 2, 3)]
     us = [swap(v) for v in vs]
     kernel = sds((4, here, 512), bf16)
     sums = sds((here, 64), f32)
@@ -383,7 +377,7 @@
         other = swap(other)
         if k:
             x = call(add_body, sds(block.shape, bf16), (own, other))
-            got.append(send(x, k))
+            got.append(across(x, k))
     x = call(gather_body, sds(block.shape, bf16), (own, other, *got))
     x = exchange(x.reshape(32, 8, 256), FACE)
     own, other = call(
@@ -403,12 +397,11 @@
     x = call(add_body, sds((16, 8, 384), f32), (own, swap(other)))
     x = exchange(x, LINE)
     keep, x = call(
-        step_body, (sds((8, 384), f32), sds((64, 128), f32)), (at, x, residual), [SM, VM, VM]
-    )
-    far = lax.ppermute(keep, "zh", SWAP)
-    x = exchange(x, HALVES)
-    x = call(beta_body, sds((4, 2, 8, 384), f32), (at, x, keep, far), [SM, VM, VM, VM])
-    x = exchange(x, ("y",))
+        step_body, (sds((8, 384), f32), sds((32, 128), f32)), (at, x, residual), [SM, VM, VM]
+    )
+    x = exchange(x, ROW)
+    x = call(beta_body, sds((8, 8, 384), f32), (x, keep))
+    x = exchange(x, ("zh", "y"))
     out = sds((64, 256), f32)
     return call(final_body, (out, out, out), (x, iterate, direction))
 

time: 179 us -> 184 us (1.028)
  blocking collectives: 86.4 us -> 106 us
  starting transfers between devices: 32 us -> 21.9 us
  waiting for transfers between devices: 16.1 us -> 11.6 us
    all_to_all x7 -> x8, blocking collectives: 86.4 us -> 106 us  [exchange(): return lax.all_to_all(v, axes, 0, 0, tiled=True)]
    all_to_all x1 -> x0, starting transfers between devices: 6.79 us -> none  [exchange(): return lax.all_to_all(v, axes, 0, 0, tiled=True)]
    all_to_all x1 -> x0, waiting for transfers between devices: 2.54 us -> none  [exchange(): return lax.all_to_all(v, axes, 0, 0, tiled=True)]
    ppermute x7 -> x6, starting transfers between devices: 10.2 us -> 7.96 us  [across(): return lax.ppermute(v, 'x', [(i, i ^ k) for i in range(4)])]
    ppermute x7 -> x6, waiting for transfers between devices: 9.29 us -> 7.41 us  [across(): return lax.ppermute(v, 'x', [(i, i ^ k) for i in range(4)])]
  transfers between devices with their start and end apart: 20 -> 18, of which waited for: 11 -> 8; matrix products, arithmetic and copies ran while one was open for 0% -> 0% of each run, Pallas kernels for 13% -> 12%
where the time goes in v6:
time: 184 us
  blocking collectives  106 us (58%)
  Pallas kernels  42.8 us (23%)
  starting transfers between devices  21.9 us (12%)
  waiting for transfers between devices  11.6 us (6%)
    all_to_all x8, blocking collectives, exchange(): return lax.all_to_all(v, axes, 0, 0, tiled=True)  106 us
    pallas_call x23, Pallas kernels, call(): pl.pallas_call(body, out_shape=outs, in_specs=specs or [VM] * len(args),...  42.8 us
    ppermute x12, starting transfers between devices, swap(): return lax.ppermute(v, 'c', SWAP)  13.9 us
    ppermute x6, starting transfers between devices, across(): return lax.ppermute(v, 'x', [(i, i ^ k) for i in range(4)])  7.96 us
    ppermute x6, waiting for transfers between devices, across(): return lax.ppermute(v, 'x', [(i, i ^ k) for i in range(4)])  7.41 us
    ppermute x12, waiting for transfers between devices, swap(): return lax.ppermute(v, 'c', SWAP)  4.23 us
  transfers between devices with their start and end apart: 18, of which 8 were waited for; matrix products, arithmetic and copies ran while one was open for 0% of the time, Pallas kernels for 12%

profile of v6, /device:TPU:1, one launch (start us, length us, event | category | flops | bytes accessed | tf_op | source)
XLA Modules:
  0.0 183.8 jit_solution(641313976514658927)
XLA Ops:
  2.3 18.5 %all_to_all.46.x_ref = bf16[16,32,256]{2,1,0:T(8,128)(2,1)S(1)} all-to-all(bf16[16,32,256]{2,1,0:T(8,128)(2,1)S(1)} %shard_map.94), channel_id=1, replica_groups=mesh['zh'=2,'y'=4,'zl'=4,'x'=4,'c'=2] {'zl','x'}, dimensions={0} | all-to-all | bytes 524288 | tf_op jit(solution)/shard_map/all_to_all | solution.py:42
  20.8 2.1 %collective-permute-start = (bf16[16,32,256]{2,1,0:T(8,128)(2,1)S(1)}, bf16[16,32,256]{2,1,0:T(8,128)(2,1)S(1)}, u32[]{:S(2)}, u32[]{:S(2)}) collective-permute-start(bf16[16,32,256]{2,1,0:T(8,128)(2,1)S(1)} %all_to_all.46.x_ref), channel_id=1, source_target_pairs={{0,1},{1,0},{2,3},{3,2},{4,5},{5,4},{6,7},{7,6},{8,9},{9,8},{10,11... | collective-permute-start | bytes 786440 | tf_op jit(solution)/shard_map/ppermute | solution.py:317
  24.0 5.6 %shard_map.95 = (f32[16,256]{1,0:T(8,128)S(1)}, f32[16,256]{1,0:T(8,128)S(1)}, bf16[16,16,256]{2,1,0:T(8,128)(2,1)S(1)}) custom-call(s32[4]{0:T(128)S(1)} %pad_add_fusion.at_ref, bf16[16,32,256]{2,1,0:T(8,128)(2,1)S(1)} %all_to_all.46.x_ref, bf16[16,32,256]{2,1,0:T(8,128)(2,1)S(1)} %collective-permute-done.y_ref, bf16[256,8192]{1,0:T(8,128)(2,1)} %f_ref.5), custom_call_target="tpu_custom_call" | custom-call | tf_op jit(solution)/shard_map/pallas_call | solution.py:26
  29.6 11.1 %all_to_all.47.x_ref = bf16[16,16,256]{2,1,0:T(8,128)(2,1)S(1)} all-to-all(bf16[16,16,256]{2,1,0:T(8,128)(2,1)S(1)} %get-tuple-element.28), channel_id=1, replica_groups=mesh['zh'=2,'y'=4,'zl'=4,'x'=4,'c'=2] {'zl','x'}, dimensions={0} | all-to-all | bytes 262144 | tf_op jit(solution)/shard_map/all_to_all | solution.py:42
  40.7 1.8 collective-permute-start.1
  45.2 11.5 %all_to_all.48 = bf16[16,16,256]{2,1,0:T(8,128)(2,1)S(1)} all-to-all(bf16[16,16,256]{2,1,0:T(8,128)(2,1)S(1)} %shard_map.96), channel_id=1, replica_groups=mesh['zh'=2,'y'=4,'zl'=4,'x'=4,'c'=2] {'y','zl'}, dimensions={0} | all-to-all | bytes 262144 | tf_op jit(solution)/shard_map/all_to_all | solution.py:42
  56.7 1.9 %collective-permute-start.8 = (bf16[4,4,16,256]{3,2,1,0:T(8,128)(2,1)S(1)}, bf16[4,4,16,256]{3,2,1,0:T(8,128)(2,1)S(1)}, u32[]{:S(2)}, u32[]{:S(2)}) collective-permute-start(bf16[4,4,16,256]{3,2,1,0:T(8,128)(2,1)S(1)} %bitcast.11), channel_id=1, source_target_pairs={{0,1},{1,0},{2,3},{3,2},{4,5},{5,4},{6,7},{7,6},{8,9},{9,8},{10,11... | collective-permute-start | bytes 393224 | tf_op jit(solution)/shard_map/ppermute | solution.py:317
  58.7 2.1 %collective-permute-start.4 = (bf16[4,4,16,256]{3,2,1,0:T(8,128)(2,1)S(1)}, bf16[4,4,16,256]{3,2,1,0:T(8,128)(2,1)S(1)}, u32[]{:S(2)}, u32[]{:S(2)}) collective-permute-start(bf16[4,4,16,256]{3,2,1,0:T(8,128)(2,1)S(1)} %bitcast.13), channel_id=1, source_target_pairs={{0,4},{2,6},{4,0},{6,2},{1,5},{3,7},{5,1},{7,3},{8,12},{10,14},{12... | collective-permute-start | bytes 393224 | tf_op jit(solution)/shard_map/ppermute | solution.py:320
  62.5 4.0 %shard_map.97 = (bf16[2048,256]{1,0:T(8,128)(2,1)S(1)}, bf16[4,2048,512]{2,1,0:T(8,128)(2,1)S(1)}) custom-call(s32[4]{0:T(128)S(1)} %pad_add_fusion.at_ref, bf16[2048,128]{1,0:T(8,128)(2,1)S(1)} %copy-done.7, bf16[8192,128]{1,0:T(8,128)(2,1)S(1)} %copy-done.6), custom_call_target="tpu_custom_call" | custom-call | flops 4000000000 | tf_op jit(solution)/shard_map/pallas_call | solution.py:26
  70.6 5.5 %shard_map.98 = (bf16[4,2048,512]{2,1,0:T(8,128)(2,1)S(1)}, f32[2048,64]{1,0:T(8,128)S(1)}) custom-call(s32[4]{0:T(128)S(1)} %pad_add_fusion.at_ref, bf16[2048,256]{1,0:T(8,128)(2,1)S(1)} %get-tuple-element.29.pa_ref, bf16[8192,128]{1,0:T(8,128)(2,1)S(1)} %copy-done.6, bf16[4,4,16,256]{3,2,1,0:T(8,128)(2,1)S(1)} %bitcast.15, ...), custom_call_target="tpu_custom_call" | custom-call | flops 4000000000 | tf_op jit(solution)/shard_map/pallas_call | solution.py:26
  76.1 5.6 %shard_map.99 = (bf16[4,2048,512]{2,1,0:T(8,128)(2,1)S(1)}, f32[2048,64]{1,0:T(8,128)S(1)}) custom-call(s32[4]{0:T(128)S(1)} %pad_add_fusion.at_ref, bf16[2048,256]{1,0:T(8,128)(2,1)S(1)} %get-tuple-element.29.pa_ref, bf16[8192,128]{1,0:T(8,128)(2,1)S(1)} %copy-done.6, bf16[4,4,16,256]{3,2,1,0:T(8,128)(2,1)S(1)} %collective-permute-done.6.v_ref, ...), custom_call_target="tpu_custom_call" | custom-call | flops 4000000000 | tf_op jit(solution)/shard_map/pallas_call | solution.py:26
  81.7 5.6 %shard_map.100 = (bf16[4,2048,512]{2,1,0:T(8,128)(2,1)S(1)}, f32[2048,64]{1,0:T(8,128)S(1)}) custom-call(s32[4]{0:T(128)S(1)} %pad_add_fusion.at_ref, bf16[2048,256]{1,0:T(8,128)(2,1)S(1)} %get-tuple-element.29.pa_ref, bf16[8192,128]{1,0:T(8,128)(2,1)S(1)} %copy-done.6, bf16[4,4,16,256]{3,2,1,0:T(8,128)(2,1)S(1)} %collective-permute-done.4.v_ref, ...), custom_call_target="tpu_custom_call" | custom-call | flops 4000000000 | tf_op jit(solution)/shard_map/pallas_call | solution.py:26
  87.3 3.0 %shard_map.101.fit_ref = bf16[64,2048]{1,0:T(8,128)(2,1)S(1)} custom-call(bf16[4,4,16,256]{3,2,1,0:T(8,128)(2,1)S(1)} %collective-permute-done.2.v_ref, bf16[4,4,16,256]{3,2,1,0:T(8,128)(2,1)S(1)} %collective-permute-done.3.u_ref, bf16[4,2048,512]{2,1,0:T(8,128)(2,1)S(1)} %get-tuple-element.35.k_ref, f32[2048,64]{1,0:T(8,128)S(1)} %get-tuple-element.36.old_ref), custom_call_target="tpu_custom_call" | custom-call | flops 2000000000 | tf_op jit(solution)/shard_map/pallas_call | solution.py:26
  98.5 1.8 collective-permute-start.15
  100.5 2.2 %collective-permute-start.11 = (bf16[2,4,4,8,256]{4,3,2,1,0:T(8,128)(2,1)S(1)}, bf16[2,4,4,8,256]{4,3,2,1,0:T(8,128)(2,1)S(1)}, u32[]{:S(2)}, u32[]{:S(2)}) collective-permute-start(bf16[2,4,4,8,256]{4,3,2,1,0:T(8,128)(2,1)S(1)} %shard_map.104), channel_id=1, source_target_pairs={{0,4},{2,6},{4,0},{6,2},{1,5},{3,7},{5,1},{7,3},{8,12},{10,14},{12... | collective-permute-start | bytes 393224 | tf_op jit(solution)/shard_map/ppermute | solution.py:320
  102.7 2.0 %collective-permute-done.15.e_ref = bf16[2,4,4,8,256]{4,3,2,1,0:T(8,128)(2,1)S(1)} collective-permute-done((bf16[2,4,4,8,256]{4,3,2,1,0:T(8,128)(2,1)S(1)}, bf16[2,4,4,8,256]{4,3,2,1,0:T(8,128)(2,1)S(1)}, u32[]{:S(2)}, u32[]{:S(2)}) %collective-permute-start.15) | collective-permute-done | bytes 131104 | tf_op jit(solution)/shard_map/ppermute | solution.py:320
  105.0 3.5 %collective-permute-done.11.c_ref = bf16[2,4,4,8,256]{4,3,2,1,0:T(8,128)(2,1)S(1)} collective-permute-done((bf16[2,4,4,8,256]{4,3,2,1,0:T(8,128)(2,1)S(1)}, bf16[2,4,4,8,256]{4,3,2,1,0:T(8,128)(2,1)S(1)}, u32[]{:S(2)}, u32[]{:S(2)}) %collective-permute-start.11) | collective-permute-done | bytes 131104 | tf_op jit(solution)/shard_map/ppermute | solution.py:320
  108.6 16.2 %all_to_all.49.x_ref = bf16[32,8,256]{2,1,0:T(8,128)(2,1)S(1)} all-to-all(bf16[32,8,256]{2,1,0:T(8,128)(2,1)S(1)} %bitcast.10), channel_id=1, replica_groups=mesh['zh'=2,'y'=4,'zl'=4,'x'=4,'c'=2] {'zh','y','zl'}, dimensions={0} | all-to-all | bytes 262144 | tf_op jit(solution)/shard_map/all_to_all | solution.py:42
  126.0 2.8 %collective-permute-start.16 = (f32[16,8,256]{2,1,0:T(8,128)S(1)}, f32[16,8,256]{2,1,0:T(8,128)S(1)}, u32[]{:S(2)}, u32[]{:S(2)}) collective-permute-start(f32[16,8,256]{2,1,0:T(8,128)S(1)} %get-tuple-element.46), channel_id=1, source_target_pairs={{0,1},{1,0},{2,3},{3,2},{4,5},{5,4},{6,7},{7,6},{8,9},{9,8},{10,11... | collective-permute-start | bytes 393224 | tf_op jit(solution)/shard_map/ppermute | solution.py:317
  129.7 10.8 %all_to_all.50.x_ref = f32[16,8,256]{2,1,0:T(8,128)S(1)} all-to-all(f32[16,8,256]{2,1,0:T(8,128)S(1)} %shard_map.111), channel_id=1, replica_groups=mesh['zh'=2,'y'=4,'zl'=4,'x'=4,'c'=2] {'zl','x'}, dimensions={0} | all-to-all | bytes 262144 | tf_op jit(solution)/shard_map/all_to_all | solution.py:42
  141.7 1.8 collective-permute-start.17
  144.6 11.5 %all_to_all.51.x_ref = f32[16,8,384]{2,1,0:T(8,128)S(1)} all-to-all(f32[16,8,384]{2,1,0:T(8,128)S(1)} %shard_map.113), channel_id=1, replica_groups=mesh['zh'=2,'y'=4,'zl'=4,'x'=4,'c'=2] {'zl','x'}, dimensions={0} | all-to-all | bytes 393216 | tf_op jit(solution)/shard_map/all_to_all | solution.py:42
  156.9 12.4 %all_to_all.52 = f32[32,1,128]{2,1,0:T(1,128)S(1)} all-to-all(f32[32,1,128]{2,1,0:T(1,128)S(1)} %bitcast.17), channel_id=1, replica_groups=mesh['zh'=2,'y'=4,'zl'=4,'x'=4,'c'=2] {'zl','x','c'}, dimensions={0} | all-to-all | bytes 32768 | tf_op jit(solution)/shard_map/all_to_all | solution.py:42
  169.4 13.7 %all_to_all.53.x_ref = f32[8,8,384]{2,1,0:T(8,128)S(1)} all-to-all(f32[8,8,384]{2,1,0:T(8,128)S(1)} %shard_map.115), channel_id=1, replica_groups=mesh['zh'=2,'y'=4,'zl'=4,'x'=4,'c'=2] {'zh','y'}, dimensions={0} | all-to-all | bytes 196608 | tf_op jit(solution)/shard_map/all_to_all | solution.py:42
  (60 shorter events, 26.2 us)
Async XLA Ops:
  1.7 60.8 %copy-start.6 = (bf16[8192,128]{1,0:T(8,128)(2,1)S(1)}, bf16[8192,128]{1,0:T(8,128)(2,1)}, u32[]{:S(2)}) copy-start(bf16[8192,128]{1,0:T(8,128)(2,1)} %cen_ref.7) | copy-start | bytes 6291460
  1.7 60.8 %copy-start.7 = (bf16[2048,128]{1,0:T(8,128)(2,1)S(1)}, bf16[2048,128]{1,0:T(8,128)(2,1)}, u32[]{:S(2)}) copy-start(bf16[2048,128]{1,0:T(8,128)(2,1)} %p_ref.1) | copy-start | bytes 1572868
  20.8 3.2 %collective-permute-start = (bf16[16,32,256]{2,1,0:T(8,128)(2,1)S(1)}, bf16[16,32,256]{2,1,0:T(8,128)(2,1)S(1)}, u32[]{:S(2)}, u32[]{:S(2)}) collective-permute-start(bf16[16,32,256]{2,1,0:T(8,128)(2,1)S(1)} %all_to_all.46.x_ref), channel_id=1, source_target_pairs={{0,1},{1,0},{2,3},{3,2},{4,5},{5,4},{6,7},{7,6},{8,9},{9,8},{10,11... | collective-permute-start | bytes 786440 | tf_op jit(solution)/shard_map/ppermute | solution.py:317
  40.7 2.8 %collective-permute-start.1 = (bf16[16,16,256]{2,1,0:T(8,128)(2,1)S(1)}, bf16[16,16,256]{2,1,0:T(8,128)(2,1)S(1)}, u32[]{:S(2)}, u32[]{:S(2)}) collective-permute-start(bf16[16,16,256]{2,1,0:T(8,128)(2,1)S(1)} %all_to_all.47.x_ref), channel_id=1, source_target_pairs={{0,1},{1,0},{2,3},{3,2},{4,5},{5,4},{6,7},{7,6},{8,9},{9,8},{10,11... | collective-permute-start | bytes 393224 | tf_op jit(solution)/shard_map/ppermute | solution.py:317
  56.7 13.8 %collective-permute-start.8 = (bf16[4,4,16,256]{3,2,1,0:T(8,128)(2,1)S(1)}, bf16[4,4,16,256]{3,2,1,0:T(8,128)(2,1)S(1)}, u32[]{:S(2)}, u32[]{:S(2)}) collective-permute-start(bf16[4,4,16,256]{3,2,1,0:T(8,128)(2,1)S(1)} %bitcast.11), channel_id=1, source_target_pairs={{0,1},{1,0},{2,3},{3,2},{4,5},{5,4},{6,7},{7,6},{8,9},{9,8},{10,11... | collective-permute-start | bytes 393224 | tf_op jit(solution)/shard_map/ppermute | solution.py:317
  58.6 7.9 %collective-permute-start.6 = (bf16[4,4,16,256]{3,2,1,0:T(8,128)(2,1)S(1)}, bf16[4,4,16,256]{3,2,1,0:T(8,128)(2,1)S(1)}, u32[]{:S(2)}, u32[]{:S(2)}) collective-permute-start(bf16[4,4,16,256]{3,2,1,0:T(8,128)(2,1)S(1)} %bitcast.12), channel_id=1, source_target_pairs={{0,2},{2,0},{4,6},{6,4},{1,3},{3,1},{5,7},{7,5},{8,10},{10,8},{12,... | collective-permute-start | bytes 393224 | tf_op jit(solution)/shard_map/ppermute | solution.py:320
  58.7 8.8 %collective-permute-start.4 = (bf16[4,4,16,256]{3,2,1,0:T(8,128)(2,1)S(1)}, bf16[4,4,16,256]{3,2,1,0:T(8,128)(2,1)S(1)}, u32[]{:S(2)}, u32[]{:S(2)}) collective-permute-start(bf16[4,4,16,256]{3,2,1,0:T(8,128)(2,1)S(1)} %bitcast.13), channel_id=1, source_target_pairs={{0,4},{2,6},{4,0},{6,2},{1,5},{3,7},{5,1},{7,3},{8,12},{10,14},{12... | collective-permute-start | bytes 393224 | tf_op jit(solution)/shard_map/ppermute | solution.py:320
  60.8 9.0 %collective-permute-start.2 = (bf16[4,4,16,256]{3,2,1,0:T(8,128)(2,1)S(1)}, bf16[4,4,16,256]{3,2,1,0:T(8,128)(2,1)S(1)}, u32[]{:S(2)}, u32[]{:S(2)}) collective-permute-start(bf16[4,4,16,256]{3,2,1,0:T(8,128)(2,1)S(1)} %bitcast.14), channel_id=1, source_target_pairs={{0,6},{2,4},{4,2},{6,0},{1,7},{3,5},{5,3},{7,1},{8,14},{10,12},{12... | collective-permute-start | bytes 393224 | tf_op jit(solution)/shard_map/ppermute | solution.py:320
  66.6 9.5 %collective-permute-start.7 = (bf16[4,4,16,256]{3,2,1,0:T(8,128)(2,1)S(1)}, bf16[4,4,16,256]{3,2,1,0:T(8,128)(2,1)S(1)}, u32[]{:S(2)}, u32[]{:S(2)}) collective-permute-start(bf16[4,4,16,256]{3,2,1,0:T(8,128)(2,1)S(1)} %collective-permute-done.6.v_ref), channel_id=1, source_target_pairs={{0,1},{1,0},{2,3},{3,2},{4,5},{5,4},{6,7},{7,6},{8,9},{9,8},{10,11... | collective-permute-start | bytes 393224 | tf_op jit(solution)/shard_map/ppermute | solution.py:317
  67.5 14.2 %collective-permute-start.5 = (bf16[4,4,16,256]{3,2,1,0:T(8,128)(2,1)S(1)}, bf16[4,4,16,256]{3,2,1,0:T(8,128)(2,1)S(1)}, u32[]{:S(2)}, u32[]{:S(2)}) collective-permute-start(bf16[4,4,16,256]{3,2,1,0:T(8,128)(2,1)S(1)} %collective-permute-done.4.v_ref), channel_id=1, source_target_pairs={{0,1},{1,0},{2,3},{3,2},{4,5},{5,4},{6,7},{7,6},{8,9},{9,8},{10,11... | collective-permute-start | bytes 393224 | tf_op jit(solution)/shard_map/ppermute | solution.py:317
  69.8 17.5 %collective-permute-start.3 = (bf16[4,4,16,256]{3,2,1,0:T(8,128)(2,1)S(1)}, bf16[4,4,16,256]{3,2,1,0:T(8,128)(2,1)S(1)}, u32[]{:S(2)}, u32[]{:S(2)}) collective-permute-start(bf16[4,4,16,256]{3,2,1,0:T(8,128)(2,1)S(1)} %collective-permute-done.2.v_ref), channel_id=1, source_target_pairs={{0,1},{1,0},{2,3},{3,2},{4,5},{5,4},{6,7},{7,6},{8,9},{9,8},{10,11... | collective-permute-start | bytes 393224 | tf_op jit(solution)/shard_map/ppermute | solution.py:317
  95.5 3.0 %collective-permute-start.14 = (f32[2,4,4,8,256]{4,3,2,1,0:T(8,128)S(1)}, f32[2,4,4,8,256]{4,3,2,1,0:T(8,128)S(1)}, u32[]{:S(2)}, u32[]{:S(2)}) collective-permute-start(f32[2,4,4,8,256]{4,3,2,1,0:T(8,128)S(1)} %get-tuple-element.44), channel_id=1, source_target_pairs={{0,1},{1,0},{2,3},{3,2},{4,5},{5,4},{6,7},{7,6},{8,9},{9,8},{10,11... | collective-permute-start | bytes 786440 | tf_op jit(solution)/shard_map/ppermute | solution.py:317
  95.6 4.6 %collective-permute-start.12 = (f32[2,4,4,8,256]{4,3,2,1,0:T(8,128)S(1)}, f32[2,4,4,8,256]{4,3,2,1,0:T(8,128)S(1)}, u32[]{:S(2)}, u32[]{:S(2)}) collective-permute-start(f32[2,4,4,8,256]{4,3,2,1,0:T(8,128)S(1)} %get-tuple-element.42), channel_id=1, source_target_pairs={{0,1},{1,0},{2,3},{3,2},{4,5},{5,4},{6,7},{7,6},{8,9},{9,8},{10,11... | collective-permute-start | bytes 786440 | tf_op jit(solution)/shard_map/ppermute | solution.py:317
  96.1 44.4 %copy-start.1 = (bf16[256,8192]{1,0:T(8,128)(2,1)S(1)}, bf16[256,8192]{1,0:T(8,128)(2,1)}, u32[]{:S(2)}) copy-start(bf16[256,8192]{1,0:T(8,128)(2,1)} %f_ref.5) | copy-start | bytes 12582916
  96.1 44.4 %copy-start.2 = (f32[64,256]{1,0:T(8,128)S(1)}, f32[64,256]{1,0:T(8,128)}, u32[]{:S(2)}) copy-start(f32[64,256]{1,0:T(8,128)} %res_ref.3) | copy-start | bytes 196612
  96.1 4.3 %collective-permute-start.10 = (f32[2,4,4,8,256]{4,3,2,1,0:T(8,128)S(1)}, f32[2,4,4,8,256]{4,3,2,1,0:T(8,128)S(1)}, u32[]{:S(2)}, u32[]{:S(2)}) collective-permute-start(f32[2,4,4,8,256]{4,3,2,1,0:T(8,128)S(1)} %get-tuple-element.40), channel_id=1, source_target_pairs={{0,1},{1,0},{2,3},{3,2},{4,5},{5,4},{6,7},{7,6},{8,9},{9,8},{10,11... | collective-permute-start | bytes 786440 | tf_op jit(solution)/shard_map/ppermute | solution.py:317
  98.1 85.0 %copy-start.4 = (f32[64,256]{1,0:T(8,128)S(1)}, f32[64,256]{1,0:T(8,128)}, u32[]{:S(2)}) copy-start(f32[64,256]{1,0:T(8,128)} %d_ref.3) | copy-start | bytes 196612
  98.1 85.0 %copy-start.5 = (f32[64,256]{1,0:T(8,128)S(1)}, f32[64,256]{1,0:T(8,128)}, u32[]{:S(2)}) copy-start(f32[64,256]{1,0:T(8,128)} %it_ref.1) | copy-start | bytes 196612
  98.1 4.6 %collective-permute-start.9 = (f32[2,4,4,8,256]{4,3,2,1,0:T(8,128)S(1)}, f32[2,4,4,8,256]{4,3,2,1,0:T(8,128)S(1)}, u32[]{:S(2)}, u32[]{:S(2)}) collective-permute-start(f32[2,4,4,8,256]{4,3,2,1,0:T(8,128)S(1)} %get-tuple-element.38), channel_id=1, source_target_pairs={{0,1},{1,0},{2,3},{3,2},{4,5},{5,4},{6,7},{7,6},{8,9},{9,8},{10,11... | collective-permute-start | bytes 786440 | tf_op jit(solution)/shard_map/ppermute | solution.py:317
  98.5 6.1 %collective-permute-start.15 = (bf16[2,4,4,8,256]{4,3,2,1,0:T(8,128)(2,1)S(1)}, bf16[2,4,4,8,256]{4,3,2,1,0:T(8,128)(2,1)S(1)}, u32[]{:S(2)}, u32[]{:S(2)}) collective-permute-start(bf16[2,4,4,8,256]{4,3,2,1,0:T(8,128)(2,1)S(1)} %shard_map.108), channel_id=1, source_target_pairs={{0,6},{2,4},{4,2},{6,0},{1,7},{3,5},{5,3},{7,1},{8,14},{10,12},{12... | collective-permute-start | bytes 393224 | tf_op jit(solution)/shard_map/ppermute | solution.py:320
  100.3 4.7 %collective-permute-start.13 = (bf16[2,4,4,8,256]{4,3,2,1,0:T(8,128)(2,1)S(1)}, bf16[2,4,4,8,256]{4,3,2,1,0:T(8,128)(2,1)S(1)}, u32[]{:S(2)}, u32[]{:S(2)}) collective-permute-start(bf16[2,4,4,8,256]{4,3,2,1,0:T(8,128)(2,1)S(1)} %shard_map.106), channel_id=1, source_target_pairs={{0,2},{2,0},{4,6},{6,4},{1,3},{3,1},{5,7},{7,5},{8,10},{10,8},{12,... | collective-permute-start | bytes 393224 | tf_op jit(solution)/shard_map/ppermute | solution.py:320
  100.5 8.0 %collective-permute-start.11 = (bf16[2,4,4,8,256]{4,3,2,1,0:T(8,128)(2,1)S(1)}, bf16[2,4,4,8,256]{4,3,2,1,0:T(8,128)(2,1)S(1)}, u32[]{:S(2)}, u32[]{:S(2)}) collective-permute-start(bf16[2,4,4,8,256]{4,3,2,1,0:T(8,128)(2,1)S(1)} %shard_map.104), channel_id=1, source_target_pairs={{0,4},{2,6},{4,0},{6,2},{1,5},{3,7},{5,1},{7,3},{8,12},{10,14},{12... | collective-permute-start | bytes 393224 | tf_op jit(solution)/shard_map/ppermute | solution.py:320
  126.0 3.7 %collective-permute-start.16 = (f32[16,8,256]{2,1,0:T(8,128)S(1)}, f32[16,8,256]{2,1,0:T(8,128)S(1)}, u32[]{:S(2)}, u32[]{:S(2)}) collective-permute-start(f32[16,8,256]{2,1,0:T(8,128)S(1)} %get-tuple-element.46), channel_id=1, source_target_pairs={{0,1},{1,0},{2,3},{3,2},{4,5},{5,4},{6,7},{7,6},{8,9},{9,8},{10,11... | collective-permute-start | bytes 393224 | tf_op jit(solution)/shard_map/ppermute | solution.py:317
  141.7 2.9 %collective-permute-start.17 = (f32[16,8,384]{2,1,0:T(8,128)S(1)}, f32[16,8,384]{2,1,0:T(8,128)S(1)}, u32[]{:S(2)}, u32[]{:S(2)}) collective-permute-start(f32[16,8,384]{2,1,0:T(8,128)S(1)} %get-tuple-element.50), channel_id=1, source_target_pairs={{0,1},{1,0},{2,3},{3,2},{4,5},{5,4},{6,7},{7,6},{8,9},{9,8},{10,11... | collective-permute-start | bytes 589832 | tf_op jit(solution)/shard_map/ppermute | solution.py:317
  (2 other events, 43.8 us)

commit v7 on v6

--- a/solution.py
+++ b/solution.py
@@ -65,7 +65,7 @@
     d = own_rows(at_ref, d_ref)
     hi = d.astype(bf16)
     lo = (d - hi.astype(f32)).astype(bf16)
-    spread(jnp.concatenate([hi, lo], axis=0), out_ref)
+    out_ref[...] = jnp.concatenate([hi, lo], axis=0)
 
 
 def rows_dot(at_ref, x_ref, y_ref, f_ref):
@@ -79,32 +79,26 @@
     return acc
 
 
-def inner_body(at_ref, x_ref, y_ref, hbm_ref, term_ref, full_ref, out_ref, f_ref, sem):
-    parts = sem.shape[0]
-    width = hbm_ref.shape[1] // parts
-    copies = [
-        pltpu.make_async_copy(
-            hbm_ref.at[:, pl.ds(q * width, width)], f_ref.at[:, pl.ds(q * width, width)], sem.at[q]
-        )
-        for q in range(parts)
-    ]
-    for copy in copies[:2]:
-        copy.start()
+def inner_body(at_ref, *refs):
+    f_ref, term_ref, full_ref, out_ref = refs[8:]
     acc = None
-    count = x_ref.shape[0] // parts
-    for q in range(parts):
-        copies[q].wait()
-        if q + 2 < parts:
-            copies[q + 2].start()
-        for z in range(q * count, q * count + count):
-            for which, ref in ((0, x_ref), (1, y_ref)):
+    for which in range(2):
+        for k in range(4):
+            ref = refs[which * 4 + k]
+            for m in range(4):
+                z = (at_ref[4] ^ m) * 4 + (at_ref[2] ^ k)
                 part = lax.dot_general(
-                    ref[z], f_ref[:, columns(at_ref, z, which)], LAST, preferred_element_type=f32
+                    ref[m], f_ref[:, columns(at_ref, z, which)], LAST, preferred_element_type=f32
                 )
                 acc = part if acc is None else acc + part
     term_ref[...] = acc[:16]
     full_ref[...] = acc[:16] + acc[16:]
     spread(acc[:16].astype(bf16), out_ref)
+
+
+def stack_body(a_ref, b_ref, c_ref, d_ref, out_ref):
+    for m, ref in enumerate((a_ref, b_ref, c_ref, d_ref)):
+        out_ref[m] = ref[...]
 
 
 def outer_body(at_ref, x_ref, y_ref, f_ref, out_ref):
@@ -159,11 +153,18 @@
     lax.fori_loop(0, 2, two, 0)
 
 
-def fill_body(at_ref, p_ref, cen_ref, pa_ref, k_ref, ca_ref):
+def augment_body(p_ref, pa_ref):
     pa_ref[:, :128] = p_ref[...]
-    for r in range(p_ref.shape[0] // 256):
-        rows = pl.ds(r * 256, 256)
+
+    def block(r, carry):
+        rows = pl.ds(pl.multiple_of(r * 512, 512), 512)
         pa_ref[rows, 128:] = norm_lanes(p_ref[rows, :], True)
+        return carry
+
+    lax.fori_loop(0, p_ref.shape[0] // 512, block, 0)
+
+
+def fill_body(at_ref, pa_ref, cen_ref, k_ref, ca_ref):
     chunks(at_ref, 0, pa_ref, cen_ref, ca_ref, k_ref)
 
 
@@ -309,7 +310,7 @@
 
 
 def iteration(points, centers, inner_factor, outer_factor, iterate, residual, direction):
-    at = jnp.stack([lax.axis_index(n) for n in ("y", "c", "x", "zh")])
+    at = jnp.stack([lax.axis_index(n) for n in ("y", "c", "x", "zh", "zl")])
     here = points.shape[0]
     count = float(here * 256)
 
@@ -319,31 +320,30 @@
     def across(v, k):
         return lax.ppermute(v, "x", [(i, i ^ k) for i in range(4)])
 
-    x = call(prep_body, sds((16, 32, 256), bf16), (at, direction), [SM, VM])
-    x = exchange(x, LINE)
+    ca = pltpu.VMEM((2, 512, 256), bf16)
+    kernel = sds((4, here, 512), bf16)
+    sums = sds((here, 64), f32)
+    x = call(prep_body, sds((32, 256), bf16), (at, direction), [SM, VM])
+    line = [x]
+    for k in (1, 2, 3):
+        line.append(lax.ppermute(x, "zl", [(i, i ^ k) for i in range(4)]))
+    pa = call(augment_body, sds((here, 256), bf16), (points,), flops=FILL // 4)
+    x = call(stack_body, sds((4, 32, 256), bf16), line)
+    mine = [x]
+    for k in (1, 2, 3):
+        mine.append(across(x, k))
+    k0 = call(fill_body, kernel, (at, pa, centers), [SM, VM, VM], scratch=[ca], flops=FILL)
     term, full, x = call(
         inner_body,
         (sds((16, 256), f32), sds((16, 256), f32), sds((16, 16, 256), bf16)),
-        (at, x, swap(x), pltpu.with_memory_space_constraint(inner_factor, pltpu.HBM)),
-        [SM, VM, VM, pl.BlockSpec(memory_space=pltpu.HBM)],
-        scratch=[pltpu.VMEM(inner_factor.shape, bf16), pltpu.SemaphoreType.DMA((8,))],
+        (at, *mine, *[swap(v) for v in mine], inner_factor),
+        [SM] + [VM] * 9,
     )
     x = exchange(x, LINE)
     x = call(outer_body, sds((16, 16, 256), bf16), (at, x, swap(x), outer_factor), [SM] + [VM] * 3)
     v = exchange(x, SIDE).reshape(4, 4, 16, 256)
     vs = [v] + [across(v, k) for k in (1, 2, 3)]
     us = [swap(v) for v in vs]
-    kernel = sds((4, here, 512), bf16)
-    sums = sds((here, 64), f32)
-    ca = pltpu.VMEM((2, 512, 256), bf16)
-    pa, k0 = call(
-        fill_body,
-        (sds((here, 256), bf16), kernel),
-        (at, points, centers),
-        [SM, VM, VM],
-        scratch=[ca],
-        flops=FILL,
-    )
     k1, fit = call(
         both_first_body,
         (kernel, sums),

time: 184 us -> 186 us (1.011)
  blocking collectives: 106 us -> 75.5 us
  starting transfers between devices: 21.9 us -> 41 us
  waiting for transfers between devices: 11.6 us -> 21 us
  local copies, waits for them, and re-layouts: 1.02 us -> 7.54 us
  Pallas kernels: 42.8 us -> 40.1 us
    all_to_all x8 -> x6, blocking collectives: 106 us -> 75.5 us  [exchange(): return lax.all_to_all(v, axes, 0, 0, tiled=True)]
    unnamed x16 -> x24, local copies, waits for them, and re-layouts: 1.02 us -> 7.45 us
    ppermute x0 -> x3, starting transfers between devices: none -> 5.54 us  [iteration(): line.append(lax.ppermute(x, 'zl', [(i, i ^ k) for i in range(4)]))]
    all_to_all x0 -> x1, waiting for transfers between devices: none -> 5.47 us  [exchange(): return lax.all_to_all(v, axes, 0, 0, tiled=True)]
    ppermute x12 -> x15, starting transfers between devices: 13.9 us -> 19.1 us  [swap(): return lax.ppermute(v, 'c', SWAP)]
    all_to_all x0 -> x1, starting transfers between devices: none -> 4.48 us  [exchange(): return lax.all_to_all(v, axes, 0, 0, tiled=True)]
    ppermute x0 -> x3, waiting for transfers between devices: none -> 4.38 us  [iteration(): line.append(lax.ppermute(x, 'zl', [(i, i ^ k) for i in range(4)]))]
    ppermute x6 -> x9, starting transfers between devices: 7.96 us -> 11.8 us  [across(): return lax.ppermute(v, 'x', [(i, i ^ k) for i in range(4)])]
  transfers between devices with their start and end apart: 18 -> 28, of which waited for: 8 -> 11; matrix products, arithmetic and copies ran while one was open for 0% -> 0% of each run, Pallas kernels for 12% -> 12%
where the time goes in v7:
time: 186 us
  blocking collectives  75.5 us (41%)
  starting transfers between devices  41 us (22%)
  Pallas kernels  40.1 us (22%)
  waiting for transfers between devices  21 us (11%)
  local copies, waits for them, and re-layouts  7.54 us (4%)
    all_to_all x6, blocking collectives, exchange(): return lax.all_to_all(v, axes, 0, 0, tiled=True)  75.5 us
    pallas_call x25, Pallas kernels, call(): pl.pallas_call(body, out_shape=outs, in_specs=specs or [VM] * len(args),...  40.1 us
    ppermute x15, starting transfers between devices, swap(): return lax.ppermute(v, 'c', SWAP)  19.1 us
    ppermute x9, starting transfers between devices, across(): return lax.ppermute(v, 'x', [(i, i ^ k) for i in range(4)])  11.8 us
    unnamed x24, local copies, waits for them, and re-layouts  7.45 us
    ppermute x9, waiting for transfers between devices, across(): return lax.ppermute(v, 'x', [(i, i ^ k) for i in range(4)])  7.16 us
    ppermute x3, starting transfers between devices, iteration(): line.append(lax.ppermute(x, 'zl', [(i, i ^ k) for i in range(4)]))  5.54 us
    all_to_all x1, waiting for transfers between devices, exchange(): return lax.all_to_all(v, axes, 0, 0, tiled=True)  5.47 us
  transfers between devices with their start and end apart: 28, of which 11 were waited for; matrix products, arithmetic and copies ran while one was open for 0% of the time, Pallas kernels for 12%

profile of v7, /device:TPU:1, one launch (start us, length us, event | category | flops | bytes accessed | tf_op | source)
XLA Modules:
  0.0 185.9 jit_solution(6863694124197397738)
XLA Ops:
  2.1 2.5 %collective-permute-start = (bf16[32,256]{1,0:T(8,128)(2,1)S(1)}, bf16[32,256]{1,0:T(8,128)(2,1)S(1)}, u32[]{:S(2)}, u32[]{:S(2)}) collective-permute-start(bf16[32,256]{1,0:T(8,128)(2,1)S(1)} %shard_map.94.a_ref), channel_id=1, source_target_pairs={{0,8},{8,0},{16,24},{24,16},{1,9},{9,1},{17,25},{25,17},{2,10},{10... | collective-permute-start | bytes 49160 | tf_op jit(solution)/shard_map/ppermute | solution.py:329
  4.7 3.0 %collective-permute-start.1 = (bf16[32,256]{1,0:T(8,128)(2,1)S(1)}, bf16[32,256]{1,0:T(8,128)(2,1)S(1)}, u32[]{:S(2)}, u32[]{:S(2)}) collective-permute-start(bf16[32,256]{1,0:T(8,128)(2,1)S(1)} %shard_map.94.a_ref), channel_id=1, source_target_pairs={{0,16},{8,24},{16,0},{24,8},{1,17},{9,25},{17,1},{25,9},{2,18},{10... | collective-permute-start | bytes 49160 | tf_op jit(solution)/shard_map/ppermute | solution.py:329
  8.9 3.2 %collective-permute-done.2.d_ref = bf16[32,256]{1,0:T(8,128)(2,1)S(1)} collective-permute-done((bf16[32,256]{1,0:T(8,128)(2,1)S(1)}, bf16[32,256]{1,0:T(8,128)(2,1)S(1)}, u32[]{:S(2)}, u32[]{:S(2)}) %collective-permute-start.2) | collective-permute-done | bytes 16416 | tf_op jit(solution)/shard_map/ppermute | solution.py:329
  13.3 2.5 %collective-permute-start.4 = (bf16[4,32,256]{2,1,0:T(8,128)(2,1)S(1)}, bf16[4,32,256]{2,1,0:T(8,128)(2,1)S(1)}, u32[]{:S(2)}, u32[]{:S(2)}) collective-permute-start(bf16[4,32,256]{2,1,0:T(8,128)(2,1)S(1)} %shard_map.95.refs_0_), channel_id=1, source_target_pairs={{0,4},{2,6},{4,0},{6,2},{1,5},{3,7},{5,1},{7,3},{8,12},{10,14},{12... | collective-permute-start | bytes 196616 | tf_op jit(solution)/shard_map/ppermute | solution.py:321
  15.9 3.2 %collective-permute-start.6 = (bf16[4,32,256]{2,1,0:T(8,128)(2,1)S(1)}, bf16[4,32,256]{2,1,0:T(8,128)(2,1)S(1)}, u32[]{:S(2)}, u32[]{:S(2)}) collective-permute-start(bf16[4,32,256]{2,1,0:T(8,128)(2,1)S(1)} %shard_map.95.refs_0_), channel_id=1, source_target_pairs={{0,1},{1,0},{2,3},{3,2},{4,5},{5,4},{6,7},{7,6},{8,9},{9,8},{10,11... | collective-permute-start | bytes 196616 | tf_op jit(solution)/shard_map/ppermute | solution.py:318
  19.1 2.5 %collective-permute-start.8 = (bf16[4,32,256]{2,1,0:T(8,128)(2,1)S(1)}, bf16[4,32,256]{2,1,0:T(8,128)(2,1)S(1)}, u32[]{:S(2)}, u32[]{:S(2)}) collective-permute-start(bf16[4,32,256]{2,1,0:T(8,128)(2,1)S(1)} %collective-permute-done.4.refs_2_), channel_id=1, source_target_pairs={{0,1},{1,0},{2,3},{3,2},{4,5},{5,4},{6,7},{7,6},{8,9},{9,8},{10,11... | collective-permute-start | bytes 196616 | tf_op jit(solution)/shard_map/ppermute | solution.py:318
  21.7 2.4 %collective-permute-start.9 = (bf16[4,32,256]{2,1,0:T(8,128)(2,1)S(1)}, bf16[4,32,256]{2,1,0:T(8,128)(2,1)S(1)}, u32[]{:S(2)}, u32[]{:S(2)}) collective-permute-start(bf16[4,32,256]{2,1,0:T(8,128)(2,1)S(1)} %collective-permute-done.5.refs_3_), channel_id=1, source_target_pairs={{0,1},{1,0},{2,3},{3,2},{4,5},{5,4},{6,7},{7,6},{8,9},{9,8},{10,11... | collective-permute-start | bytes 196616 | tf_op jit(solution)/shard_map/ppermute | solution.py:318
  29.1 10.6 %all_to_all.41.x_ref = bf16[16,16,256]{2,1,0:T(8,128)(2,1)S(1)} all-to-all(bf16[16,16,256]{2,1,0:T(8,128)(2,1)S(1)} %get-tuple-element.26), channel_id=1, replica_groups=mesh['zh'=2,'y'=4,'zl'=4,'x'=4,'c'=2] {'zl','x'}, dimensions={0} | all-to-all | bytes 262144 | tf_op jit(solution)/shard_map/all_to_all | solution.py:42
  44.4 2.4 %shard_map.97 = bf16[16,16,256]{2,1,0:T(8,128)(2,1)} custom-call(s32[5]{0:T(128)S(1)} %stack.23.at_ref, bf16[16,16,256]{2,1,0:T(8,128)(2,1)S(1)} %all_to_all.41.x_ref, bf16[16,16,256]{2,1,0:T(8,128)(2,1)S(1)} %collective-permute-done.10.y_ref, bf16[256,8192]{1,0:T(8,128)(2,1)S(1)} %copy-done), custom_call_target="tpu_custom_call" | custom-call | tf_op jit(solution)/shard_map/pallas_call | solution.py:26
  46.8 4.5 %all-to-all-start.1 = ((bf16[16,16,256]{2,1,0:T(8,128)(2,1)}), bf16[16,16,256]{2,1,0:T(8,128)(2,1)S(1)}, u32[]{:S(2)}, u32[]{:S(2)}) async-start(bf16[16,16,256]{2,1,0:T(8,128)(2,1)} %shard_map.97), calls=%async_computation.1 | async-start | bytes 262144 | tf_op jit(solution)/shard_map/all_to_all | solution.py:42
  53.0 5.5 %all-to-all-done.1 = bf16[16,16,256]{2,1,0:T(8,128)(2,1)S(1)} async-done(((bf16[16,16,256]{2,1,0:T(8,128)(2,1)}), bf16[16,16,256]{2,1,0:T(8,128)(2,1)S(1)}, u32[]{:S(2)}, u32[]{:S(2)}) %all-to-all-start.1) | async-done | bytes 131104 | tf_op jit(solution)/shard_map/all_to_all | solution.py:42
  65.5 3.6 %shard_map.99.k_ref = bf16[4,2048,512]{2,1,0:T(8,128)(2,1)S(1)} custom-call(s32[5]{0:T(128)S(1)} %stack.23.at_ref, bf16[2048,256]{1,0:T(8,128)(2,1)S(1)} %copy-done.11, bf16[8192,128]{1,0:T(8,128)(2,1)S(1)} %copy-done.8), custom_call_target="tpu_custom_call" | custom-call | flops 4000000000 | tf_op jit(solution)/shard_map/pallas_call | solution.py:26
  72.3 5.5 %shard_map.100 = (bf16[4,2048,512]{2,1,0:T(8,128)(2,1)S(1)}, f32[2048,64]{1,0:T(8,128)S(1)}) custom-call(s32[5]{0:T(128)S(1)} %stack.23.at_ref, bf16[2048,256]{1,0:T(8,128)(2,1)S(1)} %copy-done.11, bf16[8192,128]{1,0:T(8,128)(2,1)S(1)} %copy-done.8, bf16[4,4,16,256]{3,2,1,0:T(8,128)(2,1)S(1)} %bitcast.16, ...), custom_call_target="tpu_custom_call" | custom-call | flops 4000000000 | tf_op jit(solution)/shard_map/pallas_call | solution.py:26
  77.8 5.6 %shard_map.101 = (bf16[4,2048,512]{2,1,0:T(8,128)(2,1)S(1)}, f32[2048,64]{1,0:T(8,128)S(1)}) custom-call(s32[5]{0:T(128)S(1)} %stack.23.at_ref, bf16[2048,256]{1,0:T(8,128)(2,1)S(1)} %copy-done.11, bf16[8192,128]{1,0:T(8,128)(2,1)S(1)} %copy-done.8, bf16[4,4,16,256]{3,2,1,0:T(8,128)(2,1)S(1)} %collective-permute-done.15.v_ref, ...), custom_call_target="tpu_custom_call" | custom-call | flops 4000000000 | tf_op jit(solution)/shard_map/pallas_call | solution.py:26
  83.4 5.6 %shard_map.102 = (bf16[4,2048,512]{2,1,0:T(8,128)(2,1)S(1)}, f32[2048,64]{1,0:T(8,128)S(1)}) custom-call(s32[5]{0:T(128)S(1)} %stack.23.at_ref, bf16[2048,256]{1,0:T(8,128)(2,1)S(1)} %copy-done.11, bf16[8192,128]{1,0:T(8,128)(2,1)S(1)} %copy-done.8, bf16[4,4,16,256]{3,2,1,0:T(8,128)(2,1)S(1)} %collective-permute-done.13.v_ref, ...), custom_call_target="tpu_custom_call" | custom-call | flops 4000000000 | tf_op jit(solution)/shard_map/pallas_call | solution.py:26
  89.1 3.0 %shard_map.103.fit_ref = bf16[64,2048]{1,0:T(8,128)(2,1)S(1)} custom-call(bf16[4,4,16,256]{3,2,1,0:T(8,128)(2,1)S(1)} %collective-permute-done.11.v_ref, bf16[4,4,16,256]{3,2,1,0:T(8,128)(2,1)S(1)} %collective-permute-done.12.u_ref, bf16[4,2048,512]{2,1,0:T(8,128)(2,1)S(1)} %get-tuple-element.31.k_ref, f32[2048,64]{1,0:T(8,128)S(1)} %get-tuple-element.32.old_ref), custom_call_target="tpu_custom_call" | custom-call | flops 2000000000 | tf_op jit(solution)/shard_map/pallas_call | solution.py:26
  102.2 2.2 %collective-permute-start.20 = (bf16[2,4,4,8,256]{4,3,2,1,0:T(8,128)(2,1)S(1)}, bf16[2,4,4,8,256]{4,3,2,1,0:T(8,128)(2,1)S(1)}, u32[]{:S(2)}, u32[]{:S(2)}) collective-permute-start(bf16[2,4,4,8,256]{4,3,2,1,0:T(8,128)(2,1)S(1)} %shard_map.106), channel_id=1, source_target_pairs={{0,4},{2,6},{4,0},{6,2},{1,5},{3,7},{5,1},{7,3},{8,12},{10,14},{12... | collective-permute-start | bytes 393224 | tf_op jit(solution)/shard_map/ppermute | solution.py:321
  106.7 3.5 %collective-permute-done.20.c_ref = bf16[2,4,4,8,256]{4,3,2,1,0:T(8,128)(2,1)S(1)} collective-permute-done((bf16[2,4,4,8,256]{4,3,2,1,0:T(8,128)(2,1)S(1)}, bf16[2,4,4,8,256]{4,3,2,1,0:T(8,128)(2,1)S(1)}, u32[]{:S(2)}, u32[]{:S(2)}) %collective-permute-start.20) | collective-permute-done | bytes 131104 | tf_op jit(solution)/shard_map/ppermute | solution.py:321
  110.3 16.6 %all_to_all.42.x_ref = bf16[32,8,256]{2,1,0:T(8,128)(2,1)S(1)} all-to-all(bf16[32,8,256]{2,1,0:T(8,128)(2,1)S(1)} %bitcast.11), channel_id=1, replica_groups=mesh['zh'=2,'y'=4,'zl'=4,'x'=4,'c'=2] {'zh','y','zl'}, dimensions={0} | all-to-all | bytes 262144 | tf_op jit(solution)/shard_map/all_to_all | solution.py:42
  128.1 2.8 %collective-permute-start.25 = (f32[16,8,256]{2,1,0:T(8,128)S(1)}, f32[16,8,256]{2,1,0:T(8,128)S(1)}, u32[]{:S(2)}, u32[]{:S(2)}) collective-permute-start(f32[16,8,256]{2,1,0:T(8,128)S(1)} %get-tuple-element.42), channel_id=1, source_target_pairs={{0,1},{1,0},{2,3},{3,2},{4,5},{5,4},{6,7},{7,6},{8,9},{9,8},{10,11... | collective-permute-start | bytes 393224 | tf_op jit(solution)/shard_map/ppermute | solution.py:318
  131.8 10.8 %all_to_all.43.x_ref = f32[16,8,256]{2,1,0:T(8,128)S(1)} all-to-all(f32[16,8,256]{2,1,0:T(8,128)S(1)} %shard_map.113), channel_id=1, replica_groups=mesh['zh'=2,'y'=4,'zl'=4,'x'=4,'c'=2] {'zl','x'}, dimensions={0} | all-to-all | bytes 262144 | tf_op jit(solution)/shard_map/all_to_all | solution.py:42
  146.7 11.5 %all_to_all.44.x_ref = f32[16,8,384]{2,1,0:T(8,128)S(1)} all-to-all(f32[16,8,384]{2,1,0:T(8,128)S(1)} %shard_map.115), channel_id=1, replica_groups=mesh['zh'=2,'y'=4,'zl'=4,'x'=4,'c'=2] {'zl','x'}, dimensions={0} | all-to-all | bytes 393216 | tf_op jit(solution)/shard_map/all_to_all | solution.py:42
  159.0 12.4 %all_to_all.45 = f32[32,1,128]{2,1,0:T(1,128)S(1)} all-to-all(f32[32,1,128]{2,1,0:T(1,128)S(1)} %bitcast.18), channel_id=1, replica_groups=mesh['zh'=2,'y'=4,'zl'=4,'x'=4,'c'=2] {'zl','x','c'}, dimensions={0} | all-to-all | bytes 32768 | tf_op jit(solution)/shard_map/all_to_all | solution.py:42
  171.5 13.7 %all_to_all.46.x_ref = f32[8,8,384]{2,1,0:T(8,128)S(1)} all-to-all(f32[8,8,384]{2,1,0:T(8,128)S(1)} %shard_map.117), channel_id=1, replica_groups=mesh['zh'=2,'y'=4,'zl'=4,'x'=4,'c'=2] {'zh','y'}, dimensions={0} | all-to-all | bytes 196608 | tf_op jit(solution)/shard_map/all_to_all | solution.py:42
  (88 shorter events, 46.0 us)
Async XLA Ops:
  2.1 5.5 %collective-permute-start = (bf16[32,256]{1,0:T(8,128)(2,1)S(1)}, bf16[32,256]{1,0:T(8,128)(2,1)S(1)}, u32[]{:S(2)}, u32[]{:S(2)}) collective-permute-start(bf16[32,256]{1,0:T(8,128)(2,1)S(1)} %shard_map.94.a_ref), channel_id=1, source_target_pairs={{0,8},{8,0},{16,24},{24,16},{1,9},{9,1},{17,25},{25,17},{2,10},{10... | collective-permute-start | bytes 49160 | tf_op jit(solution)/shard_map/ppermute | solution.py:329
  4.7 4.2 %collective-permute-start.1 = (bf16[32,256]{1,0:T(8,128)(2,1)S(1)}, bf16[32,256]{1,0:T(8,128)(2,1)S(1)}, u32[]{:S(2)}, u32[]{:S(2)}) collective-permute-start(bf16[32,256]{1,0:T(8,128)(2,1)S(1)} %shard_map.94.a_ref), channel_id=1, source_target_pairs={{0,16},{8,24},{16,0},{24,8},{1,17},{9,25},{17,1},{25,9},{2,18},{10... | collective-permute-start | bytes 49160 | tf_op jit(solution)/shard_map/ppermute | solution.py:329
  7.7 4.4 %collective-permute-start.2 = (bf16[32,256]{1,0:T(8,128)(2,1)S(1)}, bf16[32,256]{1,0:T(8,128)(2,1)S(1)}, u32[]{:S(2)}, u32[]{:S(2)}) collective-permute-start(bf16[32,256]{1,0:T(8,128)(2,1)S(1)} %shard_map.94.a_ref), channel_id=1, source_target_pairs={{0,24},{8,16},{16,8},{24,0},{1,25},{9,17},{17,9},{25,1},{2,26},{10... | collective-permute-start | bytes 49160 | tf_op jit(solution)/shard_map/ppermute | solution.py:329
  12.0 7.1 %collective-permute-start.3 = (bf16[4,32,256]{2,1,0:T(8,128)(2,1)S(1)}, bf16[4,32,256]{2,1,0:T(8,128)(2,1)S(1)}, u32[]{:S(2)}, u32[]{:S(2)}) collective-permute-start(bf16[4,32,256]{2,1,0:T(8,128)(2,1)S(1)} %shard_map.95.refs_0_), channel_id=1, source_target_pairs={{0,2},{2,0},{4,6},{6,4},{1,3},{3,1},{5,7},{7,5},{8,10},{10,8},{12,... | collective-permute-start | bytes 196616 | tf_op jit(solution)/shard_map/ppermute | solution.py:321
  13.3 5.9 %collective-permute-start.4 = (bf16[4,32,256]{2,1,0:T(8,128)(2,1)S(1)}, bf16[4,32,256]{2,1,0:T(8,128)(2,1)S(1)}, u32[]{:S(2)}, u32[]{:S(2)}) collective-permute-start(bf16[4,32,256]{2,1,0:T(8,128)(2,1)S(1)} %shard_map.95.refs_0_), channel_id=1, source_target_pairs={{0,4},{2,6},{4,0},{6,2},{1,5},{3,7},{5,1},{7,3},{8,12},{10,14},{12... | collective-permute-start | bytes 196616 | tf_op jit(solution)/shard_map/ppermute | solution.py:321
  15.7 6.0 %collective-permute-start.5 = (bf16[4,32,256]{2,1,0:T(8,128)(2,1)S(1)}, bf16[4,32,256]{2,1,0:T(8,128)(2,1)S(1)}, u32[]{:S(2)}, u32[]{:S(2)}) collective-permute-start(bf16[4,32,256]{2,1,0:T(8,128)(2,1)S(1)} %shard_map.95.refs_0_), channel_id=1, source_target_pairs={{0,6},{2,4},{4,2},{6,0},{1,7},{3,5},{5,3},{7,1},{8,14},{10,12},{12... | collective-permute-start | bytes 196616 | tf_op jit(solution)/shard_map/ppermute | solution.py:321
  15.9 8.2 %collective-permute-start.6 = (bf16[4,32,256]{2,1,0:T(8,128)(2,1)S(1)}, bf16[4,32,256]{2,1,0:T(8,128)(2,1)S(1)}, u32[]{:S(2)}, u32[]{:S(2)}) collective-permute-start(bf16[4,32,256]{2,1,0:T(8,128)(2,1)S(1)} %shard_map.95.refs_0_), channel_id=1, source_target_pairs={{0,1},{1,0},{2,3},{3,2},{4,5},{5,4},{6,7},{7,6},{8,9},{9,8},{10,11... | collective-permute-start | bytes 196616 | tf_op jit(solution)/shard_map/ppermute | solution.py:318
  19.1 5.0 %collective-permute-start.7 = (bf16[4,32,256]{2,1,0:T(8,128)(2,1)S(1)}, bf16[4,32,256]{2,1,0:T(8,128)(2,1)S(1)}, u32[]{:S(2)}, u32[]{:S(2)}) collective-permute-start(bf16[4,32,256]{2,1,0:T(8,128)(2,1)S(1)} %collective-permute-done.3.refs_1_), channel_id=1, source_target_pairs={{0,1},{1,0},{2,3},{3,2},{4,5},{5,4},{6,7},{7,6},{8,9},{9,8},{10,11... | collective-permute-start | bytes 196616 | tf_op jit(solution)/shard_map/ppermute | solution.py:318
  19.1 5.0 %collective-permute-start.8 = (bf16[4,32,256]{2,1,0:T(8,128)(2,1)S(1)}, bf16[4,32,256]{2,1,0:T(8,128)(2,1)S(1)}, u32[]{:S(2)}, u32[]{:S(2)}) collective-permute-start(bf16[4,32,256]{2,1,0:T(8,128)(2,1)S(1)} %collective-permute-done.4.refs_2_), channel_id=1, source_target_pairs={{0,1},{1,0},{2,3},{3,2},{4,5},{5,4},{6,7},{7,6},{8,9},{9,8},{10,11... | collective-permute-start | bytes 196616 | tf_op jit(solution)/shard_map/ppermute | solution.py:318
  46.8 11.7 %all-to-all-start.1 = ((bf16[16,16,256]{2,1,0:T(8,128)(2,1)}), bf16[16,16,256]{2,1,0:T(8,128)(2,1)S(1)}, u32[]{:S(2)}, u32[]{:S(2)}) async-start(bf16[16,16,256]{2,1,0:T(8,128)(2,1)} %shard_map.97), calls=%async_computation.1 | async-start | bytes 262144 | tf_op jit(solution)/shard_map/all_to_all | solution.py:42
  58.5 13.8 %collective-permute-start.17 = (bf16[4,4,16,256]{3,2,1,0:T(8,128)(2,1)S(1)}, bf16[4,4,16,256]{3,2,1,0:T(8,128)(2,1)S(1)}, u32[]{:S(2)}, u32[]{:S(2)}) collective-permute-start(bf16[4,4,16,256]{3,2,1,0:T(8,128)(2,1)S(1)} %bitcast.12), channel_id=1, source_target_pairs={{0,1},{1,0},{2,3},{3,2},{4,5},{5,4},{6,7},{7,6},{8,9},{9,8},{10,11... | collective-permute-start | bytes 393224 | tf_op jit(solution)/shard_map/ppermute | solution.py:318
  60.4 8.7 %collective-permute-start.15 = (bf16[4,4,16,256]{3,2,1,0:T(8,128)(2,1)S(1)}, bf16[4,4,16,256]{3,2,1,0:T(8,128)(2,1)S(1)}, u32[]{:S(2)}, u32[]{:S(2)}) collective-permute-start(bf16[4,4,16,256]{3,2,1,0:T(8,128)(2,1)S(1)} %bitcast.13), channel_id=1, source_target_pairs={{0,2},{2,0},{4,6},{6,4},{1,3},{3,1},{5,7},{7,5},{8,10},{10,8},{12,... | collective-permute-start | bytes 393224 | tf_op jit(solution)/shard_map/ppermute | solution.py:321
  60.5 9.5 %collective-permute-start.13 = (bf16[4,4,16,256]{3,2,1,0:T(8,128)(2,1)S(1)}, bf16[4,4,16,256]{3,2,1,0:T(8,128)(2,1)S(1)}, u32[]{:S(2)}, u32[]{:S(2)}) collective-permute-start(bf16[4,4,16,256]{3,2,1,0:T(8,128)(2,1)S(1)} %bitcast.14), channel_id=1, source_target_pairs={{0,4},{2,6},{4,0},{6,2},{1,5},{3,7},{5,1},{7,3},{8,12},{10,14},{12... | collective-permute-start | bytes 393224 | tf_op jit(solution)/shard_map/ppermute | solution.py:321
  62.6 9.0 %collective-permute-start.11 = (bf16[4,4,16,256]{3,2,1,0:T(8,128)(2,1)S(1)}, bf16[4,4,16,256]{3,2,1,0:T(8,128)(2,1)S(1)}, u32[]{:S(2)}, u32[]{:S(2)}) collective-permute-start(bf16[4,4,16,256]{3,2,1,0:T(8,128)(2,1)S(1)} %bitcast.15), channel_id=1, source_target_pairs={{0,6},{2,4},{4,2},{6,0},{1,7},{3,5},{5,3},{7,1},{8,14},{10,12},{12... | collective-permute-start | bytes 393224 | tf_op jit(solution)/shard_map/ppermute | solution.py:321
  69.1 8.7 %collective-permute-start.16 = (bf16[4,4,16,256]{3,2,1,0:T(8,128)(2,1)S(1)}, bf16[4,4,16,256]{3,2,1,0:T(8,128)(2,1)S(1)}, u32[]{:S(2)}, u32[]{:S(2)}) collective-permute-start(bf16[4,4,16,256]{3,2,1,0:T(8,128)(2,1)S(1)} %collective-permute-done.15.v_ref), channel_id=1, source_target_pairs={{0,1},{1,0},{2,3},{3,2},{4,5},{5,4},{6,7},{7,6},{8,9},{9,8},{10,11... | collective-permute-start | bytes 393224 | tf_op jit(solution)/shard_map/ppermute | solution.py:318
  70.1 13.4 %collective-permute-start.14 = (bf16[4,4,16,256]{3,2,1,0:T(8,128)(2,1)S(1)}, bf16[4,4,16,256]{3,2,1,0:T(8,128)(2,1)S(1)}, u32[]{:S(2)}, u32[]{:S(2)}) collective-permute-start(bf16[4,4,16,256]{3,2,1,0:T(8,128)(2,1)S(1)} %collective-permute-done.13.v_ref), channel_id=1, source_target_pairs={{0,1},{1,0},{2,3},{3,2},{4,5},{5,4},{6,7},{7,6},{8,9},{9,8},{10,11... | collective-permute-start | bytes 393224 | tf_op jit(solution)/shard_map/ppermute | solution.py:318
  71.5 17.5 %collective-permute-start.12 = (bf16[4,4,16,256]{3,2,1,0:T(8,128)(2,1)S(1)}, bf16[4,4,16,256]{3,2,1,0:T(8,128)(2,1)S(1)}, u32[]{:S(2)}, u32[]{:S(2)}) collective-permute-start(bf16[4,4,16,256]{3,2,1,0:T(8,128)(2,1)S(1)} %collective-permute-done.11.v_ref), channel_id=1, source_target_pairs={{0,1},{1,0},{2,3},{3,2},{4,5},{5,4},{6,7},{7,6},{8,9},{9,8},{10,11... | collective-permute-start | bytes 393224 | tf_op jit(solution)/shard_map/ppermute | solution.py:318
  97.4 4.7 %collective-permute-start.21 = (f32[2,4,4,8,256]{4,3,2,1,0:T(8,128)S(1)}, f32[2,4,4,8,256]{4,3,2,1,0:T(8,128)S(1)}, u32[]{:S(2)}, u32[]{:S(2)}) collective-permute-start(f32[2,4,4,8,256]{4,3,2,1,0:T(8,128)S(1)} %get-tuple-element.38), channel_id=1, source_target_pairs={{0,1},{1,0},{2,3},{3,2},{4,5},{5,4},{6,7},{7,6},{8,9},{9,8},{10,11... | collective-permute-start | bytes 786440 | tf_op jit(solution)/shard_map/ppermute | solution.py:318
  97.9 4.3 %collective-permute-start.19 = (f32[2,4,4,8,256]{4,3,2,1,0:T(8,128)S(1)}, f32[2,4,4,8,256]{4,3,2,1,0:T(8,128)S(1)}, u32[]{:S(2)}, u32[]{:S(2)}) collective-permute-start(f32[2,4,4,8,256]{4,3,2,1,0:T(8,128)S(1)} %get-tuple-element.36), channel_id=1, source_target_pairs={{0,1},{1,0},{2,3},{3,2},{4,5},{5,4},{6,7},{7,6},{8,9},{9,8},{10,11... | collective-permute-start | bytes 786440 | tf_op jit(solution)/shard_map/ppermute | solution.py:318
  99.8 4.6 %collective-permute-start.18 = (f32[2,4,4,8,256]{4,3,2,1,0:T(8,128)S(1)}, f32[2,4,4,8,256]{4,3,2,1,0:T(8,128)S(1)}, u32[]{:S(2)}, u32[]{:S(2)}) collective-permute-start(f32[2,4,4,8,256]{4,3,2,1,0:T(8,128)S(1)} %get-tuple-element.34), channel_id=1, source_target_pairs={{0,1},{1,0},{2,3},{3,2},{4,5},{5,4},{6,7},{7,6},{8,9},{9,8},{10,11... | collective-permute-start | bytes 786440 | tf_op jit(solution)/shard_map/ppermute | solution.py:318
  100.2 6.1 %collective-permute-start.24 = (bf16[2,4,4,8,256]{4,3,2,1,0:T(8,128)(2,1)S(1)}, bf16[2,4,4,8,256]{4,3,2,1,0:T(8,128)(2,1)S(1)}, u32[]{:S(2)}, u32[]{:S(2)}) collective-permute-start(bf16[2,4,4,8,256]{4,3,2,1,0:T(8,128)(2,1)S(1)} %shard_map.110), channel_id=1, source_target_pairs={{0,6},{2,4},{4,2},{6,0},{1,7},{3,5},{5,3},{7,1},{8,14},{10,12},{12... | collective-permute-start | bytes 393224 | tf_op jit(solution)/shard_map/ppermute | solution.py:321
  102.1 4.7 %collective-permute-start.22 = (bf16[2,4,4,8,256]{4,3,2,1,0:T(8,128)(2,1)S(1)}, bf16[2,4,4,8,256]{4,3,2,1,0:T(8,128)(2,1)S(1)}, u32[]{:S(2)}, u32[]{:S(2)}) collective-permute-start(bf16[2,4,4,8,256]{4,3,2,1,0:T(8,128)(2,1)S(1)} %shard_map.108), channel_id=1, source_target_pairs={{0,2},{2,0},{4,6},{6,4},{1,3},{3,1},{5,7},{7,5},{8,10},{10,8},{12,... | collective-permute-start | bytes 393224 | tf_op jit(solution)/shard_map/ppermute | solution.py:321
  102.2 8.0 %collective-permute-start.20 = (bf16[2,4,4,8,256]{4,3,2,1,0:T(8,128)(2,1)S(1)}, bf16[2,4,4,8,256]{4,3,2,1,0:T(8,128)(2,1)S(1)}, u32[]{:S(2)}, u32[]{:S(2)}) collective-permute-start(bf16[2,4,4,8,256]{4,3,2,1,0:T(8,128)(2,1)S(1)} %shard_map.106), channel_id=1, source_target_pairs={{0,4},{2,6},{4,0},{6,2},{1,5},{3,7},{5,1},{7,3},{8,12},{10,14},{12... | collective-permute-start | bytes 393224 | tf_op jit(solution)/shard_map/ppermute | solution.py:321
  128.1 3.7 %collective-permute-start.25 = (f32[16,8,256]{2,1,0:T(8,128)S(1)}, f32[16,8,256]{2,1,0:T(8,128)S(1)}, u32[]{:S(2)}, u32[]{:S(2)}) collective-permute-start(f32[16,8,256]{2,1,0:T(8,128)S(1)} %get-tuple-element.42), channel_id=1, source_target_pairs={{0,1},{1,0},{2,3},{3,2},{4,5},{5,4},{6,7},{7,6},{8,9},{9,8},{10,11... | collective-permute-start | bytes 393224 | tf_op jit(solution)/shard_map/ppermute | solution.py:318
  (16 other events, 371.7 us)

commit v8 on v7

--- a/solution.py
+++ b/solution.py
@@ -20,6 +20,7 @@
 LAST = (((1,), (1,)), ((), ()))
 VM = pl.BlockSpec(memory_space=pltpu.VMEM)
 SM = pl.BlockSpec(memory_space=pltpu.SMEM)
+HB = pl.BlockSpec(memory_space=pltpu.HBM)
 
 
 def call(body, outs, args, specs=None, scratch=(), vmem=10, flops=0):
@@ -120,18 +121,20 @@
     return jnp.where(lane == a, one, out).astype(bf16)
 
 
-def chunks(at_ref, shift, pa_ref, cen_ref, ca_ref, k_ref, fit=None):
+def chunks(at_ref, shift, pa_ref, cen_ref, ca_ref, k_ref, fit=None, landed=None):
     step = 256
 
     def load(i, slot):
         z = i * 4 + (at_ref[2] ^ shift)
         for h in range(2):
             cols = slice(h * 256, h * 256 + 256)
-            block = cen_ref[columns(at_ref, z, h), :]
+            block = cen_ref[columns(at_ref, z, h), :] if landed is None else cen_ref[i * 2 + h]
             ca_ref[slot, cols, :128] = block
             ca_ref[slot, cols, 128:] = norm_lanes(block, False)
 
     load(0, 0)
+    for copy in landed or ():
+        copy.wait()
 
     def two(j, carry):
         for slot in range(2):
@@ -153,19 +156,36 @@
     lax.fori_loop(0, 2, two, 0)
 
 
-def augment_body(p_ref, pa_ref):
-    pa_ref[:, :128] = p_ref[...]
-
-    def block(r, carry):
-        rows = pl.ds(pl.multiple_of(r * 512, 512), 512)
+def augment_body(hbm_ref, pa_ref, p_ref, sem):
+    part = p_ref.shape[0] // sem.shape[0]
+    copies = []
+    for q in range(sem.shape[0]):
+        rows = pl.ds(q * part, part)
+        copies.append(pltpu.make_async_copy(hbm_ref.at[rows, :], p_ref.at[rows, :], sem.at[q]))
+        copies[q].start()
+    for copy in copies:
+        copy.wait()
+
+    def block(q, carry):
+        rows = pl.ds(pl.multiple_of(q * part, part), part)
+        pa_ref[rows, :128] = p_ref[rows, :]
         pa_ref[rows, 128:] = norm_lanes(p_ref[rows, :], True)
         return carry
 
-    lax.fori_loop(0, p_ref.shape[0] // 512, block, 0)
-
-
-def fill_body(at_ref, pa_ref, cen_ref, k_ref, ca_ref):
-    chunks(at_ref, 0, pa_ref, cen_ref, ca_ref, k_ref)
+    lax.fori_loop(0, sem.shape[0], block, 0)
+
+
+def fill_body(at_ref, pa_ref, hbm_ref, k_ref, ca_ref, cen_ref, sem):
+    copies = []
+    for i in range(4):
+        for h in range(2):
+            rows = columns(at_ref, i * 4 + at_ref[2], h)
+            n = i * 2 + h
+            copies.append(pltpu.make_async_copy(hbm_ref.at[rows, :], cen_ref.at[n], sem.at[n]))
+            copies[n].start()
+    for copy in copies[:2]:
+        copy.wait()
+    chunks(at_ref, 0, pa_ref, cen_ref, ca_ref, k_ref, landed=copies[2:])
 
 
 class Fitter:
@@ -327,12 +347,26 @@
     line = [x]
     for k in (1, 2, 3):
         line.append(lax.ppermute(x, "zl", [(i, i ^ k) for i in range(4)]))
-    pa = call(augment_body, sds((here, 256), bf16), (points,), flops=FILL // 4)
+    pa = call(
+        augment_body,
+        sds((here, 256), bf16),
+        (pltpu.with_memory_space_constraint(points, pltpu.HBM),),
+        [HB],
+        scratch=[pltpu.VMEM(points.shape, bf16), pltpu.SemaphoreType.DMA((4,))],
+        flops=FILL // 4,
+    )
     x = call(stack_body, sds((4, 32, 256), bf16), line)
     mine = [x]
     for k in (1, 2, 3):
         mine.append(across(x, k))
-    k0 = call(fill_body, kernel, (at, pa, centers), [SM, VM, VM], scratch=[ca], flops=FILL)
+    k0 = call(
+        fill_body,
+        kernel,
+        (at, pa, pltpu.with_memory_space_constraint(centers, pltpu.HBM)),
+        [SM, VM, HB],
+        scratch=[ca, pltpu.VMEM((8, 256, 128), bf16), pltpu.SemaphoreType.DMA((8,))],
+        flops=FILL,
+    )
     term, full, x = call(
         inner_body,
         (sds((16, 256), f32), sds((16, 256), f32), sds((16, 16, 256), bf16)),

time: 186 us -> 187 us (level)
  local copies, waits for them, and re-layouts: 7.54 us -> 5.33 us
  Pallas kernels: 40.1 us -> 42.2 us
    unnamed x24 -> x18, local copies, waits for them, and re-layouts: 7.45 us -> 5.25 us
    pallas_call x25, Pallas kernels: 40.1 us -> 42.2 us  [call(): pl.pallas_call(body, out_shape=outs, in_specs=specs or [VM] * len(args),...]
  transfers between devices with their start and end apart: 28 -> 28, of which waited for: 11 -> 11; matrix products, arithmetic and copies ran while one was open for 0% -> 0% of each run, Pallas kernels for 12% -> 13%
where the time goes in v8:
time: 187 us; the launch traced here: 186 us
  blocking collectives  75.5 us (40%)
  Pallas kernels  42.2 us (23%)
  starting transfers between devices  41 us (22%)
  waiting for transfers between devices  21 us (11%)
  local copies, waits for them, and re-layouts  5.33 us (3%)
    all_to_all x6, blocking collectives, exchange(): return lax.all_to_all(v, axes, 0, 0, tiled=True)  75.5 us
    pallas_call x25, Pallas kernels, call(): pl.pallas_call(body, out_shape=outs, in_specs=specs or [VM] * len(args),...  42.2 us
    ppermute x15, starting transfers between devices, swap(): return lax.ppermute(v, 'c', SWAP)  19.2 us
    ppermute x9, starting transfers between devices, across(): return lax.ppermute(v, 'x', [(i, i ^ k) for i in range(4)])  11.8 us
    ppermute x9, waiting for transfers between devices, across(): return lax.ppermute(v, 'x', [(i, i ^ k) for i in range(4)])  7.41 us
    ppermute x3, starting transfers between devices, iteration(): line.append(lax.ppermute(x, 'zl', [(i, i ^ k) for i in range(4)]))  5.54 us
    all_to_all x1, waiting for transfers between devices, exchange(): return lax.all_to_all(v, axes, 0, 0, tiled=True)  5.25 us
    unnamed x18, local copies, waits for them, and re-layouts  5.25 us
  transfers between devices with their start and end apart: 28, of which 11 were waited for; matrix products, arithmetic and copies ran while one was open for 0% of the time, Pallas kernels for 13%

profile of v8, /device:TPU:1, one launch (start us, length us, event | category | flops | bytes accessed | tf_op | source)
XLA Modules:
  0.0 186.0 jit_solution(8204536376192452090)
XLA Ops:
  2.1 2.5 %collective-permute-start = (bf16[32,256]{1,0:T(8,128)(2,1)S(1)}, bf16[32,256]{1,0:T(8,128)(2,1)S(1)}, u32[]{:S(2)}, u32[]{:S(2)}) collective-permute-start(bf16[32,256]{1,0:T(8,128)(2,1)S(1)} %shard_map.94.a_ref), channel_id=1, source_target_pairs={{0,8},{8,0},{16,24},{24,16},{1,9},{9,1},{17,25},{25,17},{2,10},{10... | collective-permute-start | bytes 49160 | tf_op jit(solution)/shard_map/ppermute | solution.py:349
  4.7 3.0 %collective-permute-start.1 = (bf16[32,256]{1,0:T(8,128)(2,1)S(1)}, bf16[32,256]{1,0:T(8,128)(2,1)S(1)}, u32[]{:S(2)}, u32[]{:S(2)}) collective-permute-start(bf16[32,256]{1,0:T(8,128)(2,1)S(1)} %shard_map.94.a_ref), channel_id=1, source_target_pairs={{0,16},{8,24},{16,0},{24,8},{1,17},{9,25},{17,1},{25,9},{2,18},{10... | collective-permute-start | bytes 49160 | tf_op jit(solution)/shard_map/ppermute | solution.py:349
  8.9 3.2 %collective-permute-done.2.d_ref = bf16[32,256]{1,0:T(8,128)(2,1)S(1)} collective-permute-done((bf16[32,256]{1,0:T(8,128)(2,1)S(1)}, bf16[32,256]{1,0:T(8,128)(2,1)S(1)}, u32[]{:S(2)}, u32[]{:S(2)}) %collective-permute-start.2) | collective-permute-done | bytes 16416 | tf_op jit(solution)/shard_map/ppermute | solution.py:349
  13.3 2.5 %collective-permute-start.4 = (bf16[4,32,256]{2,1,0:T(8,128)(2,1)S(1)}, bf16[4,32,256]{2,1,0:T(8,128)(2,1)S(1)}, u32[]{:S(2)}, u32[]{:S(2)}) collective-permute-start(bf16[4,32,256]{2,1,0:T(8,128)(2,1)S(1)} %shard_map.95.refs_0_), channel_id=1, source_target_pairs={{0,4},{2,6},{4,0},{6,2},{1,5},{3,7},{5,1},{7,3},{8,12},{10,14},{12... | collective-permute-start | bytes 196616 | tf_op jit(solution)/shard_map/ppermute | solution.py:341
  15.9 3.2 %collective-permute-start.6 = (bf16[4,32,256]{2,1,0:T(8,128)(2,1)S(1)}, bf16[4,32,256]{2,1,0:T(8,128)(2,1)S(1)}, u32[]{:S(2)}, u32[]{:S(2)}) collective-permute-start(bf16[4,32,256]{2,1,0:T(8,128)(2,1)S(1)} %shard_map.95.refs_0_), channel_id=1, source_target_pairs={{0,1},{1,0},{2,3},{3,2},{4,5},{5,4},{6,7},{7,6},{8,9},{9,8},{10,11... | collective-permute-start | bytes 196616 | tf_op jit(solution)/shard_map/ppermute | solution.py:338
  19.1 2.5 %collective-permute-start.8 = (bf16[4,32,256]{2,1,0:T(8,128)(2,1)S(1)}, bf16[4,32,256]{2,1,0:T(8,128)(2,1)S(1)}, u32[]{:S(2)}, u32[]{:S(2)}) collective-permute-start(bf16[4,32,256]{2,1,0:T(8,128)(2,1)S(1)} %collective-permute-done.4.refs_2_), channel_id=1, source_target_pairs={{0,1},{1,0},{2,3},{3,2},{4,5},{5,4},{6,7},{7,6},{8,9},{9,8},{10,11... | collective-permute-start | bytes 196616 | tf_op jit(solution)/shard_map/ppermute | solution.py:338
  21.7 2.4 %collective-permute-start.9 = (bf16[4,32,256]{2,1,0:T(8,128)(2,1)S(1)}, bf16[4,32,256]{2,1,0:T(8,128)(2,1)S(1)}, u32[]{:S(2)}, u32[]{:S(2)}) collective-permute-start(bf16[4,32,256]{2,1,0:T(8,128)(2,1)S(1)} %collective-permute-done.5.refs_3_), channel_id=1, source_target_pairs={{0,1},{1,0},{2,3},{3,2},{4,5},{5,4},{6,7},{7,6},{8,9},{9,8},{10,11... | collective-permute-start | bytes 196616 | tf_op jit(solution)/shard_map/ppermute | solution.py:338
  29.1 10.7 %all_to_all.41.x_ref = bf16[16,16,256]{2,1,0:T(8,128)(2,1)S(1)} all-to-all(bf16[16,16,256]{2,1,0:T(8,128)(2,1)S(1)} %get-tuple-element.26), channel_id=1, replica_groups=mesh['zh'=2,'y'=4,'zl'=4,'x'=4,'c'=2] {'zl','x'}, dimensions={0} | all-to-all | bytes 262144 | tf_op jit(solution)/shard_map/all_to_all | solution.py:43
  44.4 2.4 %shard_map.97 = bf16[16,16,256]{2,1,0:T(8,128)(2,1)} custom-call(s32[5]{0:T(128)S(1)} %stack.23.at_ref, bf16[16,16,256]{2,1,0:T(8,128)(2,1)S(1)} %all_to_all.41.x_ref, bf16[16,16,256]{2,1,0:T(8,128)(2,1)S(1)} %collective-permute-done.10.y_ref, bf16[256,8192]{1,0:T(8,128)(2,1)S(1)} %copy-done), custom_call_target="tpu_custom_call" | custom-call | tf_op jit(solution)/shard_map/pallas_call | solution.py:27
  46.8 4.5 %all-to-all-start.1 = ((bf16[16,16,256]{2,1,0:T(8,128)(2,1)}), bf16[16,16,256]{2,1,0:T(8,128)(2,1)S(1)}, u32[]{:S(2)}, u32[]{:S(2)}) async-start(bf16[16,16,256]{2,1,0:T(8,128)(2,1)} %shard_map.97), calls=%async_computation.1 | async-start | bytes 262144 | tf_op jit(solution)/shard_map/all_to_all | solution.py:43
  53.3 5.3 %all-to-all-done.1 = bf16[16,16,256]{2,1,0:T(8,128)(2,1)S(1)} async-done(((bf16[16,16,256]{2,1,0:T(8,128)(2,1)}), bf16[16,16,256]{2,1,0:T(8,128)(2,1)S(1)}, u32[]{:S(2)}, u32[]{:S(2)}) %all-to-all-start.1) | async-done | bytes 131104 | tf_op jit(solution)/shard_map/all_to_all | solution.py:43
  64.3 4.6 %shard_map.99.k_ref = bf16[4,2048,512]{2,1,0:T(8,128)(2,1)S(1)} custom-call(s32[5]{0:T(128)S(1)} %stack.23.at_ref, bf16[2048,256]{1,0:T(8,128)(2,1)S(1)} %shard_map.98.pa_ref, bf16[8192,128]{1,0:T(8,128)(2,1)} %cen_ref.5), custom_call_target="tpu_custom_call" | custom-call | flops 4000000000 | tf_op jit(solution)/shard_map/pallas_call | solution.py:27
  72.4 5.5 %shard_map.100 = (bf16[4,2048,512]{2,1,0:T(8,128)(2,1)S(1)}, f32[2048,64]{1,0:T(8,128)S(1)}) custom-call(s32[5]{0:T(128)S(1)} %stack.23.at_ref, bf16[2048,256]{1,0:T(8,128)(2,1)S(1)} %shard_map.98.pa_ref, bf16[8192,128]{1,0:T(8,128)(2,1)S(1)} %copy-done.8, bf16[4,4,16,256]{3,2,1,0:T(8,128)(2,1)S(1)} %bitcast.16, ...), custom_call_target="tpu_custom_call" | custom-call | flops 4000000000 | tf_op jit(solution)/shard_map/pallas_call | solution.py:27
  77.9 5.6 %shard_map.101 = (bf16[4,2048,512]{2,1,0:T(8,128)(2,1)S(1)}, f32[2048,64]{1,0:T(8,128)S(1)}) custom-call(s32[5]{0:T(128)S(1)} %stack.23.at_ref, bf16[2048,256]{1,0:T(8,128)(2,1)S(1)} %shard_map.98.pa_ref, bf16[8192,128]{1,0:T(8,128)(2,1)S(1)} %copy-done.8, bf16[4,4,16,256]{3,2,1,0:T(8,128)(2,1)S(1)} %collective-permute-done.15.v_ref, ...), custom_call_target="tpu_custom_call" | custom-call | flops 4000000000 | tf_op jit(solution)/shard_map/pallas_call | solution.py:27
  83.5 5.6 %shard_map.102 = (bf16[4,2048,512]{2,1,0:T(8,128)(2,1)S(1)}, f32[2048,64]{1,0:T(8,128)S(1)}) custom-call(s32[5]{0:T(128)S(1)} %stack.23.at_ref, bf16[2048,256]{1,0:T(8,128)(2,1)S(1)} %shard_map.98.pa_ref, bf16[8192,128]{1,0:T(8,128)(2,1)S(1)} %copy-done.8, bf16[4,4,16,256]{3,2,1,0:T(8,128)(2,1)S(1)} %collective-permute-done.13.v_ref, ...), custom_call_target="tpu_custom_call" | custom-call | flops 4000000000 | tf_op jit(solution)/shard_map/pallas_call | solution.py:27
  89.1 3.0 %shard_map.103.fit_ref = bf16[64,2048]{1,0:T(8,128)(2,1)S(1)} custom-call(bf16[4,4,16,256]{3,2,1,0:T(8,128)(2,1)S(1)} %collective-permute-done.11.v_ref, bf16[4,4,16,256]{3,2,1,0:T(8,128)(2,1)S(1)} %collective-permute-done.12.u_ref, bf16[4,2048,512]{2,1,0:T(8,128)(2,1)S(1)} %get-tuple-element.31.k_ref, f32[2048,64]{1,0:T(8,128)S(1)} %get-tuple-element.32.old_ref), custom_call_target="tpu_custom_call" | custom-call | flops 2000000000 | tf_op jit(solution)/shard_map/pallas_call | solution.py:27
  102.3 2.2 %collective-permute-start.20 = (bf16[2,4,4,8,256]{4,3,2,1,0:T(8,128)(2,1)S(1)}, bf16[2,4,4,8,256]{4,3,2,1,0:T(8,128)(2,1)S(1)}, u32[]{:S(2)}, u32[]{:S(2)}) collective-permute-start(bf16[2,4,4,8,256]{4,3,2,1,0:T(8,128)(2,1)S(1)} %shard_map.106), channel_id=1, source_target_pairs={{0,4},{2,6},{4,0},{6,2},{1,5},{3,7},{5,1},{7,3},{8,12},{10,14},{12... | collective-permute-start | bytes 393224 | tf_op jit(solution)/shard_map/ppermute | solution.py:341
  106.8 3.5 %collective-permute-done.20.c_ref = bf16[2,4,4,8,256]{4,3,2,1,0:T(8,128)(2,1)S(1)} collective-permute-done((bf16[2,4,4,8,256]{4,3,2,1,0:T(8,128)(2,1)S(1)}, bf16[2,4,4,8,256]{4,3,2,1,0:T(8,128)(2,1)S(1)}, u32[]{:S(2)}, u32[]{:S(2)}) %collective-permute-start.20) | collective-permute-done | bytes 131104 | tf_op jit(solution)/shard_map/ppermute | solution.py:341
  110.3 16.6 %all_to_all.42.x_ref = bf16[32,8,256]{2,1,0:T(8,128)(2,1)S(1)} all-to-all(bf16[32,8,256]{2,1,0:T(8,128)(2,1)S(1)} %bitcast.11), channel_id=1, replica_groups=mesh['zh'=2,'y'=4,'zl'=4,'x'=4,'c'=2] {'zh','y','zl'}, dimensions={0} | all-to-all | bytes 262144 | tf_op jit(solution)/shard_map/all_to_all | solution.py:43
  128.1 2.8 %collective-permute-start.25 = (f32[16,8,256]{2,1,0:T(8,128)S(1)}, f32[16,8,256]{2,1,0:T(8,128)S(1)}, u32[]{:S(2)}, u32[]{:S(2)}) collective-permute-start(f32[16,8,256]{2,1,0:T(8,128)S(1)} %get-tuple-element.42), channel_id=1, source_target_pairs={{0,1},{1,0},{2,3},{3,2},{4,5},{5,4},{6,7},{7,6},{8,9},{9,8},{10,11... | collective-permute-start | bytes 393224 | tf_op jit(solution)/shard_map/ppermute | solution.py:338
  131.9 10.8 %all_to_all.43.x_ref = f32[16,8,256]{2,1,0:T(8,128)S(1)} all-to-all(f32[16,8,256]{2,1,0:T(8,128)S(1)} %shard_map.113), channel_id=1, replica_groups=mesh['zh'=2,'y'=4,'zl'=4,'x'=4,'c'=2] {'zl','x'}, dimensions={0} | all-to-all | bytes 262144 | tf_op jit(solution)/shard_map/all_to_all | solution.py:43
  146.8 11.5 %all_to_all.44.x_ref = f32[16,8,384]{2,1,0:T(8,128)S(1)} all-to-all(f32[16,8,384]{2,1,0:T(8,128)S(1)} %shard_map.115), channel_id=1, replica_groups=mesh['zh'=2,'y'=4,'zl'=4,'x'=4,'c'=2] {'zl','x'}, dimensions={0} | all-to-all | bytes 393216 | tf_op jit(solution)/shard_map/all_to_all | solution.py:43
  159.0 12.4 %all_to_all.45 = f32[32,1,128]{2,1,0:T(1,128)S(1)} all-to-all(f32[32,1,128]{2,1,0:T(1,128)S(1)} %bitcast.18), channel_id=1, replica_groups=mesh['zh'=2,'y'=4,'zl'=4,'x'=4,'c'=2] {'zl','x','c'}, dimensions={0} | all-to-all | bytes 32768 | tf_op jit(solution)/shard_map/all_to_all | solution.py:43
  171.5 13.7 %all_to_all.46.x_ref = f32[8,8,384]{2,1,0:T(8,128)S(1)} all-to-all(f32[8,8,384]{2,1,0:T(8,128)S(1)} %shard_map.117), channel_id=1, replica_groups=mesh['zh'=2,'y'=4,'zl'=4,'x'=4,'c'=2] {'zh','y'}, dimensions={0} | all-to-all | bytes 196608 | tf_op jit(solution)/shard_map/all_to_all | solution.py:43
  (82 shorter events, 45.3 us)
Async XLA Ops:
  2.1 5.5 %collective-permute-start = (bf16[32,256]{1,0:T(8,128)(2,1)S(1)}, bf16[32,256]{1,0:T(8,128)(2,1)S(1)}, u32[]{:S(2)}, u32[]{:S(2)}) collective-permute-start(bf16[32,256]{1,0:T(8,128)(2,1)S(1)} %shard_map.94.a_ref), channel_id=1, source_target_pairs={{0,8},{8,0},{16,24},{24,16},{1,9},{9,1},{17,25},{25,17},{2,10},{10... | collective-permute-start | bytes 49160 | tf_op jit(solution)/shard_map/ppermute | solution.py:349
  4.7 4.2 %collective-permute-start.1 = (bf16[32,256]{1,0:T(8,128)(2,1)S(1)}, bf16[32,256]{1,0:T(8,128)(2,1)S(1)}, u32[]{:S(2)}, u32[]{:S(2)}) collective-permute-start(bf16[32,256]{1,0:T(8,128)(2,1)S(1)} %shard_map.94.a_ref), channel_id=1, source_target_pairs={{0,16},{8,24},{16,0},{24,8},{1,17},{9,25},{17,1},{25,9},{2,18},{10... | collective-permute-start | bytes 49160 | tf_op jit(solution)/shard_map/ppermute | solution.py:349
  7.7 4.4 %collective-permute-start.2 = (bf16[32,256]{1,0:T(8,128)(2,1)S(1)}, bf16[32,256]{1,0:T(8,128)(2,1)S(1)}, u32[]{:S(2)}, u32[]{:S(2)}) collective-permute-start(bf16[32,256]{1,0:T(8,128)(2,1)S(1)} %shard_map.94.a_ref), channel_id=1, source_target_pairs={{0,24},{8,16},{16,8},{24,0},{1,25},{9,17},{17,9},{25,1},{2,26},{10... | collective-permute-start | bytes 49160 | tf_op jit(solution)/shard_map/ppermute | solution.py:349
  12.0 7.1 %collective-permute-start.3 = (bf16[4,32,256]{2,1,0:T(8,128)(2,1)S(1)}, bf16[4,32,256]{2,1,0:T(8,128)(2,1)S(1)}, u32[]{:S(2)}, u32[]{:S(2)}) collective-permute-start(bf16[4,32,256]{2,1,0:T(8,128)(2,1)S(1)} %shard_map.95.refs_0_), channel_id=1, source_target_pairs={{0,2},{2,0},{4,6},{6,4},{1,3},{3,1},{5,7},{7,5},{8,10},{10,8},{12,... | collective-permute-start | bytes 196616 | tf_op jit(solution)/shard_map/ppermute | solution.py:341
  13.3 5.9 %collective-permute-start.4 = (bf16[4,32,256]{2,1,0:T(8,128)(2,1)S(1)}, bf16[4,32,256]{2,1,0:T(8,128)(2,1)S(1)}, u32[]{:S(2)}, u32[]{:S(2)}) collective-permute-start(bf16[4,32,256]{2,1,0:T(8,128)(2,1)S(1)} %shard_map.95.refs_0_), channel_id=1, source_target_pairs={{0,4},{2,6},{4,0},{6,2},{1,5},{3,7},{5,1},{7,3},{8,12},{10,14},{12... | collective-permute-start | bytes 196616 | tf_op jit(solution)/shard_map/ppermute | solution.py:341
  15.7 6.0 %collective-permute-start.5 = (bf16[4,32,256]{2,1,0:T(8,128)(2,1)S(1)}, bf16[4,32,256]{2,1,0:T(8,128)(2,1)S(1)}, u32[]{:S(2)}, u32[]{:S(2)}) collective-permute-start(bf16[4,32,256]{2,1,0:T(8,128)(2,1)S(1)} %shard_map.95.refs_0_), channel_id=1, source_target_pairs={{0,6},{2,4},{4,2},{6,0},{1,7},{3,5},{5,3},{7,1},{8,14},{10,12},{12... | collective-permute-start | bytes 196616 | tf_op jit(solution)/shard_map/ppermute | solution.py:341
  15.9 8.2 %collective-permute-start.6 = (bf16[4,32,256]{2,1,0:T(8,128)(2,1)S(1)}, bf16[4,32,256]{2,1,0:T(8,128)(2,1)S(1)}, u32[]{:S(2)}, u32[]{:S(2)}) collective-permute-start(bf16[4,32,256]{2,1,0:T(8,128)(2,1)S(1)} %shard_map.95.refs_0_), channel_id=1, source_target_pairs={{0,1},{1,0},{2,3},{3,2},{4,5},{5,4},{6,7},{7,6},{8,9},{9,8},{10,11... | collective-permute-start | bytes 196616 | tf_op jit(solution)/shard_map/ppermute | solution.py:338
  19.1 5.0 %collective-permute-start.7 = (bf16[4,32,256]{2,1,0:T(8,128)(2,1)S(1)}, bf16[4,32,256]{2,1,0:T(8,128)(2,1)S(1)}, u32[]{:S(2)}, u32[]{:S(2)}) collective-permute-start(bf16[4,32,256]{2,1,0:T(8,128)(2,1)S(1)} %collective-permute-done.3.refs_1_), channel_id=1, source_target_pairs={{0,1},{1,0},{2,3},{3,2},{4,5},{5,4},{6,7},{7,6},{8,9},{9,8},{10,11... | collective-permute-start | bytes 196616 | tf_op jit(solution)/shard_map/ppermute | solution.py:338
  19.1 5.0 %collective-permute-start.8 = (bf16[4,32,256]{2,1,0:T(8,128)(2,1)S(1)}, bf16[4,32,256]{2,1,0:T(8,128)(2,1)S(1)}, u32[]{:S(2)}, u32[]{:S(2)}) collective-permute-start(bf16[4,32,256]{2,1,0:T(8,128)(2,1)S(1)} %collective-permute-done.4.refs_2_), channel_id=1, source_target_pairs={{0,1},{1,0},{2,3},{3,2},{4,5},{5,4},{6,7},{7,6},{8,9},{9,8},{10,11... | collective-permute-start | bytes 196616 | tf_op jit(solution)/shard_map/ppermute | solution.py:338
  46.8 11.7 %all-to-all-start.1 = ((bf16[16,16,256]{2,1,0:T(8,128)(2,1)}), bf16[16,16,256]{2,1,0:T(8,128)(2,1)S(1)}, u32[]{:S(2)}, u32[]{:S(2)}) async-start(bf16[16,16,256]{2,1,0:T(8,128)(2,1)} %shard_map.97), calls=%async_computation.1 | async-start | bytes 262144 | tf_op jit(solution)/shard_map/all_to_all | solution.py:43
  58.5 13.8 %collective-permute-start.17 = (bf16[4,4,16,256]{3,2,1,0:T(8,128)(2,1)S(1)}, bf16[4,4,16,256]{3,2,1,0:T(8,128)(2,1)S(1)}, u32[]{:S(2)}, u32[]{:S(2)}) collective-permute-start(bf16[4,4,16,256]{3,2,1,0:T(8,128)(2,1)S(1)} %bitcast.12), channel_id=1, source_target_pairs={{0,1},{1,0},{2,3},{3,2},{4,5},{5,4},{6,7},{7,6},{8,9},{9,8},{10,11... | collective-permute-start | bytes 393224 | tf_op jit(solution)/shard_map/ppermute | solution.py:338
  60.4 8.4 %collective-permute-start.15 = (bf16[4,4,16,256]{3,2,1,0:T(8,128)(2,1)S(1)}, bf16[4,4,16,256]{3,2,1,0:T(8,128)(2,1)S(1)}, u32[]{:S(2)}, u32[]{:S(2)}) collective-permute-start(bf16[4,4,16,256]{3,2,1,0:T(8,128)(2,1)S(1)} %bitcast.13), channel_id=1, source_target_pairs={{0,2},{2,0},{4,6},{6,4},{1,3},{3,1},{5,7},{7,5},{8,10},{10,8},{12,... | collective-permute-start | bytes 393224 | tf_op jit(solution)/shard_map/ppermute | solution.py:341
  60.5 9.3 %collective-permute-start.13 = (bf16[4,4,16,256]{3,2,1,0:T(8,128)(2,1)S(1)}, bf16[4,4,16,256]{3,2,1,0:T(8,128)(2,1)S(1)}, u32[]{:S(2)}, u32[]{:S(2)}) collective-permute-start(bf16[4,4,16,256]{3,2,1,0:T(8,128)(2,1)S(1)} %bitcast.14), channel_id=1, source_target_pairs={{0,4},{2,6},{4,0},{6,2},{1,5},{3,7},{5,1},{7,3},{8,12},{10,14},{12... | collective-permute-start | bytes 393224 | tf_op jit(solution)/shard_map/ppermute | solution.py:341
  62.6 9.0 %collective-permute-start.11 = (bf16[4,4,16,256]{3,2,1,0:T(8,128)(2,1)S(1)}, bf16[4,4,16,256]{3,2,1,0:T(8,128)(2,1)S(1)}, u32[]{:S(2)}, u32[]{:S(2)}) collective-permute-start(bf16[4,4,16,256]{3,2,1,0:T(8,128)(2,1)S(1)} %bitcast.15), channel_id=1, source_target_pairs={{0,6},{2,4},{4,2},{6,0},{1,7},{3,5},{5,3},{7,1},{8,14},{10,12},{12... | collective-permute-start | bytes 393224 | tf_op jit(solution)/shard_map/ppermute | solution.py:341
  68.9 9.0 %collective-permute-start.16 = (bf16[4,4,16,256]{3,2,1,0:T(8,128)(2,1)S(1)}, bf16[4,4,16,256]{3,2,1,0:T(8,128)(2,1)S(1)}, u32[]{:S(2)}, u32[]{:S(2)}) collective-permute-start(bf16[4,4,16,256]{3,2,1,0:T(8,128)(2,1)S(1)} %collective-permute-done.15.v_ref), channel_id=1, source_target_pairs={{0,1},{1,0},{2,3},{3,2},{4,5},{5,4},{6,7},{7,6},{8,9},{9,8},{10,11... | collective-permute-start | bytes 393224 | tf_op jit(solution)/shard_map/ppermute | solution.py:338
  69.8 13.7 %collective-permute-start.14 = (bf16[4,4,16,256]{3,2,1,0:T(8,128)(2,1)S(1)}, bf16[4,4,16,256]{3,2,1,0:T(8,128)(2,1)S(1)}, u32[]{:S(2)}, u32[]{:S(2)}) collective-permute-start(bf16[4,4,16,256]{3,2,1,0:T(8,128)(2,1)S(1)} %collective-permute-done.13.v_ref), channel_id=1, source_target_pairs={{0,1},{1,0},{2,3},{3,2},{4,5},{5,4},{6,7},{7,6},{8,9},{9,8},{10,11... | collective-permute-start | bytes 393224 | tf_op jit(solution)/shard_map/ppermute | solution.py:338
  71.6 17.5 %collective-permute-start.12 = (bf16[4,4,16,256]{3,2,1,0:T(8,128)(2,1)S(1)}, bf16[4,4,16,256]{3,2,1,0:T(8,128)(2,1)S(1)}, u32[]{:S(2)}, u32[]{:S(2)}) collective-permute-start(bf16[4,4,16,256]{3,2,1,0:T(8,128)(2,1)S(1)} %collective-permute-done.11.v_ref), channel_id=1, source_target_pairs={{0,1},{1,0},{2,3},{3,2},{4,5},{5,4},{6,7},{7,6},{8,9},{9,8},{10,11... | collective-permute-start | bytes 393224 | tf_op jit(solution)/shard_map/ppermute | solution.py:338
  97.4 4.7 %collective-permute-start.21 = (f32[2,4,4,8,256]{4,3,2,1,0:T(8,128)S(1)}, f32[2,4,4,8,256]{4,3,2,1,0:T(8,128)S(1)}, u32[]{:S(2)}, u32[]{:S(2)}) collective-permute-start(f32[2,4,4,8,256]{4,3,2,1,0:T(8,128)S(1)} %get-tuple-element.38), channel_id=1, source_target_pairs={{0,1},{1,0},{2,3},{3,2},{4,5},{5,4},{6,7},{7,6},{8,9},{9,8},{10,11... | collective-permute-start | bytes 786440 | tf_op jit(solution)/shard_map/ppermute | solution.py:338
  97.9 4.3 %collective-permute-start.19 = (f32[2,4,4,8,256]{4,3,2,1,0:T(8,128)S(1)}, f32[2,4,4,8,256]{4,3,2,1,0:T(8,128)S(1)}, u32[]{:S(2)}, u32[]{:S(2)}) collective-permute-start(f32[2,4,4,8,256]{4,3,2,1,0:T(8,128)S(1)} %get-tuple-element.36), channel_id=1, source_target_pairs={{0,1},{1,0},{2,3},{3,2},{4,5},{5,4},{6,7},{7,6},{8,9},{9,8},{10,11... | collective-permute-start | bytes 786440 | tf_op jit(solution)/shard_map/ppermute | solution.py:338
  99.8 4.6 %collective-permute-start.18 = (f32[2,4,4,8,256]{4,3,2,1,0:T(8,128)S(1)}, f32[2,4,4,8,256]{4,3,2,1,0:T(8,128)S(1)}, u32[]{:S(2)}, u32[]{:S(2)}) collective-permute-start(f32[2,4,4,8,256]{4,3,2,1,0:T(8,128)S(1)} %get-tuple-element.34), channel_id=1, source_target_pairs={{0,1},{1,0},{2,3},{3,2},{4,5},{5,4},{6,7},{7,6},{8,9},{9,8},{10,11... | collective-permute-start | bytes 786440 | tf_op jit(solution)/shard_map/ppermute | solution.py:338
  100.3 6.1 %collective-permute-start.24 = (bf16[2,4,4,8,256]{4,3,2,1,0:T(8,128)(2,1)S(1)}, bf16[2,4,4,8,256]{4,3,2,1,0:T(8,128)(2,1)S(1)}, u32[]{:S(2)}, u32[]{:S(2)}) collective-permute-start(bf16[2,4,4,8,256]{4,3,2,1,0:T(8,128)(2,1)S(1)} %shard_map.110), channel_id=1, source_target_pairs={{0,6},{2,4},{4,2},{6,0},{1,7},{3,5},{5,3},{7,1},{8,14},{10,12},{12... | collective-permute-start | bytes 393224 | tf_op jit(solution)/shard_map/ppermute | solution.py:341
  102.1 4.7 %collective-permute-start.22 = (bf16[2,4,4,8,256]{4,3,2,1,0:T(8,128)(2,1)S(1)}, bf16[2,4,4,8,256]{4,3,2,1,0:T(8,128)(2,1)S(1)}, u32[]{:S(2)}, u32[]{:S(2)}) collective-permute-start(bf16[2,4,4,8,256]{4,3,2,1,0:T(8,128)(2,1)S(1)} %shard_map.108), channel_id=1, source_target_pairs={{0,2},{2,0},{4,6},{6,4},{1,3},{3,1},{5,7},{7,5},{8,10},{10,8},{12,... | collective-permute-start | bytes 393224 | tf_op jit(solution)/shard_map/ppermute | solution.py:341
  102.3 8.0 %collective-permute-start.20 = (bf16[2,4,4,8,256]{4,3,2,1,0:T(8,128)(2,1)S(1)}, bf16[2,4,4,8,256]{4,3,2,1,0:T(8,128)(2,1)S(1)}, u32[]{:S(2)}, u32[]{:S(2)}) collective-permute-start(bf16[2,4,4,8,256]{4,3,2,1,0:T(8,128)(2,1)S(1)} %shard_map.106), channel_id=1, source_target_pairs={{0,4},{2,6},{4,0},{6,2},{1,5},{3,7},{5,1},{7,3},{8,12},{10,14},{12... | collective-permute-start | bytes 393224 | tf_op jit(solution)/shard_map/ppermute | solution.py:341
  128.1 3.7 %collective-permute-start.25 = (f32[16,8,256]{2,1,0:T(8,128)S(1)}, f32[16,8,256]{2,1,0:T(8,128)S(1)}, u32[]{:S(2)}, u32[]{:S(2)}) collective-permute-start(f32[16,8,256]{2,1,0:T(8,128)S(1)} %get-tuple-element.42), channel_id=1, source_target_pairs={{0,1},{1,0},{2,3},{3,2},{4,5},{5,4},{6,7},{7,6},{8,9},{9,8},{10,11... | collective-permute-start | bytes 393224 | tf_op jit(solution)/shard_map/ppermute | solution.py:338
  (13 other events, 329.5 us)
